TPU v7x, 256 devices: a whole 4x4x8 slice. The times are simulated.
256 devices in a mesh: fsdp: 64 (over z, x_hi, y), tp: 4 (over x_lo, core).
Axes of the slice: x: 4 (x_hi: 2, x_lo: 2; x = x_hi * 2 + x_lo), y: 4, z: 8, core: 2. Of those that a mesh axis runs over, the one named last changes fastest.
Arguments:
- tokens: bfloat16 [24576, 8192], P('fsdp', 'tp'), may hold values from -16 to 16
- cotangent: bfloat16 [24576, 1024], P('fsdp', 'tp'), may hold values from -6 to 6
- response_mask: int32 [24576], P('fsdp'), may hold values 0 or 1
- key_weight: bfloat16 [8192, 1024], P('fsdp', 'tp'), may hold values from -0.0625 to 0.0625
- new_hidden: bfloat16 [256, 8, 8192], P('fsdp'), may hold values from -6 to 6
- new_values: bfloat16 [256, 8, 1024], P('fsdp', None, 'tp'), may hold values from -6 to 6
- queries: bfloat16 [256, 8, 8192], P('fsdp', None, 'tp'), may hold values from -16 to 16, as said below
- cache_keys: bfloat16 [256, 2048, 1024], P('fsdp', None, 'tp'), may hold values from -16 to 16, as said below
- cache_values: bfloat16 [256, 2048, 1024], P('fsdp', None, 'tp'), may hold values from -6 to 6
- cache_lengths: int32 [256], P('fsdp'), may hold values from 1 to 2048, as said below
Outputs:
- grad_inputs: bfloat16 [24576, 8192], P('fsdp', 'tp')
- learner_weight: bfloat16 [8192, 1024], P('fsdp', 'tp')
- new_keys: bfloat16 [256, 8, 1024], P('fsdp', None, 'tp')
- context: bfloat16 [256, 8, 8192], P('fsdp', None, 'tp')
Inputs may be any that keep to these rules, and one draw needn't show every extreme that they name: `queries`: queries of the decoded tokens, already rotated. `cache_keys`: cached keys, already rotated. `cache_lengths`: some request has exactly 2048 valid slots.
All inputs are finite; a program needn't handle non-finite values. No bound on the sum of `response_mask` on one device may be relied on, other than what follows from the above.
Results may differ from a plain program's by a relative error of at most 0.0095.
Values may be sent and summed in bfloat16 or wider, within the bound.
No kernel may reach another device: no remote copies, remote signals or barrier semaphores. Data moves between devices by JAX's collectives and lax.ppermute only.
A program may use at most 128 MiB of HBM per device.

v0:
```python
import math

import jax
import jax.numpy as jnp
from jax import lax
from jax.sharding import PartitionSpec as P

D = 8192
HD = 128


ROPE_BASE = 1000000.0


def rope_rotate(keys, positions):
    half = keys.shape[-1] // 2
    freq = ROPE_BASE ** (-jnp.arange(half, dtype=jnp.float32) * (2.0 / keys.shape[-1]))
    angle = positions.astype(jnp.float32)[..., None] * freq
    cosine = jnp.cos(angle)[..., None, :]
    sine = jnp.sin(angle)[..., None, :]
    first = keys[..., :half]
    second = keys[..., half:]
    return jnp.concatenate(
        [first * cosine - second * sine, second * cosine + first * sine], axis=-1
    )


def attend(queries, cache_keys, cache_values, new_keys, new_values, lengths):
    count, steps = (queries.shape[0], queries.shape[1])
    slots = cache_keys.shape[1]
    groups = cache_keys.shape[2] // HD
    share = queries.shape[2] // cache_keys.shape[2]
    inv = 1.0 / math.sqrt(HD)
    query = queries.reshape(count, steps, groups, share, HD)
    old_keys = cache_keys.reshape(count, slots, groups, HD)
    old_values = cache_values.reshape(count, slots, groups, HD)
    fresh_keys = new_keys.reshape(count, steps, groups, HD)
    fresh_values = new_values.reshape(count, steps, groups, HD)
    cache_scores = (
        jnp.einsum("rsjgd,rcjd->rsjgc", query, old_keys, preferred_element_type=jnp.float32) * inv
    )
    fresh_scores = (
        jnp.einsum("rsjgd,rtjd->rsjgt", query, fresh_keys, preferred_element_type=jnp.float32) * inv
    )
    cache_valid = jnp.arange(slots, dtype=jnp.int32)[None, :] < lengths[:, None]
    step_ids = jnp.arange(steps, dtype=jnp.int32)
    fresh_valid = step_ids[None, :] <= step_ids[:, None]
    cache_scores = jnp.where(cache_valid[:, None, None, None, :], cache_scores, -jnp.inf)
    fresh_scores = jnp.where(fresh_valid[None, :, None, None, :], fresh_scores, -jnp.inf)
    top = jnp.maximum(jnp.max(cache_scores, axis=-1), jnp.max(fresh_scores, axis=-1))[..., None]
    cache_exp = jnp.exp(cache_scores - top)
    fresh_exp = jnp.exp(fresh_scores - top)
    total = jnp.sum(cache_exp, axis=-1, keepdims=True) + jnp.sum(fresh_exp, axis=-1, keepdims=True)
    cache_weights = (cache_exp / total).astype(jnp.bfloat16)
    fresh_weights = (fresh_exp / total).astype(jnp.bfloat16)
    mixed = jnp.einsum(
        "rsjgc,rcjd->rsjgd", cache_weights, old_values, preferred_element_type=jnp.float32
    )
    mixed = mixed + jnp.einsum(
        "rsjgt,rtjd->rsjgd", fresh_weights, fresh_values, preferred_element_type=jnp.float32
    )
    return mixed.reshape(count, steps, groups * share * HD).astype(jnp.bfloat16)


def per_device(
    tokens,
    cotangent,
    response_mask,
    key_weight,
    new_hidden,
    new_values,
    queries,
    cache_keys,
    cache_values,
    cache_lengths,
):
    masked = cotangent * response_mask[:, None].astype(jnp.bfloat16)
    rows = key_weight.shape[0]
    scale = 1.0 / math.sqrt(D * tokens.shape[0] * lax.axis_size("fsdp"))
    full_weight = lax.all_gather(key_weight, "fsdp", axis=0, tiled=True)
    whole = lax.all_gather(tokens, "tp", axis=1, tiled=True)
    partial_value = jnp.einsum("tc,tk->ck", whole, masked, preferred_element_type=jnp.float32)
    terms = jnp.einsum("tk,ck->tc", masked, full_weight, preferred_element_type=jnp.float32)
    grad_inputs = lax.psum_scatter(
        terms.astype(jnp.bfloat16), "tp", scatter_dimension=1, tiled=True
    )
    grad = lax.psum(partial_value, "fsdp")
    rollout_weight = (full_weight.astype(jnp.float32) - grad * scale).astype(jnp.bfloat16)
    learner_weight = lax.dynamic_slice_in_dim(
        rollout_weight, lax.axis_index("fsdp") * rows, rows, 0
    )
    requests, steps = (new_hidden.shape[0], new_hidden.shape[1])
    raw = jnp.einsum("rsd,dk->rsk", new_hidden, rollout_weight, preferred_element_type=jnp.float32)
    local_width = raw.shape[2]
    positions = cache_lengths[:, None] + jnp.arange(steps, dtype=jnp.int32)[None, :]
    rotated = rope_rotate(raw.reshape(requests, steps, local_width // HD, HD), positions)
    new_keys = rotated.astype(jnp.bfloat16).reshape(requests, steps, local_width)
    context = attend(queries, cache_keys, cache_values, new_keys, new_values, cache_lengths)
    return (grad_inputs, learner_weight, new_keys, context)


def solution(mesh):
    placed = (
        P("fsdp", "tp"),
        P("fsdp", "tp"),
        P("fsdp"),
        P("fsdp", "tp"),
        P("fsdp", None, None),
        P("fsdp", None, "tp"),
        P("fsdp", None, "tp"),
        P("fsdp", None, "tp"),
        P("fsdp", None, "tp"),
        P("fsdp"),
    )
    return jax.shard_map(
        per_device,
        mesh=mesh,
        in_specs=placed,
        out_specs=(P("fsdp", "tp"), P("fsdp", "tp"), P("fsdp", None, "tp"), P("fsdp", None, "tp")),
        check_vma=False,
    )
```

profile of v0, /device:TPU:1, one launch (start us, length us, event | category | flops | bytes accessed | tf_op | source)
XLA Modules:
  0.0 1011.2 jit_solution(13662762769809048783)
XLA Ops:
  7.2 0.0 copy-start
  7.2 0.0 all-gather.5.cloned.1.call-start
  7.2 0.7 all-gather.5.cloned.1.call-update
  7.9 0.0 all-gather.3.cloned.1.call-start
  8.0 1.6 copy.22
  9.5 0.0 all-gather.3.cloned.1.call-update
  9.6 0.0 all-reduce.2.cloned.1.call-start
  9.6 0.7 convert_element_type.42
  10.3 70.2 %all-gather.5.cloned.1.call-done = bf16[384,8192]{1,0:T(8,128)(2,1)} async-done(((bf16[384,2048]{1,0:T(8,128)(2,1)}), bf16[384,8192]{1,0:T(8,128)(2,1)}) %all-gather.5.cloned.1.call-update) | async-done | bytes 6291472 | tf_op jit(solution)/shard_map/all_gather | solution.py:81
  80.5 8.6 convolution_bitcast_fusion
  89.1 0.0 copy-start.4
  89.1 0.0 all-reduce.2.cloned.1.call-update
  89.1 0.0 reduce-scatter.2.cloned.1.call-start
  89.2 120.4 %all-gather.3.cloned.1.call-done = bf16[8192,256]{0,1:T(8,128)(2,1)} async-done(((bf16[128,256]{0,1:T(8,128)(2,1)}), bf16[8192,256]{0,1:T(8,128)(2,1)}) %all-gather.3.cloned.1.call-update) | async-done | bytes 4194320 | tf_op jit(solution)/shard_map/all_gather | solution.py:80
  209.6 0.0 copy-done.4
  209.6 6.7 convolution_convert_fusion
  216.3 0.0 reduce-scatter.2.cloned.1.call-update
  216.3 6.9 reshape.100
  223.2 0.0 copy-start.6
  223.2 0.0 copy-start.5
  223.2 7.0 reshape.102
  230.3 0.0 copy-done.6
  230.3 0.1 add_convert_fusion
  230.4 0.1 multiply_cosine_fusion
  230.5 0.1 iota_compare_fusion
  230.6 0.0 copy-done.5
  230.6 5.7 bitcast_reduce_fusion
  236.3 656.1 %all-reduce.2.cloned.1.call-done = f32[8192,256]{0,1:T(8,128)} async-done(((f32[8192,256]{0,1:T(8,128)}), f32[8192,256]{0,1:T(8,128)}) %all-reduce.2.cloned.1.call-update) | async-done | bytes 8388624 | tf_op jit(solution)/shard_map/psum | solution.py:87
  892.5 5.8 subtract_convert_fusion
  898.3 0.0 copy-done
  898.3 0.0 copy-start.1
  898.3 0.0 copy-start.3
  898.3 1.3 fusion.17
  899.6 0.0 copy-start.2
  899.6 0.1 multiply_subtract_fusion
  899.7 0.7 fusion.33
  900.5 0.0 copy-done.1
  900.5 0.1 fusion.20
  900.6 1.4 copy-done.3
  902.0 1.0 fusion.7
  903.0 0.3 copy-done.2
  903.2 0.0 copy-start.7
  903.2 1.7 fusion
  905.0 0.0 copy-done.7
  905.0 0.3 fusion.16
  905.3 0.7 convert_element_type.53
  906.0 0.8 constant_dynamic-slice_fusion
  906.8 0.7 copy.30
  907.6 0.7 fusion.34
  908.3 96.4 %reduce-scatter.2.cloned.1.call-done = bf16[384,2048]{1,0:T(8,128)(2,1)} async-done(((bf16[384,8192]{1,0:T(8,128)(2,1)}), bf16[384,2048]{1,0:T(8,128)(2,1)}) %reduce-scatter.2.cloned.1.call-update) | async-done | bytes 1572880 | tf_op jit(solution)/shard_map/reduce_scatter | solution.py:84
  (5 shorter events, 0.1 us)
Async XLA Ops:
  7.2 891.1 %copy-start = (bf16[4,8,8192]{2,1,0:T(8,128)(2,1)S(1)}, bf16[4,8,8192]{2,1,0:T(8,128)(2,1)}, u32[]{:S(2)}) copy-start(bf16[4,8,8192]{2,1,0:T(8,128)(2,1)} %param.14) | copy-start | bytes 1572868
  7.2 73.3 %all-gather.5.cloned.1.call-start = ((), (), s32[]{:S(2)}) async-start(), calls=%async_computation.3 | async-start | bytes 7864320 | tf_op jit(solution)/shard_map/all_gather | solution.py:81
  7.9 201.7 %all-gather.3.cloned.1.call-start = ((), (), s32[]{:S(2)}) async-start(), calls=%async_computation.1 | async-start | bytes 4259840 | tf_op jit(solution)/shard_map/all_gather | solution.py:80
  9.6 882.9 %all-reduce.2.cloned.1.call-start = ((), (), s32[]{:S(2)}) async-start(), calls=%async_computation.4 | async-start | bytes 16777216 | tf_op jit(solution)/shard_map/psum | solution.py:87
  89.1 120.5 %copy-start.4 = (bf16[384,256]{1,0:T(8,128)(2,1)S(1)}, bf16[384,256]{1,0:T(8,128)(2,1)}, u32[]{:S(2)}) copy-start(bf16[384,256]{1,0:T(8,128)(2,1)} %param.11) | copy-start | bytes 589828
  89.1 915.5 %reduce-scatter.2.cloned.1.call-start = ((), (), s32[]{:S(2)}) async-start(), calls=%async_computation.2 | async-start | bytes 7864320 | tf_op jit(solution)/shard_map/reduce_scatter | solution.py:84
  223.2 7.1 copy-start.6
  223.2 7.4 copy-start.5
  898.3 2.2 copy-start.1
  898.3 3.7 copy-start.3
  899.6 3.6 copy-start.2
  903.2 1.7 copy-start.7
Sparse Core Ops, SparseCore 0:
  9.8 70.6 all-gather.4
  84.5 125.0 all-gather.2
  212.3 680.1 all-reduce.1
  895.5 109.1 reduce-scatter.1
where the time goes:
time: 1010 us
  waiting for transfers between devices  944 us (93%)
  matrix products  25 us (2%)
  local copies, waits for them, and re-layouts  19.5 us (2%)
  between operations  13.9 us (1%)
    psum x1, waiting for transfers between devices, per_device(): grad = lax.psum(partial_value, 'fsdp')  656 us
    all_gather x1, waiting for transfers between devices, per_device(): full_weight = lax.all_gather(key_weight, 'fsdp', axis=0, tiled=True)  120 us
    reduce_scatter x1, waiting for transfers between devices, per_device(): lax.psum_scatter(terms.astype(jnp.bfloat16), 'tp', scatter_dimension=1, t...  96.4 us
    all_gather x1, waiting for transfers between devices, per_device(): whole = lax.all_gather(tokens, 'tp', axis=1, tiled=True)  70.2 us
  transfers between devices with their start and end apart: 4, of which 4 were waited for; matrix products, arithmetic and copies ran while one was open for 5% of the time, Pallas kernels for 0%

commit v1 on v0

v1 whole, which is shorter than its diff:
```python
import math

import jax
import jax.numpy as jnp
from jax import lax
from jax.experimental import pallas as pl
from jax.experimental.pallas import tpu as pltpu
from jax.sharding import Mesh, PartitionSpec as P


D = 8192
HD = 128
NZ, NX, NY, NL, NC = 8, 2, 4, 2, 2
FSDP = ("z", "xh", "y")
TP = ("xl", "c")
F32 = jnp.float32
BF16 = jnp.bfloat16

ROPE_BASE = 1000000.0


def shift(x, axis, size, step):
    return lax.ppermute(x, axis, [(i, (i + step) % size) for i in range(size)])


def swap_owner(x, flip=0):
    pairs = []
    for z in range(NZ):
        for t in range(NL * NC):
            pairs.append((z * 4 + t, (2 * t + (z % 2 ^ flip)) * 4 + z // 2))
    return lax.ppermute(x, ("z", "xl", "c"), pairs)


def pick(x, index, axis):
    return lax.dynamic_index_in_dim(x, index, axis, keepdims=False)


def ring_sum(term, axis, size, me):
    last = size // 2
    whole = term((me + last) & (size - 1)).astype(BF16)
    half = whole.shape[0] // 2
    up, down = whole[:half], whole[half:]
    for hop in range(last, 0, -1):
        if hop < last:
            plus, minus = term((me + hop) & (size - 1)), term((me - hop) & (size - 1))
            up, down = up.astype(F32), down.astype(F32)
            if hop == last - 1:
                up = jnp.pad(up, [(0, half)] + [(0, 0)] * (up.ndim - 1))
                down = jnp.pad(down, [(half, 0)] + [(0, 0)] * (down.ndim - 1))
            up, down = (plus + up).astype(BF16), (minus + down).astype(BF16)
        up = shift(up, axis, size, 1)
        down = shift(down, axis, size, -1)
    return term(me) + up.astype(F32) + down.astype(F32)


def stacked(flat, share):
    wide = flat.astype(F32)
    return jnp.concatenate([wide[:, h * HD : (h + 1) * HD] for h in range(share)], axis=0)


def cache_kernel(lengths, q_ref, k_ref, v_ref, mixed_ref, top_ref, total_ref, *, share):
    valid = lengths[pl.program_id(0)]
    query = stacked(q_ref[0], share).astype(BF16)
    scores = lax.dot_general(
        query, k_ref[0], (((1,), (1,)), ((), ())), preferred_element_type=F32
    ) * (1.0 / math.sqrt(HD))
    slot = lax.broadcasted_iota(jnp.int32, scores.shape, 1)
    scores = jnp.where(slot < valid, scores, -jnp.inf)
    top = jnp.max(scores, axis=1, keepdims=True)
    weight = jnp.exp(scores - top)
    total = jnp.sum(weight, axis=1, keepdims=True)
    mixed_ref[0, 0] = jnp.dot(weight.astype(BF16), v_ref[0], preferred_element_type=F32)
    top_ref[0, 0] = jnp.broadcast_to(top, top_ref.shape[2:])
    total_ref[0, 0] = jnp.broadcast_to(total, total_ref.shape[2:])


def attend_cache(queries, cache_keys, cache_values, lengths):
    count, steps, width = queries.shape
    slots = cache_keys.shape[1]
    groups = cache_keys.shape[2] // HD
    share = width // cache_keys.shape[2]
    state = jax.ShapeDtypeStruct((count, groups, share * steps, HD), F32)
    state_spec = pl.BlockSpec((1, 1, share * steps, HD), lambda r, j, n: (r, j, 0, 0))
    cache_spec = pl.BlockSpec((1, slots, HD), lambda r, j, n: (r, 0, j))
    return pl.pallas_call(
        lambda *refs: cache_kernel(*refs, share=share),
        out_shape=(state, state, state),
        grid_spec=pltpu.PrefetchScalarGridSpec(
            num_scalar_prefetch=1,
            grid=(count, groups),
            in_specs=[
                pl.BlockSpec((1, steps, share * HD), lambda r, j, n: (r, 0, j)),
                cache_spec,
                cache_spec,
            ],
            out_specs=[state_spec, state_spec, state_spec],
        ),
        cost_estimate=pl.CostEstimate(
            flops=4 * count * groups * share * steps * slots * HD,
            bytes_accessed=4 * count * slots * groups * HD,
            transcendentals=count * groups * share * steps * slots,
        ),
        name="cache_attention",
    )(lengths, queries, cache_keys, cache_values)


def fresh_kernel(
    raw_ref, cos_ref, sin_ref, q_ref, v_ref, mixed_ref, top_ref, total_ref, keys_ref, out_ref, *, share
):
    raw = raw_ref[...]
    keys = raw * cos_ref[...] + pltpu.roll(raw, HD // 2, 1) * sin_ref[...]
    keys = keys.astype(BF16)
    keys_ref[0] = keys
    steps = keys.shape[0]
    query = stacked(q_ref[0], share).astype(BF16)
    scores = lax.dot_general(
        query, keys, (((1,), (1,)), ((), ())), preferred_element_type=F32
    ) * (1.0 / math.sqrt(HD))
    step = lax.broadcasted_iota(jnp.int32, scores.shape, 0) % steps
    scores = jnp.where(lax.broadcasted_iota(jnp.int32, scores.shape, 1) <= step, scores, -jnp.inf)
    top = top_ref[0, 0]
    high = jnp.maximum(top, jnp.max(scores, axis=1, keepdims=True))
    old = jnp.exp(top - high)
    weight = jnp.exp(scores - high[:, :1])
    whole = total_ref[0, 0] * old + jnp.sum(weight, axis=1, keepdims=True)
    fresh = jnp.dot(weight.astype(BF16), v_ref[0], preferred_element_type=F32)
    context = ((mixed_ref[0, 0] * old + fresh) / whole).astype(BF16).astype(F32)
    flat = [context[h * steps : (h + 1) * steps] for h in range(share)]
    out_ref[0] = jnp.concatenate(flat, axis=1).astype(BF16)


def attend_fresh(raw, cosine, sine, queries, new_values, mixed, top, total):
    count, steps, width = queries.shape
    groups = new_values.shape[2] // HD
    share = width // new_values.shape[2]
    state_spec = pl.BlockSpec((1, 1, share * steps, HD), lambda r, j: (r, j, 0, 0))
    query_spec = pl.BlockSpec((1, steps, share * HD), lambda r, j: (r, 0, j))
    value_spec = pl.BlockSpec((1, steps, HD), lambda r, j: (r, 0, j))
    angle_spec = pl.BlockSpec((steps, HD), lambda r, j: (r, 0))
    return pl.pallas_call(
        lambda *refs: fresh_kernel(*refs, share=share),
        out_shape=(
            jax.ShapeDtypeStruct(new_values.shape, BF16),
            jax.ShapeDtypeStruct(queries.shape, BF16),
        ),
        grid=(count, groups),
        in_specs=[
            pl.BlockSpec((steps, HD), lambda r, j: (r, j)),
            angle_spec,
            angle_spec,
            query_spec,
            value_spec,
            state_spec,
            state_spec,
            state_spec,
        ],
        out_specs=[value_spec, query_spec],
        name="fresh_attention",
    )(raw, cosine, sine, queries, new_values, mixed, top, total)


def input_kernel(m_ref, w_ref, out_ref):
    blocks, cols = w_ref.shape[2], w_ref.shape[5]
    total = jnp.zeros(out_ref.shape, F32)
    for block in range(blocks):
        total += lax.dot_general(
            m_ref[:, block * cols : (block + 1) * cols],
            w_ref[0, 0, block, 0],
            (((1,), (1,)), ((), ())),
            preferred_element_type=F32,
        )
    out_ref[...] = total.astype(BF16)


def input_grad(masked, weight):
    ny, nx, blocks, two, rows, cols = weight.shape
    count = masked.shape[0]
    return pl.pallas_call(
        input_kernel,
        out_shape=jax.ShapeDtypeStruct((count, two * nx * ny * rows), BF16),
        grid=(ny, nx, two),
        in_specs=[
            pl.BlockSpec((count, blocks * cols), lambda i, k, j: (0, 0)),
            pl.BlockSpec((1, 1, blocks, 1, rows, cols), lambda i, k, j: (i, k, 0, j, 0, 0)),
        ],
        out_specs=pl.BlockSpec((count, rows), lambda i, k, j: (0, (j * nx + k) * ny + i)),
        cost_estimate=pl.CostEstimate(
            flops=2 * count * weight.size, bytes_accessed=2 * weight.size, transcendentals=0
        ),
        name="input_grad",
    )(masked, weight)


def angles(lengths, steps):
    half = HD // 2
    freq = ROPE_BASE ** (-jnp.arange(half, dtype=F32) * (2.0 / HD))
    positions = lengths[:, None] + jnp.arange(steps, dtype=jnp.int32)[None, :]
    angle = positions.reshape(-1).astype(F32)[:, None] * freq
    cosine, sine = jnp.cos(angle), jnp.sin(angle)
    return jnp.concatenate([cosine, cosine], axis=1), jnp.concatenate([-sine, sine], axis=1)


def update_and_decode(
    tokens,
    cotangent,
    response_mask,
    key_weight,
    new_hidden,
    new_values,
    queries,
    cache_keys,
    cache_values,
    cache_lengths,
):
    z, xh, y = lax.axis_index("z"), lax.axis_index("xh"), lax.axis_index("y")
    xl, c = lax.axis_index("xl"), lax.axis_index("c")
    tp = xl * NC + c
    odd = z & 1
    wide = tokens.shape[1]
    cols = cotangent.shape[1]
    rows = key_weight.shape[0]
    requests, steps = new_hidden.shape[0], new_hidden.shape[1]
    lines = requests * steps

    masked = cotangent * response_mask[:, None].astype(BF16)
    masked_all = lax.all_gather(masked, TP, axis=1, tiled=True)

    hidden = new_hidden.reshape(lines, new_hidden.shape[2])
    hidden = lax.dynamic_slice_in_dim(hidden, tp * wide, wide, 1)
    hidden = hidden.reshape(lines, 2, NX * NY, rows).transpose(2, 1, 0, 3)
    hidden = lax.all_to_all(hidden, ("xh", "y"), 0, 0, tiled=True)
    hidden = hidden.transpose(1, 0, 2, 3).reshape(1, 2, NX * NY * lines, rows)
    hidden = jnp.broadcast_to(hidden, (NZ // 2,) + hidden.shape[1:]).reshape(NZ, NX * NY * lines, rows)
    hidden = lax.all_to_all(hidden, "z", 0, 0, tiled=True)
    hidden = hidden.reshape(NZ, NX, NY, lines, rows)

    own_weight = swap_owner(key_weight)
    old = lax.all_gather(own_weight, "z")
    old = lax.all_gather(old, "xh")
    old = lax.all_gather(old, "y")
    old = old.reshape(NY, NX, NL * NC, 2, rows, cols)

    def term(k):
        left = lax.dynamic_slice_in_dim(tokens, (k & 1) * (wide // 2), wide // 2, 1)
        right = lax.dynamic_slice_in_dim(masked_all, (k >> 1) * cols, cols, 1)
        return lax.dot_general(left, right, (((0,), (0,)), ((), ())), preferred_element_type=F32)

    part = ring_sum(term, "z", NZ, z).reshape(NX, NY, rows, cols)
    part = ring_sum(lambda k: pick(part, k, 1), "y", NY, y)
    other = shift(pick(part, 1 - xh, 0).astype(BF16), "xh", NX, 1)
    grad = pick(part, xh, 0) + other.astype(F32)

    scale = 1.0 / math.sqrt(D * tokens.shape[0] * NZ * NX * NY)
    own_weight = (own_weight.astype(F32) - grad * scale).astype(BF16)

    def raw_term(k):
        left = pick(hidden, k, 2).reshape(NZ * NX * lines, rows)
        return jnp.dot(left, own_weight, preferred_element_type=F32)

    raw = ring_sum(raw_term, "y", NY, y).reshape(NL, NC, 2, NX, lines, cols)
    other = shift(pick(raw, 1 - xh, 3).astype(BF16), "xh", NX, 1)
    raw = pick(raw, xh, 3) + other.astype(F32)
    other = shift(pick(raw, 1 - c, 1), "c", NC, 1)
    raw = pick(raw, c, 1) + other
    other = shift(pick(raw, 1 - xl, 0), "xl", NL, 1)
    raw = pick(raw, xl, 0) + other
    same = swap_owner(pick(raw, odd, 0))
    other = swap_owner(pick(raw, 1 - odd, 0), 1)
    raw = same + other

    learner_weight = swap_owner(own_weight)

    state = attend_cache(queries, cache_keys, cache_values, cache_lengths)
    cosine, sine = angles(cache_lengths, steps)
    new_keys, context = attend_fresh(raw, cosine, sine, queries, new_values, *state)

    grad_inputs = input_grad(masked_all, old)
    return (grad_inputs, learner_weight, new_keys, context)


def solution(mesh):
    split = Mesh(mesh.devices.reshape(NZ, NX, NY, NL, NC), ("z", "xh", "y", "xl", "c"))
    placed = (
        P(FSDP, TP),
        P(FSDP, TP),
        P(FSDP),
        P(FSDP, TP),
        P(FSDP, None, None),
        P(FSDP, None, TP),
        P(FSDP, None, TP),
        P(FSDP, None, TP),
        P(FSDP, None, TP),
        P(FSDP),
    )
    return jax.shard_map(
        update_and_decode,
        mesh=split,
        in_specs=placed,
        out_specs=(P(FSDP, TP), P(FSDP, TP), P(FSDP, None, TP), P(FSDP, None, TP)),
        check_vma=False,
    )
```

time: 1010 us -> 236 us (0.23)
  the two profiles are of different devices: /device:TPU:1 before, /device:TPU:26 now
where the time goes in v1:
time: 236 us; the launch traced here: 235 us
  waiting for transfers between devices  63 us (27%)
  starting transfers between devices  62.9 us (27%)
  blocking collectives  42.9 us (18%)
  Pallas kernels  28.7 us (12%)
  between operations  14.5 us (6%)
  other arithmetic  12.7 us (5%)
  matrix products  5.43 us (2%)
  local copies, waits for them, and re-layouts  4.55 us (2%)
    ppermute x20, waiting for transfers between devices, shift(): return lax.ppermute(x, axis, [(i, (i + step) % size) for i in range(size)])  43.6 us
    all_gather x1, blocking collectives, update_and_decode(): old = lax.all_gather(own_weight, 'z')  34.7 us
    ppermute x20, starting transfers between devices, shift(): return lax.ppermute(x, axis, [(i, (i + step) % size) for i in range(size)])  26.8 us
    ppermute x4, starting transfers between devices, swap_owner(): return lax.ppermute(x, ('z', 'xl', 'c'), pairs)  23.4 us
    pallas_call x1, Pallas kernels, input_grad(): pl.pallas_call(input_kernel, out_shape=jax.ShapeDtypeStruct((count, two *...  12.6 us
    all_gather x1, waiting for transfers between devices, update_and_decode(): old = lax.all_gather(old, 'xh')  10.9 us
    pallas_call x1, Pallas kernels, attend_cache(): pl.pallas_call(lambda *refs: cache_kernel(*refs, share=share), out_shape=...  9.55 us
    all_gather x1, blocking collectives, update_and_decode(): masked_all = lax.all_gather(masked, TP, axis=1, tiled=True)  8.19 us
  transfers between devices with their start and end apart: 28, of which 13 were waited for; matrix products, arithmetic and copies ran while one was open for 8% of the time, Pallas kernels for 7%

profile of v1, /device:TPU:26, one launch (start us, length us, event | category | flops | bytes accessed | tf_op | source)
XLA Modules:
  0.0 234.6 jit_solution(17355354415476598396)
XLA Ops:
  7.2 0.8 convert_element_type.126
  8.0 1.0 broadcast_multiply_fusion
  9.1 8.2 %all_gather.21.m_ref = bf16[384,1024]{1,0:T(8,128)(2,1)S(1)} all-gather(bf16[384,256]{1,0:T(8,128)(2,1)S(1)} %broadcast_multiply_fusion), channel_id=1, replica_groups=mesh['z'=8,'xh'=2,'y'=4,'xl'=2,'c'=2] {'xl','c'}, dimensions={1}, use_global_device_ids=true | all-gather | bytes 983040 | tf_op jit(solution)/shard_map/all_gather | solution.py:226
  17.3 0.5 convolution_convert_fusion
  17.8 2.0 collective-permute-start.1
  19.8 4.0 %collective-permute-start.5 = (bf16[512,256]{1,0:T(8,128)(2,1)S(1)}, bf16[512,256]{1,0:T(8,128)(2,1)S(1)}, u32[]{:S(2)}, u32[]{:S(2)}) collective-permute-start(bf16[512,256]{1,0:T(8,128)(2,1)S(1)} %get-tuple-element.21), channel_id=1, source_target_pairs={{0,224},{32,0},{64,32},{96,64},{128,96},{160,128},{192,160},{224,1... | collective-permute-start | bytes 786440 | tf_op jit(solution)/shard_map/ppermute | solution.py:23
  23.8 6.7 %collective-permute-start = (bf16[128,256]{1,0:T(8,128)(2,1)S(1)}, bf16[128,256]{1,0:T(8,128)(2,1)S(1)}, u32[]{:S(2)}, u32[]{:S(2)}) collective-permute-start(bf16[128,256]{1,0:T(8,128)(2,1)S(1)} %copy-done.6), channel_id=1, source_target_pairs={{0,0},{1,64},{2,128},{3,192},{32,32},{33,96},{34,160},{35,224},{64... | collective-permute-start | bytes 196616 | tf_op jit(solution)/shard_map/ppermute | solution.py:31
  30.6 1.3 add_convert_fusion.5
  31.9 2.9 %collective-permute-done = bf16[128,256]{1,0:T(8,128)(2,1)S(1)} collective-permute-done((bf16[128,256]{1,0:T(8,128)(2,1)S(1)}, bf16[128,256]{1,0:T(8,128)(2,1)S(1)}, u32[]{:S(2)}, u32[]{:S(2)}) %collective-permute-start) | collective-permute-done | bytes 65568 | tf_op jit(solution)/shard_map/ppermute | solution.py:31
  34.8 34.7 %all-gather = bf16[1024,256]{1,0:T(8,128)(2,1)} all-gather(bf16[128,256]{1,0:T(8,128)(2,1)S(1)} %collective-permute-done), channel_id=2, replica_groups=mesh['z'=8,'xh'=2,'y'=4,'xl'=2,'c'=2] {'z'}, dimensions={0}, use_global_device_ids=true | all-gather | bytes 589824 | tf_op jit(solution)/shard_map/all_gather | solution.py:238
  69.6 0.5 add_convert_fusion.2
  70.0 0.7 collective-permute-start.6
  70.7 0.5 fusion.12
  71.2 0.5 fusion.5
  71.7 1.0 add_convert_fusion.4
  72.6 1.4 collective-permute-start.3
  74.1 8.8 %collective-permute-done.6 = bf16[1024,256]{1,0:T(8,128)(2,1)S(1)} collective-permute-done((bf16[1024,256]{1,0:T(8,128)(2,1)S(1)}, bf16[1024,256]{1,0:T(8,128)(2,1)S(1)}, u32[]{:S(2)}, u32[]{:S(2)}) %collective-permute-start.6) | collective-permute-done | bytes 524320 | tf_op jit(solution)/shard_map/ppermute | solution.py:23
  82.9 0.9 add_convert_fusion.1
  83.8 0.9 collective-permute-start.7
  84.7 0.5 fusion.14
  85.2 10.9 %all-gather.6.cloned.1.call-done = bf16[16,128,256]{2,1,0:T(8,128)(2,1)} async-done(((bf16[8,128,256]{2,1,0:T(8,128)(2,1)}), bf16[16,128,256]{2,1,0:T(8,128)(2,1)}) %all-gather.6.cloned.1.call-update) | async-done | bytes 1048592 | tf_op jit(solution)/shard_map/all_gather | solution.py:239
  96.1 0.5 fusion.7
  96.6 2.0 add_convert_fusion.3
  98.6 1.6 collective-permute-start.4
  100.2 1.9 add_convert_fusion
  102.1 1.8 collective-permute-start.8
  103.9 0.9 dynamic-slice_bitcast_fusion.1
  104.8 0.8 copy.15
  105.6 5.7 %all-to-all-start = ((bf16[8,2,32,128]{3,1,2,0:T(2,128)(2,1)}), bf16[8,2,32,128]{3,1,2,0:T(2,128)(2,1)S(1)}, u32[]{:S(2)}, u32[]{:S(2)}) async-start(bf16[8,2,32,128]{3,1,2,0:T(2,128)(2,1)} %copy.15), calls=%async_computation | async-start | bytes 262144 | tf_op jit(solution)/shard_map/all_to_all | solution.py:231
  111.3 0.5 fusion.16
  111.7 5.6 %all-to-all-done = bf16[8,2,32,128]{3,1,2,0:T(2,128)(2,1)S(1)} async-done(((bf16[8,2,32,128]{3,1,2,0:T(2,128)(2,1)}), bf16[8,2,32,128]{3,1,2,0:T(2,128)(2,1)S(1)}, u32[]{:S(2)}, u32[]{:S(2)}) %all-to-all-start) | async-done | bytes 131104 | tf_op jit(solution)/shard_map/all_to_all | solution.py:231
  117.3 0.9 broadcast_in_dim.5
  118.3 6.9 %all-to-all-start.1 = ((bf16[8,256,128]{2,1,0:T(8,128)(2,1)}), bf16[8,256,128]{2,1,0:T(8,128)(2,1)S(1)}, u32[]{:S(2)}, u32[]{:S(2)}) async-start(bf16[8,256,128]{2,1,0:T(8,128)(2,1)} %bitcast.15), calls=%async_computation.1 | async-start | bytes 1048576 | tf_op jit(solution)/shard_map/all_to_all | solution.py:234
  125.2 1.3 convert_add_fusion
  126.6 1.0 copy-done.2
  127.6 0.7 collective-permute-start.11
  128.2 2.8 %collective-permute-start.9 = (bf16[1,128,256]{2,1,0:T(8,128)(2,1)S(1)}, bf16[1,128,256]{2,1,0:T(8,128)(2,1)S(1)}, u32[]{:S(2)}, u32[]{:S(2)}) collective-permute-start(bf16[1,128,256]{2,1,0:T(8,128)(2,1)S(1)} %get-tuple-element.24), channel_id=1, source_target_pairs={{0,4},{4,8},{8,12},{12,0},{1,5},{5,9},{9,13},{13,1},{2,6},{6,10},{... | collective-permute-start | bytes 196616 | tf_op jit(solution)/shard_map/ppermute | solution.py:23
  131.1 3.8 %collective-permute-done.11 = bf16[1,128,256]{2,1,0:T(8,128)(2,1)S(1)} collective-permute-done((bf16[1,128,256]{2,1,0:T(8,128)(2,1)S(1)}, bf16[1,128,256]{2,1,0:T(8,128)(2,1)S(1)}, u32[]{:S(2)}, u32[]{:S(2)}) %collective-permute-start.11) | collective-permute-done | bytes 65568 | tf_op jit(solution)/shard_map/ppermute | solution.py:23
  134.8 1.1 fusion.19
  135.9 3.3 %collective-permute-start.10 = (bf16[2,128,256]{2,1,0:T(8,128)(2,1)S(1)}, bf16[2,128,256]{2,1,0:T(8,128)(2,1)S(1)}, u32[]{:S(2)}, u32[]{:S(2)}) collective-permute-start(bf16[2,128,256]{2,1,0:T(8,128)(2,1)S(1)} %get-tuple-element.14), channel_id=1, source_target_pairs={{0,4},{4,8},{8,12},{12,0},{1,5},{5,9},{9,13},{13,1},{2,6},{6,10},{... | collective-permute-start | bytes 393224 | tf_op jit(solution)/shard_map/ppermute | solution.py:23
  139.2 5.4 %collective-permute-done.10 = bf16[2,128,256]{2,1,0:T(8,128)(2,1)S(1)} collective-permute-done((bf16[2,128,256]{2,1,0:T(8,128)(2,1)S(1)}, bf16[2,128,256]{2,1,0:T(8,128)(2,1)S(1)}, u32[]{:S(2)}, u32[]{:S(2)}) %collective-permute-start.10) | collective-permute-done | bytes 131104 | tf_op jit(solution)/shard_map/ppermute | solution.py:23
  144.6 3.7 %collective-permute-done.12 = bf16[2,128,256]{2,1,0:T(8,128)(2,1)S(1)} collective-permute-done((bf16[2,128,256]{2,1,0:T(8,128)(2,1)S(1)}, bf16[2,128,256]{2,1,0:T(8,128)(2,1)S(1)}, u32[]{:S(2)}, u32[]{:S(2)}) %collective-permute-start.12) | collective-permute-done | bytes 131104 | tf_op jit(solution)/shard_map/ppermute | solution.py:23
  148.3 1.0 fusion.20
  149.4 1.5 collective-permute-start.13
  150.9 4.3 %collective-permute-done.13 = bf16[128,256]{1,0:T(8,128)(2,1)S(1)} collective-permute-done((bf16[128,256]{1,0:T(8,128)(2,1)S(1)}, bf16[128,256]{1,0:T(8,128)(2,1)S(1)}, u32[]{:S(2)}, u32[]{:S(2)}) %collective-permute-start.13) | collective-permute-done | bytes 65568 | tf_op jit(solution)/shard_map/ppermute | solution.py:23
  155.6 2.0 collective-permute-start.17
  157.6 3.5 %collective-permute-done.15 = bf16[256,256]{1,0:T(8,128)(2,1)S(1)} collective-permute-done((bf16[256,256]{1,0:T(8,128)(2,1)S(1)}, bf16[256,256]{1,0:T(8,128)(2,1)S(1)}, u32[]{:S(2)}, u32[]{:S(2)}) %collective-permute-start.15) | collective-permute-done | bytes 131104 | tf_op jit(solution)/shard_map/ppermute | solution.py:23
  161.3 2.1 collective-permute-start.16
  163.8 4.0 %collective-permute-done.16 = bf16[512,256]{1,0:T(8,128)(2,1)S(1)} collective-permute-done((bf16[512,256]{1,0:T(8,128)(2,1)S(1)}, bf16[512,256]{1,0:T(8,128)(2,1)S(1)}, u32[]{:S(2)}, u32[]{:S(2)}) %collective-permute-start.16) | collective-permute-done | bytes 262176 | tf_op jit(solution)/shard_map/ppermute | solution.py:23
  167.8 3.6 %collective-permute-done.18 = bf16[512,256]{1,0:T(8,128)(2,1)S(1)} collective-permute-done((bf16[512,256]{1,0:T(8,128)(2,1)S(1)}, bf16[512,256]{1,0:T(8,128)(2,1)S(1)}, u32[]{:S(2)}, u32[]{:S(2)}) %collective-permute-start.18) | collective-permute-done | bytes 262176 | tf_op jit(solution)/shard_map/ppermute | solution.py:23
  171.3 0.2 fusion
  171.6 1.1 collective-permute-start.19
  172.9 5.3 %collective-permute-done.19 = bf16[2,2,2,32,256]{4,3,2,1,0:T(8,128)(2,1)S(1)} collective-permute-done((bf16[2,2,2,32,256]{4,3,2,1,0:T(8,128)(2,1)S(1)}, bf16[2,2,2,32,256]{4,3,2,1,0:T(8,128)(2,1)S(1)}, u32[]{:S(2)}, u32[]{:S(2)}) %collective-permute-start.19) | collective-permute-done | bytes 131104 | tf_op jit(solution)/shard_map/ppermute | solution.py:23
  178.4 1.2 collective-permute-done.20
  179.7 0.7 collective-permute-start.21
  180.3 0.7 pad_maximum_fusion
  181.0 8.7 %collective-permute-start.14 = (bf16[128,256]{1,0:T(8,128)(2,1)S(1)}, bf16[128,256]{1,0:T(8,128)(2,1)S(1)}, u32[]{:S(2)}, u32[]{:S(2)}) collective-permute-start(bf16[128,256]{1,0:T(8,128)(2,1)S(1)} %fusion.40), channel_id=1, source_target_pairs={{0,0},{1,64},{2,128},{3,192},{32,32},{33,96},{34,160},{35,224},{64... | collective-permute-start | bytes 196616 | tf_op jit(solution)/shard_map/ppermute | solution.py:31
  189.8 2.1 collective-permute-start.22
  191.9 5.8 %collective-permute-start.23 = (f32[32,256]{1,0:T(8,128)S(1)}, f32[32,256]{1,0:T(8,128)S(1)}, u32[]{:S(2)}, u32[]{:S(2)}) collective-permute-start(f32[32,256]{1,0:T(8,128)S(1)} %get-tuple-element.26), channel_id=1, source_target_pairs={{0,32},{1,96},{2,160},{3,224},{32,0},{33,64},{34,128},{35,192},{64... | collective-permute-start | bytes 98312 | tf_op jit(solution)/shard_map/ppermute | solution.py:31
  197.8 9.5 %cache_attention.1 = (f32[4,2,64,128]{3,2,1,0:T(8,128)}, f32[4,2,64,128]{3,2,1,0:T(8,128)}, f32[4,2,64,128]{3,2,1,0:T(8,128)}) custom-call(s32[4]{0:T(128)} %refs_0_.1, bf16[4,8,2048]{2,1,0:T(8,128)(2,1)} %refs_3_.3, bf16[4,2048,256]{2,1,0:T(8,128)(2,1)} %refs_2_.1, bf16[4,2048,256]{2,1,0:T(8,128)(2,1)} %refs_3_.2), custom_call_target="tpu_custom_call" | custom-call | flops 536870912 | bytes 8388608 | tf_op jit(solution)/shard_map/cache_attention/pallas_call | solution.py:85
  207.3 0.6 add.281.refs_0_
  208.0 6.6 %fresh_attention.1 = (bf16[4,8,256]{2,1,0:T(8,128)(2,1)}, bf16[4,8,2048]{2,1,0:T(8,128)(2,1)}) custom-call(f32[32,256]{1,0:T(8,128)} %add.281.refs_0_, f32[32,128]{1,0:T(8,128)} %get-tuple-element.31.refs_1_, f32[32,128]{1,0:T(8,128)} %get-tuple-element.32.refs_2_, bf16[4,8,2048]{2,1,0:T(8,128)(2,1)} %refs_3_.3, bf16[4,8,256]{2,1,0:T(8,128)(2,1)} %refs_4_.1, ...), custom_call_target="tpu_custom_call" | custom-call | tf_op jit(solution)/shard_map/fresh_attention/pallas_call | solution.py:140
  214.6 12.6 %input_grad.1 = bf16[384,2048]{1,0:T(8,128)(2,1)} custom-call(bf16[384,1024]{1,0:T(8,128)(2,1)} %copy-done.1, bf16[4,2,4,2,128,256]{5,4,3,2,1,0:T(8,128)(2,1)} %bitcast.71), custom_call_target="tpu_custom_call" | custom-call | flops 1610612736 | bytes 4194304 | tf_op jit(solution)/shard_map/input_grad/pallas_call | solution.py:178
  227.1 0.6 copy.19
  (60 shorter events, 1.7 us)
Async XLA Ops:
  7.2 10.1 %copy-start = (bf16[384,2048]{1,0:T(8,128)(2,1)S(1)}, bf16[384,2048]{1,0:T(8,128)(2,1)}, u32[]{:S(2)}) copy-start(bf16[384,2048]{1,0:T(8,128)(2,1)} %param.10) | copy-start | bytes 4718596
  7.2 88.9 %all-gather.6.cloned.1.call-start = ((), (), s32[]{:S(2)}) async-start(), calls=%async_computation.2 | async-start | bytes 1572864 | tf_op jit(solution)/shard_map/all_gather | solution.py:239
  17.3 94.0 %copy-start.1 = (bf16[384,1024]{1,0:T(8,128)(2,1)}, bf16[384,1024]{1,0:T(8,128)(2,1)S(1)}, u32[]{:S(2)}) copy-start(bf16[384,1024]{1,0:T(8,128)(2,1)S(1)} %all_gather.21.m_ref) | copy-start | bytes 2359300
  17.3 6.6 %copy-start.6 = (bf16[128,256]{1,0:T(8,128)(2,1)S(1)}, bf16[128,256]{1,0:T(8,128)(2,1)}, u32[]{:S(2)}) copy-start(bf16[128,256]{1,0:T(8,128)(2,1)} %param.13) | copy-start | bytes 196612
  17.8 12.8 %collective-permute-start.1 = (bf16[512,256]{1,0:T(8,128)(2,1)S(1)}, bf16[512,256]{1,0:T(8,128)(2,1)S(1)}, u32[]{:S(2)}, u32[]{:S(2)}) collective-permute-start(bf16[512,256]{1,0:T(8,128)(2,1)S(1)} %get-tuple-element.20), channel_id=1, source_target_pairs={{0,32},{32,64},{64,96},{96,128},{128,160},{160,192},{192,224},{224... | collective-permute-start | bytes 786440 | tf_op jit(solution)/shard_map/ppermute | solution.py:23
  19.8 49.8 %collective-permute-start.5 = (bf16[512,256]{1,0:T(8,128)(2,1)S(1)}, bf16[512,256]{1,0:T(8,128)(2,1)S(1)}, u32[]{:S(2)}, u32[]{:S(2)}) collective-permute-start(bf16[512,256]{1,0:T(8,128)(2,1)S(1)} %get-tuple-element.21), channel_id=1, source_target_pairs={{0,224},{32,0},{64,32},{96,64},{128,96},{160,128},{192,160},{224,1... | collective-permute-start | bytes 786440 | tf_op jit(solution)/shard_map/ppermute | solution.py:23
  23.8 11.0 %collective-permute-start = (bf16[128,256]{1,0:T(8,128)(2,1)S(1)}, bf16[128,256]{1,0:T(8,128)(2,1)S(1)}, u32[]{:S(2)}, u32[]{:S(2)}) collective-permute-start(bf16[128,256]{1,0:T(8,128)(2,1)S(1)} %copy-done.6), channel_id=1, source_target_pairs={{0,0},{1,64},{2,128},{3,192},{32,32},{33,96},{34,160},{35,224},{64... | collective-permute-start | bytes 196616 | tf_op jit(solution)/shard_map/ppermute | solution.py:31
  31.9 39.8 %collective-permute-start.2 = (bf16[1024,256]{1,0:T(8,128)(2,1)}, bf16[1024,256]{1,0:T(8,128)(2,1)S(1)}, u32[]{:S(2)}, u32[]{:S(2)}) collective-permute-start(bf16[1024,256]{1,0:T(8,128)(2,1)} %add_convert_fusion.5), channel_id=1, source_target_pairs={{0,32},{32,64},{64,96},{96,128},{128,160},{160,192},{192,224},{224... | collective-permute-start | bytes 1572872 | tf_op jit(solution)/shard_map/ppermute | solution.py:23
  34.8 35.3 %copy-start.3 = (bf16[128,256]{1,0:T(8,128)(2,1)}, bf16[128,256]{1,0:T(8,128)(2,1)S(1)}, u32[]{:S(2)}) copy-start(bf16[128,256]{1,0:T(8,128)(2,1)S(1)} %collective-permute-done) | copy-start | bytes 196612
  69.5 145.1 %all-gather.8.cloned.1.call-start = ((), (), s32[]{:S(2)}) async-start(), calls=%async_computation.3 | async-start | bytes 5242880 | tf_op jit(solution)/shard_map/all_gather | solution.py:240
  70.0 12.9 %collective-permute-start.6 = (bf16[1024,256]{1,0:T(8,128)(2,1)S(1)}, bf16[1024,256]{1,0:T(8,128)(2,1)S(1)}, u32[]{:S(2)}, u32[]{:S(2)}) collective-permute-start(bf16[1024,256]{1,0:T(8,128)(2,1)S(1)} %add_convert_fusion.2), channel_id=1, source_target_pairs={{0,224},{32,0},{64,32},{96,64},{128,96},{160,128},{192,160},{224,1... | collective-permute-start | bytes 1572872 | tf_op jit(solution)/shard_map/ppermute | solution.py:23
  72.6 24.0 %collective-permute-start.3 = (bf16[1024,256]{1,0:T(8,128)(2,1)}, bf16[1024,256]{1,0:T(8,128)(2,1)}, u32[]{:S(2)}, u32[]{:S(2)}) collective-permute-start(bf16[1024,256]{1,0:T(8,128)(2,1)} %add_convert_fusion.4), channel_id=1, source_target_pairs={{0,32},{32,64},{64,96},{96,128},{128,160},{160,192},{192,224},{224... | collective-permute-start | bytes 1572872 | tf_op jit(solution)/shard_map/ppermute | solution.py:23
  83.8 16.3 %collective-permute-start.7 = (bf16[1024,256]{1,0:T(8,128)(2,1)}, bf16[1024,256]{1,0:T(8,128)(2,1)}, u32[]{:S(2)}, u32[]{:S(2)}) collective-permute-start(bf16[1024,256]{1,0:T(8,128)(2,1)} %add_convert_fusion.1), channel_id=1, source_target_pairs={{0,224},{32,0},{64,32},{96,64},{128,96},{160,128},{192,160},{224,1... | collective-permute-start | bytes 1572872 | tf_op jit(solution)/shard_map/ppermute | solution.py:23
  98.6 26.6 %collective-permute-start.4 = (bf16[1024,256]{1,0:T(8,128)(2,1)}, bf16[1024,256]{1,0:T(8,128)(2,1)}, u32[]{:S(2)}, u32[]{:S(2)}) collective-permute-start(bf16[1024,256]{1,0:T(8,128)(2,1)} %add_convert_fusion.3), channel_id=1, source_target_pairs={{0,32},{32,64},{64,96},{96,128},{128,160},{160,192},{192,224},{224... | collective-permute-start | bytes 1572872 | tf_op jit(solution)/shard_map/ppermute | solution.py:23
  102.1 23.1 %collective-permute-start.8 = (bf16[1024,256]{1,0:T(8,128)(2,1)}, bf16[1024,256]{1,0:T(8,128)(2,1)}, u32[]{:S(2)}, u32[]{:S(2)}) collective-permute-start(bf16[1024,256]{1,0:T(8,128)(2,1)} %add_convert_fusion), channel_id=1, source_target_pairs={{0,224},{32,0},{64,32},{96,64},{128,96},{160,128},{192,160},{224,1... | collective-permute-start | bytes 1572872 | tf_op jit(solution)/shard_map/ppermute | solution.py:23
  105.6 11.7 %all-to-all-start = ((bf16[8,2,32,128]{3,1,2,0:T(2,128)(2,1)}), bf16[8,2,32,128]{3,1,2,0:T(2,128)(2,1)S(1)}, u32[]{:S(2)}, u32[]{:S(2)}) async-start(bf16[8,2,32,128]{3,1,2,0:T(2,128)(2,1)} %copy.15), calls=%async_computation | async-start | bytes 262144 | tf_op jit(solution)/shard_map/all_to_all | solution.py:231
  118.3 32.6 %all-to-all-start.1 = ((bf16[8,256,128]{2,1,0:T(8,128)(2,1)}), bf16[8,256,128]{2,1,0:T(8,128)(2,1)S(1)}, u32[]{:S(2)}, u32[]{:S(2)}) async-start(bf16[8,256,128]{2,1,0:T(8,128)(2,1)} %bitcast.15), calls=%async_computation.1 | async-start | bytes 1048576 | tf_op jit(solution)/shard_map/all_to_all | solution.py:234
  126.6 1.0 copy-start.2
  127.5 27.7 %copy-start.4 = (bf16[128,256]{1,0:T(8,128)(2,1)S(1)}, bf16[128,256]{1,0:T(8,128)(2,1)}, u32[]{:S(2)}) copy-start(bf16[128,256]{1,0:T(8,128)(2,1)} %copy-done.3) | copy-start | bytes 196612
  127.6 7.3 %collective-permute-start.11 = (bf16[1,128,256]{2,1,0:T(8,128)(2,1)S(1)}, bf16[1,128,256]{2,1,0:T(8,128)(2,1)S(1)}, u32[]{:S(2)}, u32[]{:S(2)}) collective-permute-start(bf16[1,128,256]{2,1,0:T(8,128)(2,1)S(1)} %get-tuple-element.25), channel_id=1, source_target_pairs={{0,12},{4,0},{8,4},{12,8},{1,13},{5,1},{9,5},{13,9},{2,14},{6,2},{... | collective-permute-start | bytes 196616 | tf_op jit(solution)/shard_map/ppermute | solution.py:23
  128.2 6.6 %collective-permute-start.9 = (bf16[1,128,256]{2,1,0:T(8,128)(2,1)S(1)}, bf16[1,128,256]{2,1,0:T(8,128)(2,1)S(1)}, u32[]{:S(2)}, u32[]{:S(2)}) collective-permute-start(bf16[1,128,256]{2,1,0:T(8,128)(2,1)S(1)} %get-tuple-element.24), channel_id=1, source_target_pairs={{0,4},{4,8},{8,12},{12,0},{1,5},{5,9},{9,13},{13,1},{2,6},{6,10},{... | collective-permute-start | bytes 196616 | tf_op jit(solution)/shard_map/ppermute | solution.py:23
  135.9 8.7 %collective-permute-start.10 = (bf16[2,128,256]{2,1,0:T(8,128)(2,1)S(1)}, bf16[2,128,256]{2,1,0:T(8,128)(2,1)S(1)}, u32[]{:S(2)}, u32[]{:S(2)}) collective-permute-start(bf16[2,128,256]{2,1,0:T(8,128)(2,1)S(1)} %get-tuple-element.14), channel_id=1, source_target_pairs={{0,4},{4,8},{8,12},{12,0},{1,5},{5,9},{9,13},{13,1},{2,6},{6,10},{... | collective-permute-start | bytes 393224 | tf_op jit(solution)/shard_map/ppermute | solution.py:23
  139.2 9.1 %collective-permute-start.12 = (bf16[2,128,256]{2,1,0:T(8,128)(2,1)S(1)}, bf16[2,128,256]{2,1,0:T(8,128)(2,1)S(1)}, u32[]{:S(2)}, u32[]{:S(2)}) collective-permute-start(bf16[2,128,256]{2,1,0:T(8,128)(2,1)S(1)} %get-tuple-element.15), channel_id=1, source_target_pairs={{0,12},{4,0},{8,4},{12,8},{1,13},{5,1},{9,5},{13,9},{2,14},{6,2},{... | collective-permute-start | bytes 393224 | tf_op jit(solution)/shard_map/ppermute | solution.py:23
  149.4 5.9 %collective-permute-start.13 = (bf16[128,256]{1,0:T(8,128)(2,1)S(1)}, bf16[128,256]{1,0:T(8,128)(2,1)S(1)}, u32[]{:S(2)}, u32[]{:S(2)}) collective-permute-start(bf16[128,256]{1,0:T(8,128)(2,1)S(1)} %fusion.41), channel_id=1, source_target_pairs={{0,16},{16,0},{1,17},{17,1},{2,18},{18,2},{3,19},{19,3},{4,20},{20... | collective-permute-start | bytes 196616 | tf_op jit(solution)/shard_map/ppermute | solution.py:23
  155.5 17.3 %copy-start.5 = (s32[4]{0:T(128)S(1)}, s32[4]{0:T(128)}, u32[]{:S(2)}) copy-start(s32[4]{0:T(128)} %refs_0_.1) | copy-start | bytes 52
  155.5 5.6 %collective-permute-start.15 = (bf16[256,256]{1,0:T(8,128)(2,1)S(1)}, bf16[256,256]{1,0:T(8,128)(2,1)S(1)}, u32[]{:S(2)}, u32[]{:S(2)}) collective-permute-start(bf16[256,256]{1,0:T(8,128)(2,1)S(1)} %get-tuple-element.22), channel_id=1, source_target_pairs={{0,4},{4,8},{8,12},{12,0},{1,5},{5,9},{9,13},{13,1},{2,6},{6,10},{... | collective-permute-start | bytes 393224 | tf_op jit(solution)/shard_map/ppermute | solution.py:23
  155.6 7.9 %collective-permute-start.17 = (bf16[256,256]{1,0:T(8,128)(2,1)S(1)}, bf16[256,256]{1,0:T(8,128)(2,1)S(1)}, u32[]{:S(2)}, u32[]{:S(2)}) collective-permute-start(bf16[256,256]{1,0:T(8,128)(2,1)S(1)} %get-tuple-element.23), channel_id=1, source_target_pairs={{0,12},{4,0},{8,4},{12,8},{1,13},{5,1},{9,5},{13,9},{2,14},{6,2},{... | collective-permute-start | bytes 393224 | tf_op jit(solution)/shard_map/ppermute | solution.py:23
  161.3 6.4 %collective-permute-start.16 = (bf16[512,256]{1,0:T(8,128)(2,1)S(1)}, bf16[512,256]{1,0:T(8,128)(2,1)S(1)}, u32[]{:S(2)}, u32[]{:S(2)}) collective-permute-start(bf16[512,256]{1,0:T(8,128)(2,1)S(1)} %fusion.1), channel_id=1, source_target_pairs={{0,4},{4,8},{8,12},{12,0},{1,5},{5,9},{9,13},{13,1},{2,6},{6,10},{... | collective-permute-start | bytes 786440 | tf_op jit(solution)/shard_map/ppermute | solution.py:23
  163.7 7.7 %collective-permute-start.18 = (bf16[512,256]{1,0:T(8,128)(2,1)S(1)}, bf16[512,256]{1,0:T(8,128)(2,1)S(1)}, u32[]{:S(2)}, u32[]{:S(2)}) collective-permute-start(bf16[512,256]{1,0:T(8,128)(2,1)S(1)} %fusion.2), channel_id=1, source_target_pairs={{0,12},{4,0},{8,4},{12,8},{1,13},{5,1},{9,5},{13,9},{2,14},{6,2},{... | collective-permute-start | bytes 786440 | tf_op jit(solution)/shard_map/ppermute | solution.py:23
  171.6 6.6 %collective-permute-start.19 = (bf16[2,2,2,32,256]{4,3,2,1,0:T(8,128)(2,1)S(1)}, bf16[2,2,2,32,256]{4,3,2,1,0:T(8,128)(2,1)S(1)}, u32[]{:S(2)}, u32[]{:S(2)}) collective-permute-start(bf16[2,2,2,32,256]{4,3,2,1,0:T(8,128)(2,1)S(1)} %fusion.37), channel_id=1, source_target_pairs={{0,16},{16,0},{1,17},{17,1},{2,18},{18,2},{3,19},{19,3},{4,20},{20... | collective-permute-start | bytes 393224 | tf_op jit(solution)/shard_map/ppermute | solution.py:23
  178.2 1.4 collective-permute-start.20
  179.7 10.1 %collective-permute-start.21 = (f32[2,32,256]{2,1,0:T(8,128)S(1)}, f32[2,32,256]{2,1,0:T(8,128)S(1)}, u32[]{:S(2)}, u32[]{:S(2)}) collective-permute-start(f32[2,32,256]{2,1,0:T(8,128)S(1)} %dynamic-slice_bitcast_fusion.2), channel_id=1, source_target_pairs={{0,2},{2,0},{1,3},{3,1},{4,6},{6,4},{5,7},{7,5},{8,10},{10,8},{9,1... | collective-permute-start | bytes 196616 | tf_op jit(solution)/shard_map/ppermute | solution.py:23
  181.0 26.3 %collective-permute-start.14 = (bf16[128,256]{1,0:T(8,128)(2,1)S(1)}, bf16[128,256]{1,0:T(8,128)(2,1)S(1)}, u32[]{:S(2)}, u32[]{:S(2)}) collective-permute-start(bf16[128,256]{1,0:T(8,128)(2,1)S(1)} %fusion.40), channel_id=1, source_target_pairs={{0,0},{1,64},{2,128},{3,192},{32,32},{33,96},{34,160},{35,224},{64... | collective-permute-start | bytes 196616 | tf_op jit(solution)/shard_map/ppermute | solution.py:31
  189.8 17.5 %collective-permute-start.22 = (f32[32,256]{1,0:T(8,128)S(1)}, f32[32,256]{1,0:T(8,128)S(1)}, u32[]{:S(2)}, u32[]{:S(2)}) collective-permute-start(f32[32,256]{1,0:T(8,128)S(1)} %get-tuple-element.27), channel_id=1, source_target_pairs={{0,0},{1,64},{2,128},{3,192},{32,32},{33,96},{34,160},{35,224},{64... | collective-permute-start | bytes 98312 | tf_op jit(solution)/shard_map/ppermute | solution.py:31
  191.9 15.4 %collective-permute-start.23 = (f32[32,256]{1,0:T(8,128)S(1)}, f32[32,256]{1,0:T(8,128)S(1)}, u32[]{:S(2)}, u32[]{:S(2)}) collective-permute-start(f32[32,256]{1,0:T(8,128)S(1)} %get-tuple-element.26), channel_id=1, source_target_pairs={{0,32},{1,96},{2,160},{3,224},{32,0},{33,64},{34,128},{35,192},{64... | collective-permute-start | bytes 98312 | tf_op jit(solution)/shard_map/ppermute | solution.py:31
Sparse Core Ops, SparseCore 0:
  69.6 26.4 all-gather.5
  97.9 54.5 all-gather.7

commit v2 on v1

--- a/solution.py
+++ b/solution.py
@@ -105,90 +105,88 @@
 
 
 def fresh_kernel(
-    raw_ref, cos_ref, sin_ref, q_ref, v_ref, mixed_ref, top_ref, total_ref, keys_ref, out_ref, *, share
+    same_ref, other_ref, cos_ref, sin_ref, q_ref, v_ref, mixed_ref, top_ref, total_ref, keys_ref, out_ref
 ):
-    raw = raw_ref[...]
-    keys = raw * cos_ref[...] + pltpu.roll(raw, HD // 2, 1) * sin_ref[...]
-    keys = keys.astype(BF16)
-    keys_ref[0] = keys
-    steps = keys.shape[0]
-    query = stacked(q_ref[0], share).astype(BF16)
-    scores = lax.dot_general(
-        query, keys, (((1,), (1,)), ((), ())), preferred_element_type=F32
-    ) * (1.0 / math.sqrt(HD))
-    step = lax.broadcasted_iota(jnp.int32, scores.shape, 0) % steps
-    scores = jnp.where(lax.broadcasted_iota(jnp.int32, scores.shape, 1) <= step, scores, -jnp.inf)
-    top = top_ref[0, 0]
-    high = jnp.maximum(top, jnp.max(scores, axis=1, keepdims=True))
-    old = jnp.exp(top - high)
-    weight = jnp.exp(scores - high[:, :1])
-    whole = total_ref[0, 0] * old + jnp.sum(weight, axis=1, keepdims=True)
-    fresh = jnp.dot(weight.astype(BF16), v_ref[0], preferred_element_type=F32)
-    context = ((mixed_ref[0, 0] * old + fresh) / whole).astype(BF16).astype(F32)
-    flat = [context[h * steps : (h + 1) * steps] for h in range(share)]
-    out_ref[0] = jnp.concatenate(flat, axis=1).astype(BF16)
-
-
-def attend_fresh(raw, cosine, sine, queries, new_values, mixed, top, total):
-    count, steps, width = queries.shape
-    groups = new_values.shape[2] // HD
-    share = width // new_values.shape[2]
-    state_spec = pl.BlockSpec((1, 1, share * steps, HD), lambda r, j: (r, j, 0, 0))
-    query_spec = pl.BlockSpec((1, steps, share * HD), lambda r, j: (r, 0, j))
-    value_spec = pl.BlockSpec((1, steps, HD), lambda r, j: (r, 0, j))
-    angle_spec = pl.BlockSpec((steps, HD), lambda r, j: (r, 0))
+    count, steps, width = q_ref.shape
+    groups = v_ref.shape[2] // HD
+    share = width // v_ref.shape[2]
+    for r in range(count):
+        lines = slice(r * steps, (r + 1) * steps)
+        for j in range(groups):
+            lanes = slice(j * HD, (j + 1) * HD)
+            heads = slice(j * share * HD, (j + 1) * share * HD)
+            raw = same_ref[lines, lanes] + other_ref[lines, lanes]
+            keys = raw * cos_ref[lines, :] + pltpu.roll(raw, HD // 2, 1) * sin_ref[lines, :]
+            keys = keys.astype(BF16)
+            keys_ref[r, :, lanes] = keys
+            query = stacked(q_ref[r, :, heads], share).astype(BF16)
+            scores = lax.dot_general(
+                query, keys, (((1,), (1,)), ((), ())), preferred_element_type=F32
+            ) * (1.0 / math.sqrt(HD))
+            step = lax.broadcasted_iota(jnp.int32, scores.shape, 0) % steps
+            seen = lax.broadcasted_iota(jnp.int32, scores.shape, 1) <= step
+            scores = jnp.where(seen, scores, -jnp.inf)
+            top = top_ref[r, j]
+            high = jnp.maximum(top, jnp.max(scores, axis=1, keepdims=True))
+            old = jnp.exp(top - high)
+            weight = jnp.exp(scores - high[:, :1])
+            whole = total_ref[r, j] * old + jnp.sum(weight, axis=1, keepdims=True)
+            fresh = jnp.dot(weight.astype(BF16), v_ref[r, :, lanes], preferred_element_type=F32)
+            context = (mixed_ref[r, j] * old + fresh) / whole
+            flat = [context[h * steps : (h + 1) * steps] for h in range(share)]
+            out_ref[r, :, heads] = jnp.concatenate(flat, axis=1).astype(BF16)
+
+
+def attend_fresh(same, other, cosine, sine, queries, new_values, mixed, top, total):
     return pl.pallas_call(
-        lambda *refs: fresh_kernel(*refs, share=share),
+        fresh_kernel,
         out_shape=(
             jax.ShapeDtypeStruct(new_values.shape, BF16),
             jax.ShapeDtypeStruct(queries.shape, BF16),
         ),
-        grid=(count, groups),
-        in_specs=[
-            pl.BlockSpec((steps, HD), lambda r, j: (r, j)),
-            angle_spec,
-            angle_spec,
-            query_spec,
-            value_spec,
-            state_spec,
-            state_spec,
-            state_spec,
-        ],
-        out_specs=[value_spec, query_spec],
         name="fresh_attention",
-    )(raw, cosine, sine, queries, new_values, mixed, top, total)
-
-
-def input_kernel(m_ref, w_ref, out_ref):
-    blocks, cols = w_ref.shape[2], w_ref.shape[5]
+    )(same, other, cosine, sine, queries, new_values, mixed, top, total)
+
+
+def input_kernel(place, m_ref, w_ref, *refs):
+    out_ref = refs[-1]
+    blocks, cols = w_ref.shape[1], w_ref.shape[4]
     total = jnp.zeros(out_ref.shape, F32)
     for block in range(blocks):
         total += lax.dot_general(
             m_ref[:, block * cols : (block + 1) * cols],
-            w_ref[0, 0, block, 0],
+            w_ref[0, block, 0],
             (((1,), (1,)), ((), ())),
             preferred_element_type=F32,
         )
     out_ref[...] = total.astype(BF16)
 
 
-def input_grad(masked, weight):
-    ny, nx, blocks, two, rows, cols = weight.shape
+def input_grad(masked, weight, place, out, wide):
+    pieces, blocks, two, rows, cols = weight.shape
     count = masked.shape[0]
+    more = [] if out is None else [out]
     return pl.pallas_call(
         input_kernel,
-        out_shape=jax.ShapeDtypeStruct((count, two * nx * ny * rows), BF16),
-        grid=(ny, nx, two),
-        in_specs=[
-            pl.BlockSpec((count, blocks * cols), lambda i, k, j: (0, 0)),
-            pl.BlockSpec((1, 1, blocks, 1, rows, cols), lambda i, k, j: (i, k, 0, j, 0, 0)),
-        ],
-        out_specs=pl.BlockSpec((count, rows), lambda i, k, j: (0, (j * nx + k) * ny + i)),
+        out_shape=jax.ShapeDtypeStruct((count, wide), BF16),
+        grid_spec=pltpu.PrefetchScalarGridSpec(
+            num_scalar_prefetch=1,
+            grid=(pieces, two),
+            in_specs=[
+                pl.BlockSpec((count, blocks * cols), lambda q, j, n: (0, 0)),
+                pl.BlockSpec((1, blocks, 1, rows, cols), lambda q, j, n: (q, 0, j, 0, 0)),
+            ]
+            + [pl.BlockSpec(memory_space=pl.ANY) for _ in more],
+            out_specs=pl.BlockSpec(
+                (count, rows), lambda q, j, n: (0, j * NX * NY + (q ^ n[0]) * NY + n[1])
+            ),
+        ),
+        input_output_aliases={3: 0} if more else {},
         cost_estimate=pl.CostEstimate(
             flops=2 * count * weight.size, bytes_accessed=2 * weight.size, transcendentals=0
         ),
         name="input_grad",
-    )(masked, weight)
+    )(jnp.stack(place).astype(jnp.int32), masked, weight, *more)
 
 
 def angles(lengths, steps):
@@ -232,13 +230,18 @@
     hidden = hidden.transpose(1, 0, 2, 3).reshape(1, 2, NX * NY * lines, rows)
     hidden = jnp.broadcast_to(hidden, (NZ // 2,) + hidden.shape[1:]).reshape(NZ, NX * NY * lines, rows)
     hidden = lax.all_to_all(hidden, "z", 0, 0, tiled=True)
-    hidden = hidden.reshape(NZ, NX, NY, lines, rows)
+    hidden = hidden.reshape(NZ, NX * NY, lines, rows).transpose(1, 0, 2, 3).reshape(-1, rows)
 
     own_weight = swap_owner(key_weight)
-    old = lax.all_gather(own_weight, "z")
-    old = lax.all_gather(old, "xh")
-    old = lax.all_gather(old, "y")
-    old = old.reshape(NY, NX, NL * NC, 2, rows, cols)
+    old = jnp.broadcast_to(own_weight, (NZ, rows, cols))
+    old = lax.all_to_all(old, "z", 0, 0, tiled=True)
+    old = old.reshape(NL * NC, 2, rows, cols)
+    other = shift(old, "xh", NX, 1)
+    old = jnp.stack([old, other])
+    up = shift(old, "y", NY, 1)
+    down = shift(old, "y", NY, -1)
+    far_up = shift(up[:1], "y", NY, 1)
+    far_down = shift(down[1:], "y", NY, -1)
 
     def term(k):
         left = lax.dynamic_slice_in_dim(tokens, (k & 1) * (wide // 2), wide // 2, 1)
@@ -246,35 +249,39 @@
         return lax.dot_general(left, right, (((0,), (0,)), ((), ())), preferred_element_type=F32)
 
     part = ring_sum(term, "z", NZ, z).reshape(NX, NY, rows, cols)
-    part = ring_sum(lambda k: pick(part, k, 1), "y", NY, y)
-    other = shift(pick(part, 1 - xh, 0).astype(BF16), "xh", NX, 1)
-    grad = pick(part, xh, 0) + other.astype(F32)
+    part = part.astype(BF16).reshape(NX * NY, rows, cols)
+    part = lax.all_to_all(part, ("xh", "y"), 0, 0, tiled=True)
+    grad = jnp.sum(part.astype(F32), axis=0)
 
     scale = 1.0 / math.sqrt(D * tokens.shape[0] * NZ * NX * NY)
     own_weight = (own_weight.astype(F32) - grad * scale).astype(BF16)
 
-    def raw_term(k):
-        left = pick(hidden, k, 2).reshape(NZ * NX * lines, rows)
-        return jnp.dot(left, own_weight, preferred_element_type=F32)
-
-    raw = ring_sum(raw_term, "y", NY, y).reshape(NL, NC, 2, NX, lines, cols)
-    other = shift(pick(raw, 1 - xh, 3).astype(BF16), "xh", NX, 1)
-    raw = pick(raw, xh, 3) + other.astype(F32)
+    raw = jnp.dot(hidden, own_weight, preferred_element_type=F32).astype(BF16)
+    raw = raw.reshape(NX * NY, NZ * lines, cols)
+    raw = lax.all_to_all(raw, ("xh", "y"), 0, 0, tiled=True)
+    raw = jnp.sum(raw.astype(F32), axis=0).reshape(NL, NC, 2, lines, cols)
     other = shift(pick(raw, 1 - c, 1), "c", NC, 1)
     raw = pick(raw, c, 1) + other
     other = shift(pick(raw, 1 - xl, 0), "xl", NL, 1)
     raw = pick(raw, xl, 0) + other
     same = swap_owner(pick(raw, odd, 0))
     other = swap_owner(pick(raw, 1 - odd, 0), 1)
-    raw = same + other
 
     learner_weight = swap_owner(own_weight)
 
     state = attend_cache(queries, cache_keys, cache_values, cache_lengths)
     cosine, sine = angles(cache_lengths, steps)
-    new_keys, context = attend_fresh(raw, cosine, sine, queries, new_values, *state)
-
-    grad_inputs = input_grad(masked_all, old)
+    new_keys, context = attend_fresh(same, other, cosine, sine, queries, new_values, *state)
+
+    grad_inputs = None
+    for weight, across, owner in (
+        (old, xh, y),
+        (up, xh, (y - 1) & (NY - 1)),
+        (down, xh, (y + 1) & (NY - 1)),
+        (far_up, xh, y ^ 2),
+        (far_down, 1 - xh, y ^ 2),
+    ):
+        grad_inputs = input_grad(masked_all, weight, (across, owner), grad_inputs, wide)
     return (grad_inputs, learner_weight, new_keys, context)
 
 

time: 236 us -> 210 us (0.89)
  the two profiles are of different devices: /device:TPU:26 before, /device:TPU:1 now
where the time goes in v2:
time: 210 us; the launch traced here: 206 us
  starting transfers between devices  66.6 us (32%)
  waiting for transfers between devices  56.2 us (27%)
  Pallas kernels  33.6 us (16%)
  other arithmetic  18.3 us (9%)
  local copies, waits for them, and re-layouts  12 us (6%)
  blocking collectives  10.3 us (5%)
  matrix products  7.75 us (4%)
    ppermute x15, waiting for transfers between devices, shift(): return lax.ppermute(x, axis, [(i, (i + step) % size) for i in range(size)])  45.1 us
    ppermute x15, starting transfers between devices, shift(): return lax.ppermute(x, axis, [(i, (i + step) % size) for i in range(size)])  31.9 us
    pallas_call x5, Pallas kernels, input_grad(): pl.pallas_call(input_kernel, out_shape=jax.ShapeDtypeStruct((count, wide)...  21.3 us
    all_gather x1, blocking collectives, update_and_decode(): masked_all = lax.all_gather(masked, TP, axis=1, tiled=True)  10.3 us
    pallas_call x1, Pallas kernels, attend_cache(): pl.pallas_call(lambda *refs: cache_kernel(*refs, share=share), out_shape=...  9.55 us
    ppermute x4, starting transfers between devices, swap_owner(): return lax.ppermute(x, ('z', 'xl', 'c'), pairs)  8.55 us
    all_to_all x1, starting transfers between devices, update_and_decode(): part = lax.all_to_all(part, ('xh', 'y'), 0, 0, tiled=True)  6.43 us
    dot_general x8, matrix products, term(): lax.dot_general(left, right, (((0,), (0,)), ((), ())), preferred_element_...  6.37 us
  transfers between devices with their start and end apart: 24, of which 8 were waited for; matrix products, arithmetic and copies ran while one was open for 16% of the time, Pallas kernels for 15%

profile of v2, /device:TPU:1, one launch (start us, length us, event | category | flops | bytes accessed | tf_op | source)
XLA Modules:
  0.0 205.6 jit_solution(8346378136898610239)
XLA Ops:
  0.7 0.8 convert_element_type.81
  1.5 1.0 broadcast_multiply_fusion
  2.5 10.3 %all_gather.3.m_ref = bf16[384,1024]{1,0:T(8,128)(2,1)S(1)} all-gather(bf16[384,256]{1,0:T(8,128)(2,1)S(1)} %broadcast_multiply_fusion), channel_id=1, replica_groups=mesh['z'=8,'xh'=2,'y'=4,'xl'=2,'c'=2] {'xl','c'}, dimensions={1}, use_global_device_ids=true | all-gather | bytes 983040 | tf_op jit(solution)/shard_map/all_gather | solution.py:224
  13.3 5.3 %collective-permute-start.10 = (bf16[512,256]{1,0:T(8,128)(2,1)S(1)}, bf16[512,256]{1,0:T(8,128)(2,1)S(1)}, u32[]{:S(2)}, u32[]{:S(2)}) collective-permute-start(bf16[512,256]{1,0:T(8,128)(2,1)S(1)} %get-tuple-element.15), channel_id=1, source_target_pairs={{0,224},{32,0},{64,32},{96,64},{128,96},{160,128},{192,160},{224,1... | collective-permute-start | bytes 786440 | tf_op jit(solution)/shard_map/ppermute | solution.py:23
  18.6 5.5 %collective-permute-done.10 = bf16[512,256]{1,0:T(8,128)(2,1)S(1)} collective-permute-done((bf16[512,256]{1,0:T(8,128)(2,1)S(1)}, bf16[512,256]{1,0:T(8,128)(2,1)S(1)}, u32[]{:S(2)}, u32[]{:S(2)}) %collective-permute-start.10) | collective-permute-done | bytes 262176 | tf_op jit(solution)/shard_map/ppermute | solution.py:23
  24.1 1.3 add_convert_fusion.3
  25.4 3.4 %collective-permute-start.11 = (bf16[1024,256]{1,0:T(8,128)(2,1)}, bf16[1024,256]{1,0:T(8,128)(2,1)}, u32[]{:S(2)}, u32[]{:S(2)}) collective-permute-start(bf16[1024,256]{1,0:T(8,128)(2,1)} %add_convert_fusion.3), channel_id=1, source_target_pairs={{0,224},{32,0},{64,32},{96,64},{128,96},{160,128},{192,160},{224,1... | collective-permute-start | bytes 1572872 | tf_op jit(solution)/shard_map/ppermute | solution.py:23
  28.8 1.9 collective-permute-start
  30.7 0.9 dynamic-slice_bitcast_fusion.1
  31.7 0.8 copy.20
  32.4 6.4 %all-to-all-start.2 = ((bf16[8,2,32,128]{3,1,2,0:T(2,128)(2,1)}), bf16[8,2,32,128]{3,1,2,0:T(2,128)(2,1)S(1)}, u32[]{:S(2)}, u32[]{:S(2)}) async-start(bf16[8,2,32,128]{3,1,2,0:T(2,128)(2,1)} %copy.20), calls=%async_computation.2 | async-start | bytes 262144 | tf_op jit(solution)/shard_map/all_to_all | solution.py:229
  38.8 1.3 add_convert_fusion.6
  40.2 1.4 fusion.2
  42.2 3.6 %all-to-all-done.2 = bf16[8,2,32,128]{3,1,2,0:T(2,128)(2,1)S(1)} async-done(((bf16[8,2,32,128]{3,1,2,0:T(2,128)(2,1)}), bf16[8,2,32,128]{3,1,2,0:T(2,128)(2,1)S(1)}, u32[]{:S(2)}, u32[]{:S(2)}) %all-to-all-start.2) | async-done | bytes 131104 | tf_op jit(solution)/shard_map/all_to_all | solution.py:229
  45.7 1.7 broadcast_in_dim.6
  47.5 4.1 %all-to-all-start = ((bf16[8,128,256]{2,1,0:T(8,128)(2,1)}), bf16[8,128,256]{2,1,0:T(8,128)(2,1)}, u32[]{:S(2)}, u32[]{:S(2)}) async-start(bf16[8,128,256]{2,1,0:T(8,128)(2,1)} %broadcast_in_dim.6), calls=%async_computation | async-start | bytes 1048576 | tf_op jit(solution)/shard_map/all_to_all | solution.py:237
  51.6 1.5 add_convert_fusion.2
  53.1 2.7 %collective-permute-start.12 = (bf16[1024,256]{1,0:T(8,128)(2,1)S(1)}, bf16[1024,256]{1,0:T(8,128)(2,1)S(1)}, u32[]{:S(2)}, u32[]{:S(2)}) collective-permute-start(bf16[1024,256]{1,0:T(8,128)(2,1)S(1)} %add_convert_fusion.2), channel_id=1, source_target_pairs={{0,224},{32,0},{64,32},{96,64},{128,96},{160,128},{192,160},{224,1... | collective-permute-start | bytes 1572872 | tf_op jit(solution)/shard_map/ppermute | solution.py:23
  55.8 2.0 add_convert_fusion.5
  58.7 14.2 %collective-permute-done.12 = bf16[1024,256]{1,0:T(8,128)(2,1)S(1)} collective-permute-done((bf16[1024,256]{1,0:T(8,128)(2,1)S(1)}, bf16[1024,256]{1,0:T(8,128)(2,1)S(1)}, u32[]{:S(2)}, u32[]{:S(2)}) %collective-permute-start.12) | collective-permute-done | bytes 524320 | tf_op jit(solution)/shard_map/ppermute | solution.py:23
  73.0 0.9 add_convert_fusion.1
  73.9 2.8 %collective-permute-start.13 = (bf16[1024,256]{1,0:T(8,128)(2,1)}, bf16[1024,256]{1,0:T(8,128)(2,1)}, u32[]{:S(2)}, u32[]{:S(2)}) collective-permute-start(bf16[1024,256]{1,0:T(8,128)(2,1)} %add_convert_fusion.1), channel_id=1, source_target_pairs={{0,224},{32,0},{64,32},{96,64},{128,96},{160,128},{192,160},{224,1... | collective-permute-start | bytes 1572872 | tf_op jit(solution)/shard_map/ppermute | solution.py:23
  76.7 0.9 broadcast_in_dim.8
  77.6 5.6 %all-to-all-start.3 = ((bf16[8,256,128]{2,1,0:T(8,128)(2,1)}), bf16[8,256,128]{2,1,0:T(8,128)(2,1)}, u32[]{:S(2)}, u32[]{:S(2)}) async-start(bf16[8,256,128]{2,1,0:T(8,128)(2,1)} %bitcast.43), calls=%async_computation.3 | async-start | bytes 1048576 | tf_op jit(solution)/shard_map/all_to_all | solution.py:232
  83.2 2.0 add_convert_fusion.4
  85.2 1.5 collective-permute-start.9
  87.2 20.0 %collective-permute-done.9 = bf16[1024,256]{1,0:T(8,128)(2,1)S(1)} collective-permute-done((bf16[1024,256]{1,0:T(8,128)(2,1)}, bf16[1024,256]{1,0:T(8,128)(2,1)S(1)}, u32[]{:S(2)}, u32[]{:S(2)}) %collective-permute-start.9) | collective-permute-done | bytes 524320 | tf_op jit(solution)/shard_map/ppermute | solution.py:23
  107.2 2.0 add_convert_fusion
  109.2 6.4 %all-to-all-start.1 = ((bf16[8,128,256]{2,1,0:T(8,128)(2,1)}), bf16[8,128,256]{2,1,0:T(8,128)(2,1)S(1)}, u32[]{:S(2)}, u32[]{:S(2)}) async-start(bf16[8,128,256]{2,1,0:T(8,128)(2,1)} %bitcast.9), calls=%async_computation.1 | async-start | bytes 1048576 | tf_op jit(solution)/shard_map/all_to_all | solution.py:253
  115.7 3.2 %collective-permute-start.1 = (bf16[4,2,128,256]{3,2,1,0:T(8,128)(2,1)}, bf16[4,2,128,256]{3,2,1,0:T(8,128)(2,1)S(1)}, u32[]{:S(2)}, u32[]{:S(2)}) collective-permute-start(bf16[4,2,128,256]{3,2,1,0:T(8,128)(2,1)} %bitcast.3), channel_id=1, source_target_pairs={{0,16},{16,0},{1,17},{17,1},{2,18},{18,2},{3,19},{19,3},{4,20},{20... | collective-permute-start | bytes 1572872 | tf_op jit(solution)/shard_map/ppermute | solution.py:23
  118.9 1.1 copy.22
  120.0 4.5 %all-to-all-done.1 = bf16[8,128,256]{2,1,0:T(8,128)(2,1)S(1)} async-done(((bf16[8,128,256]{2,1,0:T(8,128)(2,1)}), bf16[8,128,256]{2,1,0:T(8,128)(2,1)S(1)}, u32[]{:S(2)}, u32[]{:S(2)}) %all-to-all-start.1) | async-done | bytes 524320 | tf_op jit(solution)/shard_map/all_to_all | solution.py:253
  124.5 0.9 subtract_convert_fusion
  125.4 1.4 convolution_convert_fusion
  126.8 3.6 %all-to-all-start.4 = ((bf16[8,256,256]{2,1,0:T(8,128)(2,1)}), bf16[8,256,256]{2,1,0:T(8,128)(2,1)S(1)}, u32[]{:S(2)}, u32[]{:S(2)}) async-start(bf16[8,256,256]{2,1,0:T(8,128)(2,1)} %bitcast.41), calls=%async_computation.4 | async-start | bytes 2097152 | tf_op jit(solution)/shard_map/all_to_all | solution.py:261
  130.3 0.6 pad_add_fusion.3.place
  131.0 3.2 %collective-permute-done.1 = bf16[4,2,128,256]{3,2,1,0:T(8,128)(2,1)S(1)} collective-permute-done((bf16[4,2,128,256]{3,2,1,0:T(8,128)(2,1)}, bf16[4,2,128,256]{3,2,1,0:T(8,128)(2,1)S(1)}, u32[]{:S(2)}, u32[]{:S(2)}) %collective-permute-start.1) | collective-permute-done | bytes 524320 | tf_op jit(solution)/shard_map/ppermute | solution.py:23
  134.2 2.1 %pad_maximum_fusion.w_ref = bf16[2,4,2,128,256]{4,3,2,1,0:T(8,128)(2,1)} fusion(bf16[1,4,2,128,256]{4,3,2,1,0:T(8,128)(2,1)S(1)} %bitcast.48, bf16[1,4,2,128,256]{4,3,2,1,0:T(8,128)(2,1)} %bitcast.2), kind=kLoop, calls=%fused_computation.3 | loop fusion | flops 524288 | bytes 2097152 | tf_op jit(solution)/shard_map/stack | solution.py:240
  136.3 1.2 collective-permute-start.4
  137.5 1.5 collective-permute-start.2
  139.7 0.7 pad_add_fusion.1.place
  140.3 0.6 pad_add_fusion.4.place
  141.1 0.7 pad_maximum_fusion.1
  141.8 3.0 %all-to-all-done.4 = bf16[8,256,256]{2,1,0:T(8,128)(2,1)S(1)} async-done(((bf16[8,256,256]{2,1,0:T(8,128)(2,1)}), bf16[8,256,256]{2,1,0:T(8,128)(2,1)S(1)}, u32[]{:S(2)}, u32[]{:S(2)}) %all-to-all-start.4) | async-done | bytes 1048608 | tf_op jit(solution)/shard_map/all_to_all | solution.py:261
  145.0 5.1 %collective-permute-start.15 = (f32[2,2,32,256]{3,2,1,0:T(8,128)S(1)}, f32[2,2,32,256]{3,2,1,0:T(8,128)}, u32[]{:S(2)}, u32[]{:S(2)}) collective-permute-start(f32[2,2,32,256]{3,2,1,0:T(8,128)S(1)} %dynamic-slice_bitcast_fusion), channel_id=1, source_target_pairs={{0,1},{1,0},{2,3},{3,2},{4,5},{5,4},{6,7},{7,6},{8,9},{9,8},{10,11... | collective-permute-start | bytes 393224 | tf_op jit(solution)/shard_map/ppermute | solution.py:23
  150.7 1.9 collective-permute-start.14
  152.6 9.6 %cache_attention.1 = (f32[4,2,64,128]{3,2,1,0:T(8,128)}, f32[4,2,64,128]{3,2,1,0:T(8,128)}, f32[4,2,64,128]{3,2,1,0:T(8,128)}) custom-call(s32[4]{0:T(128)} %refs_0_.1, bf16[4,8,2048]{2,1,0:T(8,128)(2,1)} %q_ref.1, bf16[4,2048,256]{2,1,0:T(8,128)(2,1)} %refs_2_.1, bf16[4,2048,256]{2,1,0:T(8,128)(2,1)} %refs_3_.1), custom_call_target="tpu_custom_call" | custom-call | flops 536870912 | bytes 8388608 | tf_op jit(solution)/shard_map/cache_attention/pallas_call | solution.py:85
  162.1 4.9 %input_grad.5.refs_0_ = bf16[384,2048]{1,0:T(8,128)(2,1)} custom-call(s32[2]{0:T(128)} %pad_add_fusion.3.place, bf16[384,1024]{1,0:T(8,128)(2,1)} %copy-done.1, bf16[2,4,2,128,256]{4,3,2,1,0:T(8,128)(2,1)} %pad_maximum_fusion.w_ref), custom_call_target="tpu_custom_call" | custom-call | flops 402653184 | bytes 1048576 | tf_op jit(solution)/shard_map/input_grad/pallas_call | solution.py:169
  167.7 2.0 collective-permute-done.4.w_ref
  169.7 1.1 slice.17
  170.9 1.9 slice.16
  172.8 2.7 %collective-permute-start.3 = (bf16[1,4,2,128,256]{4,3,2,1,0:T(8,128)(2,1)}, bf16[1,4,2,128,256]{4,3,2,1,0:T(8,128)(2,1)S(1)}, u32[]{:S(2)}, u32[]{:S(2)}) collective-permute-start(bf16[1,4,2,128,256]{4,3,2,1,0:T(8,128)(2,1)} %slice.16), channel_id=1, source_target_pairs={{0,12},{4,0},{8,4},{12,8},{1,13},{5,1},{9,5},{13,9},{2,14},{6,2},{... | collective-permute-start | bytes 1572872 | tf_op jit(solution)/shard_map/ppermute | solution.py:23
  175.4 0.9 bitcast_add_fusion
  176.4 2.5 %collective-permute-start.16 = (f32[2,32,256]{2,1,0:T(8,128)S(1)}, f32[2,32,256]{2,1,0:T(8,128)S(1)}, u32[]{:S(2)}, u32[]{:S(2)}) collective-permute-start(f32[2,32,256]{2,1,0:T(8,128)S(1)} %dynamic-slice_bitcast_fusion.2), channel_id=1, source_target_pairs={{0,2},{2,0},{1,3},{3,1},{4,6},{6,4},{5,7},{7,5},{8,10},{10,8},{9,1... | collective-permute-start | bytes 196616 | tf_op jit(solution)/shard_map/ppermute | solution.py:23
  178.8 4.9 %input_grad.6.refs_0_ = bf16[384,2048]{1,0:T(8,128)(2,1)} custom-call(s32[2]{0:T(128)} %pad_add_fusion.2.place, bf16[384,1024]{1,0:T(8,128)(2,1)} %copy-done.1, bf16[2,4,2,128,256]{4,3,2,1,0:T(8,128)(2,1)} %collective-permute-done.4.w_ref, bf16[384,2048]{1,0:T(8,128)(2,1)} %input_grad.5.refs_0_), custom_call_target="tpu_custom_call", output_to_operand_aliasing={{}: (3, {})} | custom-call | flops 402653184 | bytes 1048576 | tf_op jit(solution)/shard_map/input_grad/pallas_call | solution.py:169
  183.7 4.9 %input_grad.7.refs_0_ = bf16[384,2048]{1,0:T(8,128)(2,1)} custom-call(s32[2]{0:T(128)} %pad_add_fusion.1.place, bf16[384,1024]{1,0:T(8,128)(2,1)} %copy-done.1, bf16[2,4,2,128,256]{4,3,2,1,0:T(8,128)(2,1)} %collective-permute-done.2.w_ref, bf16[384,2048]{1,0:T(8,128)(2,1)} %input_grad.6.refs_0_), custom_call_target="tpu_custom_call", output_to_operand_aliasing={{}: (3, {})} | custom-call | flops 402653184 | bytes 1048576 | tf_op jit(solution)/shard_map/input_grad/pallas_call | solution.py:169
  188.7 3.8 %collective-permute-start.17 = (f32[32,256]{1,0:T(8,128)S(1)}, f32[32,256]{1,0:T(8,128)S(1)}, u32[]{:S(2)}, u32[]{:S(2)}) collective-permute-start(f32[32,256]{1,0:T(8,128)S(1)} %get-tuple-element.17), channel_id=1, source_target_pairs={{0,0},{1,64},{2,128},{3,192},{32,32},{33,96},{34,160},{35,224},{64... | collective-permute-start | bytes 98312 | tf_op jit(solution)/shard_map/ppermute | solution.py:31
  192.4 1.0 collective-permute-start.18
  193.4 0.8 copy-done.2
  194.2 3.3 %input_grad.8.refs_0_ = bf16[384,2048]{1,0:T(8,128)(2,1)} custom-call(s32[2]{0:T(128)} %pad_add_fusion.4.place, bf16[384,1024]{1,0:T(8,128)(2,1)} %copy-done.1, bf16[1,4,2,128,256]{4,3,2,1,0:T(8,128)(2,1)} %copy-done.2, bf16[384,2048]{1,0:T(8,128)(2,1)} %input_grad.7.refs_0_), custom_call_target="tpu_custom_call", output_to_operand_aliasing={{}: (3, {})} | custom-call | flops 201326592 | bytes 524288 | tf_op jit(solution)/shard_map/input_grad/pallas_call | solution.py:169
  197.5 0.8 copy-done.3
  198.3 3.3 %input_grad.9 = bf16[384,2048]{1,0:T(8,128)(2,1)} custom-call(s32[2]{0:T(128)} %pad_add_fusion.place, bf16[384,1024]{1,0:T(8,128)(2,1)} %copy-done.1, bf16[1,4,2,128,256]{4,3,2,1,0:T(8,128)(2,1)} %copy-done.3, bf16[384,2048]{1,0:T(8,128)(2,1)} %input_grad.8.refs_0_), custom_call_target="tpu_custom_call", output_to_operand_aliasing={{}: (3, {})} | custom-call | flops 201326592 | bytes 524288 | tf_op jit(solution)/shard_map/input_grad/pallas_call | solution.py:169
  202.3 2.8 %fresh_attention.1 = (bf16[4,8,256]{2,1,0:T(8,128)(2,1)}, bf16[4,8,2048]{2,1,0:T(8,128)(2,1)}) custom-call(f32[32,256]{1,0:T(8,128)} %copy-done.8, f32[32,256]{1,0:T(8,128)} %copy-done.9, f32[32,128]{1,0:T(8,128)} %get-tuple-element.21.cos_ref, f32[32,128]{1,0:T(8,128)} %get-tuple-element.22.sin_ref, bf16[4,8,2048]{2,1,0:T(8,128)(2,1)} %q_ref.1, ...), custom_call_target="tpu_custom_call" | custom-call | tf_op jit(solution)/shard_map/fresh_attention/pallas_call | solution.py:141
  205.0 0.6 copy.29
  (60 shorter events, 5.7 us)
Async XLA Ops:
  0.6 12.1 %copy-start = (bf16[384,2048]{1,0:T(8,128)(2,1)S(1)}, bf16[384,2048]{1,0:T(8,128)(2,1)}, u32[]{:S(2)}) copy-start(bf16[384,2048]{1,0:T(8,128)(2,1)} %param.10) | copy-start | bytes 4718596
  12.8 73.9 %copy-start.1 = (bf16[384,1024]{1,0:T(8,128)(2,1)}, bf16[384,1024]{1,0:T(8,128)(2,1)S(1)}, u32[]{:S(2)}) copy-start(bf16[384,1024]{1,0:T(8,128)(2,1)S(1)} %all_gather.3.m_ref) | copy-start | bytes 2359300
  13.3 10.8 %collective-permute-start.10 = (bf16[512,256]{1,0:T(8,128)(2,1)S(1)}, bf16[512,256]{1,0:T(8,128)(2,1)S(1)}, u32[]{:S(2)}, u32[]{:S(2)}) collective-permute-start(bf16[512,256]{1,0:T(8,128)(2,1)S(1)} %get-tuple-element.15), channel_id=1, source_target_pairs={{0,224},{32,0},{64,32},{96,64},{128,96},{160,128},{192,160},{224,1... | collective-permute-start | bytes 786440 | tf_op jit(solution)/shard_map/ppermute | solution.py:23
  18.6 20.2 %collective-permute-start.6 = (bf16[512,256]{1,0:T(8,128)(2,1)S(1)}, bf16[512,256]{1,0:T(8,128)(2,1)S(1)}, u32[]{:S(2)}, u32[]{:S(2)}) collective-permute-start(bf16[512,256]{1,0:T(8,128)(2,1)S(1)} %get-tuple-element.14), channel_id=1, source_target_pairs={{0,32},{32,64},{64,96},{96,128},{128,160},{160,192},{192,224},{224... | collective-permute-start | bytes 786440 | tf_op jit(solution)/shard_map/ppermute | solution.py:23
  25.4 26.2 %collective-permute-start.11 = (bf16[1024,256]{1,0:T(8,128)(2,1)}, bf16[1024,256]{1,0:T(8,128)(2,1)}, u32[]{:S(2)}, u32[]{:S(2)}) collective-permute-start(bf16[1024,256]{1,0:T(8,128)(2,1)} %add_convert_fusion.3), channel_id=1, source_target_pairs={{0,224},{32,0},{64,32},{96,64},{128,96},{160,128},{192,160},{224,1... | collective-permute-start | bytes 1572872 | tf_op jit(solution)/shard_map/ppermute | solution.py:23
  28.8 13.3 %collective-permute-start = (bf16[128,256]{1,0:T(8,128)(2,1)}, bf16[128,256]{1,0:T(8,128)(2,1)}, u32[]{:S(2)}, u32[]{:S(2)}) collective-permute-start(bf16[128,256]{1,0:T(8,128)(2,1)} %param.13), channel_id=1, source_target_pairs={{0,0},{1,64},{2,128},{3,192},{32,32},{33,96},{34,160},{35,224},{64... | collective-permute-start | bytes 196616 | tf_op jit(solution)/shard_map/ppermute | solution.py:31
  32.4 13.3 %all-to-all-start.2 = ((bf16[8,2,32,128]{3,1,2,0:T(2,128)(2,1)}), bf16[8,2,32,128]{3,1,2,0:T(2,128)(2,1)S(1)}, u32[]{:S(2)}, u32[]{:S(2)}) async-start(bf16[8,2,32,128]{3,1,2,0:T(2,128)(2,1)} %copy.20), calls=%async_computation.2 | async-start | bytes 262144 | tf_op jit(solution)/shard_map/all_to_all | solution.py:229
  40.1 15.7 %collective-permute-start.7 = (bf16[1024,256]{1,0:T(8,128)(2,1)}, bf16[1024,256]{1,0:T(8,128)(2,1)}, u32[]{:S(2)}, u32[]{:S(2)}) collective-permute-start(bf16[1024,256]{1,0:T(8,128)(2,1)} %add_convert_fusion.6), channel_id=1, source_target_pairs={{0,32},{32,64},{64,96},{96,128},{128,160},{160,192},{192,224},{224... | collective-permute-start | bytes 1572872 | tf_op jit(solution)/shard_map/ppermute | solution.py:23
  45.7 7.4 %copy-start.4 = (bf16[8,2,32,128]{3,1,2,0:T(2,128)(2,1)}, bf16[8,2,32,128]{3,1,2,0:T(2,128)(2,1)S(1)}, u32[]{:S(2)}) copy-start(bf16[8,2,32,128]{3,1,2,0:T(2,128)(2,1)S(1)} %all-to-all-done.2) | copy-start | bytes 393220
  47.5 29.2 %all-to-all-start = ((bf16[8,128,256]{2,1,0:T(8,128)(2,1)}), bf16[8,128,256]{2,1,0:T(8,128)(2,1)}, u32[]{:S(2)}, u32[]{:S(2)}) async-start(bf16[8,128,256]{2,1,0:T(8,128)(2,1)} %broadcast_in_dim.6), calls=%async_computation | async-start | bytes 1048576 | tf_op jit(solution)/shard_map/all_to_all | solution.py:237
  53.1 19.9 %collective-permute-start.12 = (bf16[1024,256]{1,0:T(8,128)(2,1)S(1)}, bf16[1024,256]{1,0:T(8,128)(2,1)S(1)}, u32[]{:S(2)}, u32[]{:S(2)}) collective-permute-start(bf16[1024,256]{1,0:T(8,128)(2,1)S(1)} %add_convert_fusion.2), channel_id=1, source_target_pairs={{0,224},{32,0},{64,32},{96,64},{128,96},{160,128},{192,160},{224,1... | collective-permute-start | bytes 1572872 | tf_op jit(solution)/shard_map/ppermute | solution.py:23
  57.7 1.0 copy-start.5
  57.7 25.5 %collective-permute-start.8 = (bf16[1024,256]{1,0:T(8,128)(2,1)}, bf16[1024,256]{1,0:T(8,128)(2,1)}, u32[]{:S(2)}, u32[]{:S(2)}) collective-permute-start(bf16[1024,256]{1,0:T(8,128)(2,1)} %add_convert_fusion.5), channel_id=1, source_target_pairs={{0,32},{32,64},{64,96},{96,128},{128,160},{160,192},{192,224},{224... | collective-permute-start | bytes 1572872 | tf_op jit(solution)/shard_map/ppermute | solution.py:23
  73.9 13.3 %collective-permute-start.13 = (bf16[1024,256]{1,0:T(8,128)(2,1)}, bf16[1024,256]{1,0:T(8,128)(2,1)}, u32[]{:S(2)}, u32[]{:S(2)}) collective-permute-start(bf16[1024,256]{1,0:T(8,128)(2,1)} %add_convert_fusion.1), channel_id=1, source_target_pairs={{0,224},{32,0},{64,32},{96,64},{128,96},{160,128},{192,160},{224,1... | collective-permute-start | bytes 1572872 | tf_op jit(solution)/shard_map/ppermute | solution.py:23
  77.6 31.6 %all-to-all-start.3 = ((bf16[8,256,128]{2,1,0:T(8,128)(2,1)}), bf16[8,256,128]{2,1,0:T(8,128)(2,1)}, u32[]{:S(2)}, u32[]{:S(2)}) async-start(bf16[8,256,128]{2,1,0:T(8,128)(2,1)} %bitcast.43), calls=%async_computation.3 | async-start | bytes 1048576 | tf_op jit(solution)/shard_map/all_to_all | solution.py:232
  85.2 22.0 %collective-permute-start.9 = (bf16[1024,256]{1,0:T(8,128)(2,1)}, bf16[1024,256]{1,0:T(8,128)(2,1)S(1)}, u32[]{:S(2)}, u32[]{:S(2)}) collective-permute-start(bf16[1024,256]{1,0:T(8,128)(2,1)} %add_convert_fusion.4), channel_id=1, source_target_pairs={{0,32},{32,64},{64,96},{96,128},{128,160},{160,192},{192,224},{224... | collective-permute-start | bytes 1572872 | tf_op jit(solution)/shard_map/ppermute | solution.py:23
  87.1 28.5 %copy-start.10 = (s32[4]{0:T(128)S(1)}, s32[4]{0:T(128)}, u32[]{:S(2)}) copy-start(s32[4]{0:T(128)} %refs_0_.1) | copy-start | bytes 52
  109.2 15.3 %all-to-all-start.1 = ((bf16[8,128,256]{2,1,0:T(8,128)(2,1)}), bf16[8,128,256]{2,1,0:T(8,128)(2,1)S(1)}, u32[]{:S(2)}, u32[]{:S(2)}) async-start(bf16[8,128,256]{2,1,0:T(8,128)(2,1)} %bitcast.9), calls=%async_computation.1 | async-start | bytes 1048576 | tf_op jit(solution)/shard_map/all_to_all | solution.py:253
  115.7 18.5 %collective-permute-start.1 = (bf16[4,2,128,256]{3,2,1,0:T(8,128)(2,1)}, bf16[4,2,128,256]{3,2,1,0:T(8,128)(2,1)S(1)}, u32[]{:S(2)}, u32[]{:S(2)}) collective-permute-start(bf16[4,2,128,256]{3,2,1,0:T(8,128)(2,1)} %bitcast.3), channel_id=1, source_target_pairs={{0,16},{16,0},{1,17},{17,1},{2,18},{18,2},{3,19},{19,3},{4,20},{20... | collective-permute-start | bytes 1572872 | tf_op jit(solution)/shard_map/ppermute | solution.py:23
  126.8 18.1 %all-to-all-start.4 = ((bf16[8,256,256]{2,1,0:T(8,128)(2,1)}), bf16[8,256,256]{2,1,0:T(8,128)(2,1)S(1)}, u32[]{:S(2)}, u32[]{:S(2)}) async-start(bf16[8,256,256]{2,1,0:T(8,128)(2,1)} %bitcast.41), calls=%async_computation.4 | async-start | bytes 2097152 | tf_op jit(solution)/shard_map/all_to_all | solution.py:261
  136.3 33.4 %collective-permute-start.4 = (bf16[2,4,2,128,256]{4,3,2,1,0:T(8,128)(2,1)}, bf16[2,4,2,128,256]{4,3,2,1,0:T(8,128)(2,1)}, u32[]{:S(2)}, u32[]{:S(2)}) collective-permute-start(bf16[2,4,2,128,256]{4,3,2,1,0:T(8,128)(2,1)} %pad_maximum_fusion.w_ref), channel_id=1, source_target_pairs={{0,4},{4,8},{8,12},{12,0},{1,5},{5,9},{9,13},{13,1},{2,6},{6,10},{... | collective-permute-start | bytes 3145736 | tf_op jit(solution)/shard_map/ppermute | solution.py:23
  137.5 33.4 %collective-permute-start.2 = (bf16[2,4,2,128,256]{4,3,2,1,0:T(8,128)(2,1)}, bf16[2,4,2,128,256]{4,3,2,1,0:T(8,128)(2,1)}, u32[]{:S(2)}, u32[]{:S(2)}) collective-permute-start(bf16[2,4,2,128,256]{4,3,2,1,0:T(8,128)(2,1)} %pad_maximum_fusion.w_ref), channel_id=1, source_target_pairs={{0,12},{4,0},{8,4},{12,8},{1,13},{5,1},{9,5},{13,9},{2,14},{6,2},{... | collective-permute-start | bytes 3145736 | tf_op jit(solution)/shard_map/ppermute | solution.py:23
  145.0 30.4 %collective-permute-start.15 = (f32[2,2,32,256]{3,2,1,0:T(8,128)S(1)}, f32[2,2,32,256]{3,2,1,0:T(8,128)}, u32[]{:S(2)}, u32[]{:S(2)}) collective-permute-start(f32[2,2,32,256]{3,2,1,0:T(8,128)S(1)} %dynamic-slice_bitcast_fusion), channel_id=1, source_target_pairs={{0,1},{1,0},{2,3},{3,2},{4,5},{5,4},{6,7},{7,6},{8,9},{9,8},{10,11... | collective-permute-start | bytes 393224 | tf_op jit(solution)/shard_map/ppermute | solution.py:23
  150.7 16.4 %collective-permute-start.14 = (bf16[128,256]{1,0:T(8,128)(2,1)S(1)}, bf16[128,256]{1,0:T(8,128)(2,1)S(1)}, u32[]{:S(2)}, u32[]{:S(2)}) collective-permute-start(bf16[128,256]{1,0:T(8,128)(2,1)S(1)} %subtract_convert_fusion), channel_id=1, source_target_pairs={{0,0},{1,64},{2,128},{3,192},{32,32},{33,96},{34,160},{35,224},{64... | collective-permute-start | bytes 196616 | tf_op jit(solution)/shard_map/ppermute | solution.py:31
  167.0 0.6 copy-start.6
  170.8 22.6 %collective-permute-start.5 = (bf16[1,4,2,128,256]{4,3,2,1,0:T(8,128)(2,1)S(1)}, bf16[1,4,2,128,256]{4,3,2,1,0:T(8,128)(2,1)S(1)}, u32[]{:S(2)}, u32[]{:S(2)}) collective-permute-start(bf16[1,4,2,128,256]{4,3,2,1,0:T(8,128)(2,1)S(1)} %slice.17), channel_id=1, source_target_pairs={{0,4},{4,8},{8,12},{12,0},{1,5},{5,9},{9,13},{13,1},{2,6},{6,10},{... | collective-permute-start | bytes 1572872 | tf_op jit(solution)/shard_map/ppermute | solution.py:23
  172.8 24.8 %collective-permute-start.3 = (bf16[1,4,2,128,256]{4,3,2,1,0:T(8,128)(2,1)}, bf16[1,4,2,128,256]{4,3,2,1,0:T(8,128)(2,1)S(1)}, u32[]{:S(2)}, u32[]{:S(2)}) collective-permute-start(bf16[1,4,2,128,256]{4,3,2,1,0:T(8,128)(2,1)} %slice.16), channel_id=1, source_target_pairs={{0,12},{4,0},{8,4},{12,8},{1,13},{5,1},{9,5},{13,9},{2,14},{6,2},{... | collective-permute-start | bytes 1572872 | tf_op jit(solution)/shard_map/ppermute | solution.py:23
  176.4 12.3 %collective-permute-start.16 = (f32[2,32,256]{2,1,0:T(8,128)S(1)}, f32[2,32,256]{2,1,0:T(8,128)S(1)}, u32[]{:S(2)}, u32[]{:S(2)}) collective-permute-start(f32[2,32,256]{2,1,0:T(8,128)S(1)} %dynamic-slice_bitcast_fusion.2), channel_id=1, source_target_pairs={{0,2},{2,0},{1,3},{3,1},{4,6},{6,4},{5,7},{7,5},{8,10},{10,8},{9,1... | collective-permute-start | bytes 196616 | tf_op jit(solution)/shard_map/ppermute | solution.py:23
  188.7 13.0 %collective-permute-start.17 = (f32[32,256]{1,0:T(8,128)S(1)}, f32[32,256]{1,0:T(8,128)S(1)}, u32[]{:S(2)}, u32[]{:S(2)}) collective-permute-start(f32[32,256]{1,0:T(8,128)S(1)} %get-tuple-element.17), channel_id=1, source_target_pairs={{0,0},{1,64},{2,128},{3,192},{32,32},{33,96},{34,160},{35,224},{64... | collective-permute-start | bytes 98312 | tf_op jit(solution)/shard_map/ppermute | solution.py:31
  192.4 9.2 %collective-permute-start.18 = (f32[32,256]{1,0:T(8,128)S(1)}, f32[32,256]{1,0:T(8,128)S(1)}, u32[]{:S(2)}, u32[]{:S(2)}) collective-permute-start(f32[32,256]{1,0:T(8,128)S(1)} %get-tuple-element.16), channel_id=1, source_target_pairs={{0,32},{1,96},{2,160},{3,224},{32,0},{33,64},{34,128},{35,192},{64... | collective-permute-start | bytes 98312 | tf_op jit(solution)/shard_map/ppermute | solution.py:31
  193.4 0.8 copy-start.2
  197.5 7.5 %copy-start.7 = (bf16[128,256]{1,0:T(8,128)(2,1)S(1)}, bf16[128,256]{1,0:T(8,128)(2,1)}, u32[]{:S(2)}) copy-start(bf16[128,256]{1,0:T(8,128)(2,1)} %copy-done.6) | copy-start | bytes 196612
  197.5 0.8 copy-start.3
  201.6 0.6 copy-start.8
  201.6 0.6 copy-start.9

commit v3 on v2

--- a/solution.py
+++ b/solution.py
@@ -40,13 +40,21 @@
     whole = term((me + last) & (size - 1)).astype(BF16)
     half = whole.shape[0] // 2
     up, down = whole[:half], whole[half:]
+
+    def low(x):
+        return jnp.pad(x, [(0, half), (0, 0)])
+
+    def high(x):
+        return jnp.pad(x, [(half, 0), (0, 0)])
+
     for hop in range(last, 0, -1):
         if hop < last:
             plus, minus = term((me + hop) & (size - 1)), term((me - hop) & (size - 1))
             up, down = up.astype(F32), down.astype(F32)
             if hop == last - 1:
-                up = jnp.pad(up, [(0, half)] + [(0, 0)] * (up.ndim - 1))
-                down = jnp.pad(down, [(half, 0)] + [(0, 0)] * (down.ndim - 1))
+                up, down = low(up), high(down)
+            else:
+                up, down = low(up[:half]) + high(up[half:]), low(down[:half]) + high(down[half:])
             up, down = (plus + up).astype(BF16), (minus + down).astype(BF16)
         up = shift(up, axis, size, 1)
         down = shift(down, axis, size, -1)
@@ -58,20 +66,22 @@
     return jnp.concatenate([wide[:, h * HD : (h + 1) * HD] for h in range(share)], axis=0)
 
 
-def cache_kernel(lengths, q_ref, k_ref, v_ref, mixed_ref, top_ref, total_ref, *, share):
+def cache_kernel(lengths, q_ref, k_ref, v_ref, mixed_ref, top_ref, total_ref, *, groups, share):
     valid = lengths[pl.program_id(0)]
-    query = stacked(q_ref[0], share).astype(BF16)
-    scores = lax.dot_general(
-        query, k_ref[0], (((1,), (1,)), ((), ())), preferred_element_type=F32
-    ) * (1.0 / math.sqrt(HD))
-    slot = lax.broadcasted_iota(jnp.int32, scores.shape, 1)
-    scores = jnp.where(slot < valid, scores, -jnp.inf)
-    top = jnp.max(scores, axis=1, keepdims=True)
-    weight = jnp.exp(scores - top)
-    total = jnp.sum(weight, axis=1, keepdims=True)
-    mixed_ref[0, 0] = jnp.dot(weight.astype(BF16), v_ref[0], preferred_element_type=F32)
-    top_ref[0, 0] = jnp.broadcast_to(top, top_ref.shape[2:])
-    total_ref[0, 0] = jnp.broadcast_to(total, total_ref.shape[2:])
+    for j in range(groups):
+        lanes = slice(j * HD, (j + 1) * HD)
+        query = stacked(q_ref[0, :, j * share * HD : (j + 1) * share * HD], share).astype(BF16)
+        scores = lax.dot_general(
+            query, k_ref[0, :, lanes], (((1,), (1,)), ((), ())), preferred_element_type=F32
+        ) * (1.0 / math.sqrt(HD))
+        slot = lax.broadcasted_iota(jnp.int32, scores.shape, 1)
+        scores = jnp.where(slot < valid, scores, -jnp.inf)
+        top = jnp.max(scores, axis=1, keepdims=True)
+        weight = jnp.exp(scores - top)
+        total = jnp.sum(weight, axis=1, keepdims=True)
+        mixed_ref[0, j] = jnp.dot(weight.astype(BF16), v_ref[0, :, lanes], preferred_element_type=F32)
+        top_ref[0, j] = jnp.broadcast_to(top, top_ref.shape[2:])
+        total_ref[0, j] = jnp.broadcast_to(total, total_ref.shape[2:])
 
 
 def attend_cache(queries, cache_keys, cache_values, lengths):
@@ -80,16 +90,16 @@
     groups = cache_keys.shape[2] // HD
     share = width // cache_keys.shape[2]
     state = jax.ShapeDtypeStruct((count, groups, share * steps, HD), F32)
-    state_spec = pl.BlockSpec((1, 1, share * steps, HD), lambda r, j, n: (r, j, 0, 0))
-    cache_spec = pl.BlockSpec((1, slots, HD), lambda r, j, n: (r, 0, j))
+    state_spec = pl.BlockSpec((1, groups, share * steps, HD), lambda r, n: (r, 0, 0, 0))
+    cache_spec = pl.BlockSpec((1, slots, groups * HD), lambda r, n: (r, 0, 0))
     return pl.pallas_call(
-        lambda *refs: cache_kernel(*refs, share=share),
+        lambda *refs: cache_kernel(*refs, groups=groups, share=share),
         out_shape=(state, state, state),
         grid_spec=pltpu.PrefetchScalarGridSpec(
             num_scalar_prefetch=1,
-            grid=(count, groups),
+            grid=(count,),
             in_specs=[
-                pl.BlockSpec((1, steps, share * HD), lambda r, j, n: (r, 0, j)),
+                pl.BlockSpec((1, steps, width), lambda r, n: (r, 0, 0)),
                 cache_spec,
                 cache_spec,
             ],
@@ -149,20 +159,13 @@
 
 
 def input_kernel(place, m_ref, w_ref, *refs):
-    out_ref = refs[-1]
-    blocks, cols = w_ref.shape[1], w_ref.shape[4]
-    total = jnp.zeros(out_ref.shape, F32)
-    for block in range(blocks):
-        total += lax.dot_general(
-            m_ref[:, block * cols : (block + 1) * cols],
-            w_ref[0, block, 0],
-            (((1,), (1,)), ((), ())),
-            preferred_element_type=F32,
-        )
-    out_ref[...] = total.astype(BF16)
-
-
-def input_grad(masked, weight, place, out, wide):
+    weight = jnp.concatenate([w_ref[0, b, 0] for b in range(w_ref.shape[1])], axis=1)
+    refs[-1][...] = lax.dot_general(
+        m_ref[...], weight, (((1,), (1,)), ((), ())), preferred_element_type=F32
+    ).astype(BF16)
+
+
+def input_grad(masked, weight, place, number, out, wide):
     pieces, blocks, two, rows, cols = weight.shape
     count = masked.shape[0]
     more = [] if out is None else [out]
@@ -178,7 +181,8 @@
             ]
             + [pl.BlockSpec(memory_space=pl.ANY) for _ in more],
             out_specs=pl.BlockSpec(
-                (count, rows), lambda q, j, n: (0, j * NX * NY + (q ^ n[0]) * NY + n[1])
+                (count, rows),
+                lambda q, j, n: (0, j * NX * NY + (q ^ n[0]) * NY + n[number]),
             ),
         ),
         input_output_aliases={3: 0} if more else {},
@@ -186,7 +190,7 @@
             flops=2 * count * weight.size, bytes_accessed=2 * weight.size, transcendentals=0
         ),
         name="input_grad",
-    )(jnp.stack(place).astype(jnp.int32), masked, weight, *more)
+    )(place, masked, weight, *more)
 
 
 def angles(lengths, steps):
@@ -240,8 +244,7 @@
     old = jnp.stack([old, other])
     up = shift(old, "y", NY, 1)
     down = shift(old, "y", NY, -1)
-    far_up = shift(up[:1], "y", NY, 1)
-    far_down = shift(down[1:], "y", NY, -1)
+    far = shift(up, "y", NY, 1)
 
     def term(k):
         left = lax.dynamic_slice_in_dim(tokens, (k & 1) * (wide // 2), wide // 2, 1)
@@ -273,15 +276,10 @@
     cosine, sine = angles(cache_lengths, steps)
     new_keys, context = attend_fresh(same, other, cosine, sine, queries, new_values, *state)
 
+    place = jnp.stack([xh, y, (y - 1) & (NY - 1), (y + 1) & (NY - 1), y ^ 2]).astype(jnp.int32)
     grad_inputs = None
-    for weight, across, owner in (
-        (old, xh, y),
-        (up, xh, (y - 1) & (NY - 1)),
-        (down, xh, (y + 1) & (NY - 1)),
-        (far_up, xh, y ^ 2),
-        (far_down, 1 - xh, y ^ 2),
-    ):
-        grad_inputs = input_grad(masked_all, weight, (across, owner), grad_inputs, wide)
+    for number, weight in enumerate((old, up, down, far)):
+        grad_inputs = input_grad(masked_all, weight, place, number + 1, grad_inputs, wide)
     return (grad_inputs, learner_weight, new_keys, context)
 
 

time: 210 us -> 216 us (1.029)
  the two profiles are of different devices: /device:TPU:1 before, /device:TPU:2 now
where the time goes in v3:
time: 216 us; the launch traced here: 215 us
  starting transfers between devices  73 us (34%)
  waiting for transfers between devices  69.9 us (32%)
  Pallas kernels  30.2 us (14%)
  matrix products  13.4 us (6%)
  local copies, waits for them, and re-layouts  10 us (5%)
  blocking collectives  9.35 us (4%)
  other arithmetic  8.15 us (4%)
    ppermute x14, waiting for transfers between devices, shift(): return lax.ppermute(x, axis, [(i, (i + step) % size) for i in range(size)])  56.7 us
    ppermute x14, starting transfers between devices, shift(): return lax.ppermute(x, axis, [(i, (i + step) % size) for i in range(size)])  23.4 us
    ppermute x4, starting transfers between devices, swap_owner(): return lax.ppermute(x, ('z', 'xl', 'c'), pairs)  23.3 us
    pallas_call x4, Pallas kernels, input_grad(): pl.pallas_call(input_kernel, out_shape=jax.ShapeDtypeStruct((count, wide)...  19.6 us
    dot_general x8, matrix products, term(): lax.dot_general(left, right, (((0,), (0,)), ((), ())), preferred_element_...  12 us
    all_gather x1, blocking collectives, update_and_decode(): masked_all = lax.all_gather(masked, TP, axis=1, tiled=True)  9.35 us
    pallas_call x1, Pallas kernels, attend_cache(): pl.pallas_call(lambda *refs: cache_kernel(*refs, groups=groups, share=sha...  7.84 us
    all_to_all x1, starting transfers between devices, update_and_decode(): part = lax.all_to_all(part, ('xh', 'y'), 0, 0, tiled=True)  6.27 us
  transfers between devices with their start and end apart: 23, of which 9 were waited for; matrix products, arithmetic and copies ran while one was open for 13% of the time, Pallas kernels for 12%

profile of v3, /device:TPU:2, one launch (start us, length us, event | category | flops | bytes accessed | tf_op | source)
XLA Modules:
  0.0 214.9 jit_solution(4539360570996419520)
XLA Ops:
  0.7 0.8 convert_element_type.89
  1.5 1.0 broadcast_multiply_fusion
  2.5 9.3 %all_gather.3.m_ref = bf16[384,1024]{1,0:T(8,128)(2,1)S(1)} all-gather(bf16[384,256]{1,0:T(8,128)(2,1)S(1)} %broadcast_multiply_fusion), channel_id=1, replica_groups=mesh['z'=8,'xh'=2,'y'=4,'xl'=2,'c'=2] {'xl','c'}, dimensions={1}, use_global_device_ids=true | all-gather | bytes 983040 | tf_op jit(solution)/shard_map/all_gather | solution.py:228
  11.9 0.5 convolution_convert_fusion.1
  12.4 0.8 collective-permute-start.5
  13.2 4.0 %collective-permute-start.9 = (bf16[512,256]{1,0:T(8,128)(2,1)S(1)}, bf16[512,256]{1,0:T(8,128)(2,1)S(1)}, u32[]{:S(2)}, u32[]{:S(2)}) collective-permute-start(bf16[512,256]{1,0:T(8,128)(2,1)S(1)} %get-tuple-element.15), channel_id=1, source_target_pairs={{0,224},{32,0},{64,32},{96,64},{128,96},{160,128},{192,160},{224,1... | collective-permute-start | bytes 786440 | tf_op jit(solution)/shard_map/ppermute | solution.py:23
  17.3 6.7 %collective-permute-done.5 = bf16[512,256]{1,0:T(8,128)(2,1)S(1)} collective-permute-done((bf16[512,256]{1,0:T(8,128)(2,1)S(1)}, bf16[512,256]{1,0:T(8,128)(2,1)S(1)}, u32[]{:S(2)}, u32[]{:S(2)}) %collective-permute-start.5) | collective-permute-done | bytes 262176 | tf_op jit(solution)/shard_map/ppermute | solution.py:23
  24.0 1.3 add_convert_fusion.6
  25.3 1.3 add_convert_fusion.3
  26.5 3.2 %collective-permute-start.10 = (bf16[1024,256]{1,0:T(8,128)(2,1)}, bf16[1024,256]{1,0:T(8,128)(2,1)S(1)}, u32[]{:S(2)}, u32[]{:S(2)}) collective-permute-start(bf16[1024,256]{1,0:T(8,128)(2,1)} %add_convert_fusion.3), channel_id=1, source_target_pairs={{0,224},{32,0},{64,32},{96,64},{128,96},{160,128},{192,160},{224,1... | collective-permute-start | bytes 1572872 | tf_op jit(solution)/shard_map/ppermute | solution.py:23
  29.8 0.9 dynamic-slice_bitcast_fusion.1
  30.7 0.8 copy.19
  31.5 6.0 %all-to-all-start.2 = ((bf16[8,2,32,128]{3,1,2,0:T(2,128)(2,1)}), bf16[8,2,32,128]{3,1,2,0:T(2,128)(2,1)S(1)}, u32[]{:S(2)}, u32[]{:S(2)}) async-start(bf16[8,2,32,128]{3,1,2,0:T(2,128)(2,1)} %copy.19), calls=%async_computation.2 | async-start | bytes 262144 | tf_op jit(solution)/shard_map/all_to_all | solution.py:233
  37.5 7.1 %collective-permute-start = (bf16[128,256]{1,0:T(8,128)(2,1)}, bf16[128,256]{1,0:T(8,128)(2,1)}, u32[]{:S(2)}, u32[]{:S(2)}) collective-permute-start(bf16[128,256]{1,0:T(8,128)(2,1)} %param.13), channel_id=1, source_target_pairs={{0,0},{1,64},{2,128},{3,192},{32,32},{33,96},{34,160},{35,224},{64... | collective-permute-start | bytes 196616 | tf_op jit(solution)/shard_map/ppermute | solution.py:31
  44.7 0.8 slice.33
  45.5 3.3 %collective-permute-done = bf16[128,256]{1,0:T(8,128)(2,1)} collective-permute-done((bf16[128,256]{1,0:T(8,128)(2,1)}, bf16[128,256]{1,0:T(8,128)(2,1)}, u32[]{:S(2)}, u32[]{:S(2)}) %collective-permute-start) | collective-permute-done | bytes 65568 | tf_op jit(solution)/shard_map/ppermute | solution.py:31
  48.8 1.7 broadcast_in_dim.6
  50.5 4.1 %all-to-all-start = ((bf16[8,128,256]{2,1,0:T(8,128)(2,1)}), bf16[8,128,256]{2,1,0:T(8,128)(2,1)}, u32[]{:S(2)}, u32[]{:S(2)}) async-start(bf16[8,128,256]{2,1,0:T(8,128)(2,1)} %broadcast_in_dim.6), calls=%async_computation | async-start | bytes 1048576 | tf_op jit(solution)/shard_map/all_to_all | solution.py:241
  54.6 2.4 %add_convert_fusion.5 = bf16[1024,256]{1,0:T(8,128)(2,1)} fusion(f32[512,256]{1,0:T(8,128)} %slice.33, bf16[384,2048]{1,0:T(8,128)(2,1)S(1)} %copy-done, s32[]{:T(128)S(6)} %select_n.76, pred[1024]{0:T(1024)(128)(4,1)S(1)} %copy-done.5, bf16[1024,256]{1,0:T(8,128)(2,1)S(1)} %collective-permute-done.6, bf16[384,1024]{1,0:T(8,128)(2,1)S(1)} %all_gather.3.m_ref, ...), kind=kOutput, calls=%fused_computation.10 | convolution fusion | flops 202637312 | bytes 2556936 | tf_op jit(solution)/shard_map/dot_general | solution.py:252
  57.0 1.9 collective-permute-start.7
  58.9 1.3 add_convert_fusion.2
  60.2 1.4 collective-permute-start.11
  61.6 16.3 %collective-permute-done.7 = bf16[1024,256]{1,0:T(8,128)(2,1)} collective-permute-done((bf16[1024,256]{1,0:T(8,128)(2,1)}, bf16[1024,256]{1,0:T(8,128)(2,1)}, u32[]{:S(2)}, u32[]{:S(2)}) %collective-permute-start.7) | collective-permute-done | bytes 524320 | tf_op jit(solution)/shard_map/ppermute | solution.py:23
  77.9 1.0 slice.34
  78.8 2.3 %add_convert_fusion.4 = bf16[1024,256]{1,0:T(8,128)(2,1)} fusion(f32[512,256]{1,0:T(8,128)S(1)} %slice.34, bf16[384,2048]{1,0:T(8,128)(2,1)S(1)} %copy-done, s32[]{:T(128)S(6)} %select_n.74, pred[1024]{0:T(1024)(128)(4,1)S(1)} %copy-done.5, bf16[1024,256]{1,0:T(8,128)(2,1)} %collective-permute-done.7, bf16[384,1024]{1,0:T(8,128)(2,1)S(1)} %all_gather.3.m_ref, ...), kind=kOutput, calls=%fused_computation.9 | convolution fusion | flops 202637312 | bytes 2556936 | tf_op jit(solution)/shard_map/dot_general | solution.py:252
  81.2 1.8 slice.37
  83.0 0.9 broadcast_in_dim.8
  83.9 6.0 %all-to-all-start.3 = ((bf16[8,256,128]{2,1,0:T(8,128)(2,1)}), bf16[8,256,128]{2,1,0:T(8,128)(2,1)S(1)}, u32[]{:S(2)}, u32[]{:S(2)}) async-start(bf16[8,256,128]{2,1,0:T(8,128)(2,1)} %bitcast.13), calls=%async_computation.3 | async-start | bytes 1048576 | tf_op jit(solution)/shard_map/all_to_all | solution.py:236
  89.8 2.5 %add_convert_fusion.1 = bf16[1024,256]{1,0:T(8,128)(2,1)} fusion(f32[512,256]{1,0:T(8,128)} %slice.37, bf16[384,2048]{1,0:T(8,128)(2,1)S(1)} %copy-done, s32[]{:T(128)S(6)} %select_n.82, pred[1024]{0:T(1024)(128)(4,1)S(1)} %copy-done.5, bf16[1024,256]{1,0:T(8,128)(2,1)} %collective-permute-done.11, bf16[384,1024]{1,0:T(8,128)(2,1)S(1)} %all_gather.3.m_ref, ...), kind=kOutput, calls=%fused_computation.6 | convolution fusion | flops 202637312 | bytes 2556936 | tf_op jit(solution)/shard_map/dot_general | solution.py:252
  92.3 3.2 %collective-permute-start.12 = (bf16[1024,256]{1,0:T(8,128)(2,1)}, bf16[1024,256]{1,0:T(8,128)(2,1)}, u32[]{:S(2)}, u32[]{:S(2)}) collective-permute-start(bf16[1024,256]{1,0:T(8,128)(2,1)} %add_convert_fusion.1), channel_id=1, source_target_pairs={{0,224},{32,0},{64,32},{96,64},{128,96},{160,128},{192,160},{224,1... | collective-permute-start | bytes 1572872 | tf_op jit(solution)/shard_map/ppermute | solution.py:23
  95.6 0.5 fusion.21
  96.0 3.3 %collective-permute-start.1 = (bf16[4,2,128,256]{3,2,1,0:T(8,128)(2,1)}, bf16[4,2,128,256]{3,2,1,0:T(8,128)(2,1)}, u32[]{:S(2)}, u32[]{:S(2)}) collective-permute-start(bf16[4,2,128,256]{3,2,1,0:T(8,128)(2,1)} %bitcast.6), channel_id=1, source_target_pairs={{0,16},{16,0},{1,17},{17,1},{2,18},{18,2},{3,19},{19,3},{4,20},{20... | collective-permute-start | bytes 1572872 | tf_op jit(solution)/shard_map/ppermute | solution.py:23
  99.4 0.9 collective-permute-done.8
  100.2 12.4 %collective-permute-done.12 = bf16[1024,256]{1,0:T(8,128)(2,1)} collective-permute-done((bf16[1024,256]{1,0:T(8,128)(2,1)}, bf16[1024,256]{1,0:T(8,128)(2,1)}, u32[]{:S(2)}, u32[]{:S(2)}) %collective-permute-start.12) | collective-permute-done | bytes 524320 | tf_op jit(solution)/shard_map/ppermute | solution.py:23
  112.6 2.0 add_convert_fusion
  114.6 6.3 %all-to-all-start.1 = ((bf16[8,128,256]{2,1,0:T(8,128)(2,1)}), bf16[8,128,256]{2,1,0:T(8,128)(2,1)S(1)}, u32[]{:S(2)}, u32[]{:S(2)}) async-start(bf16[8,128,256]{2,1,0:T(8,128)(2,1)} %bitcast.8), calls=%async_computation.1 | async-start | bytes 1048576 | tf_op jit(solution)/shard_map/all_to_all | solution.py:256
  121.0 2.3 %pad_maximum_fusion.w_ref = bf16[2,4,2,128,256]{4,3,2,1,0:T(8,128)(2,1)} fusion(bf16[1,4,2,128,256]{4,3,2,1,0:T(8,128)(2,1)} %bitcast.7, bf16[1,4,2,128,256]{4,3,2,1,0:T(8,128)(2,1)} %bitcast.5), kind=kLoop, calls=%fused_computation.3 | loop fusion | flops 524288 | bytes 2097152 | tf_op jit(solution)/shard_map/stack | solution.py:244
  123.3 2.0 collective-permute-start.2
  125.3 5.5 %all-to-all-done.1 = bf16[8,128,256]{2,1,0:T(8,128)(2,1)S(1)} async-done(((bf16[8,128,256]{2,1,0:T(8,128)(2,1)}), bf16[8,128,256]{2,1,0:T(8,128)(2,1)S(1)}, u32[]{:S(2)}, u32[]{:S(2)}) %all-to-all-start.1) | async-done | bytes 524320 | tf_op jit(solution)/shard_map/all_to_all | solution.py:256
  130.9 0.9 subtract_convert_fusion
  131.7 1.4 convolution_convert_fusion
  133.1 3.8 %all-to-all-start.4 = ((bf16[8,256,256]{2,1,0:T(8,128)(2,1)}), bf16[8,256,256]{2,1,0:T(8,128)(2,1)S(1)}, u32[]{:S(2)}, u32[]{:S(2)}) async-start(bf16[8,256,256]{2,1,0:T(8,128)(2,1)} %bitcast.40), calls=%async_computation.4 | async-start | bytes 2097152 | tf_op jit(solution)/shard_map/all_to_all | solution.py:264
  137.0 0.1 convert_element_type.111
  137.1 0.1 fusion.47
  137.3 3.3 %collective-permute-start.4 = (bf16[2,4,2,128,256]{4,3,2,1,0:T(8,128)(2,1)}, bf16[2,4,2,128,256]{4,3,2,1,0:T(8,128)(2,1)}, u32[]{:S(2)}, u32[]{:S(2)}) collective-permute-start(bf16[2,4,2,128,256]{4,3,2,1,0:T(8,128)(2,1)} %pad_maximum_fusion.w_ref), channel_id=1, source_target_pairs={{0,12},{4,0},{8,4},{12,8},{1,13},{5,1},{9,5},{13,9},{2,14},{6,2},{... | collective-permute-start | bytes 3145736 | tf_op jit(solution)/shard_map/ppermute | solution.py:23
  140.6 20.5 %collective-permute-done.2.w_ref = bf16[2,4,2,128,256]{4,3,2,1,0:T(8,128)(2,1)} collective-permute-done((bf16[2,4,2,128,256]{4,3,2,1,0:T(8,128)(2,1)}, bf16[2,4,2,128,256]{4,3,2,1,0:T(8,128)(2,1)}, u32[]{:S(2)}, u32[]{:S(2)}) %collective-permute-start.2) | collective-permute-done | bytes 1048608 | tf_op jit(solution)/shard_map/ppermute | solution.py:23
  161.1 3.4 %all-to-all-done.4 = bf16[8,256,256]{2,1,0:T(8,128)(2,1)S(1)} async-done(((bf16[8,256,256]{2,1,0:T(8,128)(2,1)}), bf16[8,256,256]{2,1,0:T(8,128)(2,1)S(1)}, u32[]{:S(2)}, u32[]{:S(2)}) %all-to-all-start.4) | async-done | bytes 1048608 | tf_op jit(solution)/shard_map/all_to_all | solution.py:264
  164.4 0.1 convert_reduce_fusion
  164.6 0.1 collective-permute-start.14
  164.7 7.8 %cache_attention.1 = (f32[4,2,64,128]{3,2,1,0:T(8,128)}, f32[4,2,64,128]{3,2,1,0:T(8,128)}, f32[4,2,64,128]{3,2,1,0:T(8,128)}) custom-call(s32[4]{0:T(128)} %refs_0_.1, bf16[4,8,2048]{2,1,0:T(8,128)(2,1)} %q_ref.1, bf16[4,2048,256]{2,1,0:T(8,128)(2,1)} %refs_2_.1, bf16[4,2048,256]{2,1,0:T(8,128)(2,1)} %refs_3_.1), custom_call_target="tpu_custom_call" | custom-call | flops 536870912 | bytes 8388608 | tf_op jit(solution)/shard_map/cache_attention/pallas_call | solution.py:95
  172.5 0.7 stack.29.place
  173.2 0.7 pad_maximum_fusion.1
  173.9 8.3 %collective-permute-start.13 = (bf16[128,256]{1,0:T(8,128)(2,1)S(1)}, bf16[128,256]{1,0:T(8,128)(2,1)S(1)}, u32[]{:S(2)}, u32[]{:S(2)}) collective-permute-start(bf16[128,256]{1,0:T(8,128)(2,1)S(1)} %subtract_convert_fusion), channel_id=1, source_target_pairs={{0,0},{1,64},{2,128},{3,192},{32,32},{33,96},{34,160},{35,224},{64... | collective-permute-start | bytes 196616 | tf_op jit(solution)/shard_map/ppermute | solution.py:31
  182.3 0.1 collective-permute-start.15
  182.4 4.9 %input_grad.4.refs_0_ = bf16[384,2048]{1,0:T(8,128)(2,1)} custom-call(s32[5]{0:T(128)} %stack.29.place, bf16[384,1024]{1,0:T(8,128)(2,1)} %copy-done.1, bf16[2,4,2,128,256]{4,3,2,1,0:T(8,128)(2,1)} %pad_maximum_fusion.w_ref), custom_call_target="tpu_custom_call" | custom-call | flops 402653184 | bytes 1048576 | tf_op jit(solution)/shard_map/input_grad/pallas_call | solution.py:172
  187.3 4.9 %input_grad.5.refs_0_ = bf16[384,2048]{1,0:T(8,128)(2,1)} custom-call(s32[5]{0:T(128)} %stack.29.place, bf16[384,1024]{1,0:T(8,128)(2,1)} %copy-done.1, bf16[2,4,2,128,256]{4,3,2,1,0:T(8,128)(2,1)} %collective-permute-done.2.w_ref, bf16[384,2048]{1,0:T(8,128)(2,1)} %input_grad.4.refs_0_), custom_call_target="tpu_custom_call", output_to_operand_aliasing={{}: (3, {})} | custom-call | flops 402653184 | bytes 1048576 | tf_op jit(solution)/shard_map/input_grad/pallas_call | solution.py:172
  192.2 5.9 %collective-permute-start.16 = (f32[32,256]{1,0:T(8,128)S(1)}, f32[32,256]{1,0:T(8,128)S(1)}, u32[]{:S(2)}, u32[]{:S(2)}) collective-permute-start(f32[32,256]{1,0:T(8,128)S(1)} %get-tuple-element.17), channel_id=1, source_target_pairs={{0,0},{1,64},{2,128},{3,192},{32,32},{33,96},{34,160},{35,224},{64... | collective-permute-start | bytes 98312 | tf_op jit(solution)/shard_map/ppermute | solution.py:31
  198.1 2.0 collective-permute-start.17
  200.1 4.9 %input_grad.6.refs_0_ = bf16[384,2048]{1,0:T(8,128)(2,1)} custom-call(s32[5]{0:T(128)} %stack.29.place, bf16[384,1024]{1,0:T(8,128)(2,1)} %copy-done.1, bf16[2,4,2,128,256]{4,3,2,1,0:T(8,128)(2,1)} %collective-permute-done.4.w_ref, bf16[384,2048]{1,0:T(8,128)(2,1)} %input_grad.5.refs_0_), custom_call_target="tpu_custom_call", output_to_operand_aliasing={{}: (3, {})} | custom-call | flops 402653184 | bytes 1048576 | tf_op jit(solution)/shard_map/input_grad/pallas_call | solution.py:172
  205.0 1.0 collective-permute-done.17.other_ref
  206.0 0.6 copy-done.3
  206.6 2.8 %fresh_attention.1 = (bf16[4,8,256]{2,1,0:T(8,128)(2,1)}, bf16[4,8,2048]{2,1,0:T(8,128)(2,1)}) custom-call(f32[32,256]{1,0:T(8,128)} %copy-done.2, f32[32,256]{1,0:T(8,128)} %copy-done.3, f32[32,128]{1,0:T(8,128)} %get-tuple-element.21.cos_ref, f32[32,128]{1,0:T(8,128)} %get-tuple-element.22.sin_ref, bf16[4,8,2048]{2,1,0:T(8,128)(2,1)} %q_ref.1, ...), custom_call_target="tpu_custom_call" | custom-call | tf_op jit(solution)/shard_map/fresh_attention/pallas_call | solution.py:151
  209.4 4.9 %input_grad.7 = bf16[384,2048]{1,0:T(8,128)(2,1)} custom-call(s32[5]{0:T(128)} %stack.29.place, bf16[384,1024]{1,0:T(8,128)(2,1)} %copy-done.1, bf16[2,4,2,128,256]{4,3,2,1,0:T(8,128)(2,1)} %collective-permute-done.3.w_ref, bf16[384,2048]{1,0:T(8,128)(2,1)} %input_grad.6.refs_0_), custom_call_target="tpu_custom_call", output_to_operand_aliasing={{}: (3, {})} | custom-call | flops 402653184 | bytes 1048576 | tf_op jit(solution)/shard_map/input_grad/pallas_call | solution.py:172
  214.3 0.6 copy.27
  (41 shorter events, 0.5 us)
Async XLA Ops:
  0.6 11.2 %copy-start = (bf16[384,2048]{1,0:T(8,128)(2,1)S(1)}, bf16[384,2048]{1,0:T(8,128)(2,1)}, u32[]{:S(2)}) copy-start(bf16[384,2048]{1,0:T(8,128)(2,1)} %param.10) | copy-start | bytes 4718596
  11.9 83.7 %copy-start.1 = (bf16[384,1024]{1,0:T(8,128)(2,1)}, bf16[384,1024]{1,0:T(8,128)(2,1)S(1)}, u32[]{:S(2)}) copy-start(bf16[384,1024]{1,0:T(8,128)(2,1)S(1)} %all_gather.3.m_ref) | copy-start | bytes 2359300
  12.4 11.6 %collective-permute-start.5 = (bf16[512,256]{1,0:T(8,128)(2,1)S(1)}, bf16[512,256]{1,0:T(8,128)(2,1)S(1)}, u32[]{:S(2)}, u32[]{:S(2)}) collective-permute-start(bf16[512,256]{1,0:T(8,128)(2,1)S(1)} %get-tuple-element.14), channel_id=1, source_target_pairs={{0,32},{32,64},{64,96},{96,128},{128,160},{160,192},{192,224},{224... | collective-permute-start | bytes 786440 | tf_op jit(solution)/shard_map/ppermute | solution.py:23
  13.2 12.1 %collective-permute-start.9 = (bf16[512,256]{1,0:T(8,128)(2,1)S(1)}, bf16[512,256]{1,0:T(8,128)(2,1)S(1)}, u32[]{:S(2)}, u32[]{:S(2)}) collective-permute-start(bf16[512,256]{1,0:T(8,128)(2,1)S(1)} %get-tuple-element.15), channel_id=1, source_target_pairs={{0,224},{32,0},{64,32},{96,64},{128,96},{160,128},{192,160},{224,1... | collective-permute-start | bytes 786440 | tf_op jit(solution)/shard_map/ppermute | solution.py:23
  25.3 19.4 %collective-permute-start.6 = (bf16[1024,256]{1,0:T(8,128)(2,1)}, bf16[1024,256]{1,0:T(8,128)(2,1)S(1)}, u32[]{:S(2)}, u32[]{:S(2)}) collective-permute-start(bf16[1024,256]{1,0:T(8,128)(2,1)} %add_convert_fusion.6), channel_id=1, source_target_pairs={{0,32},{32,64},{64,96},{96,128},{128,160},{160,192},{192,224},{224... | collective-permute-start | bytes 1572872 | tf_op jit(solution)/shard_map/ppermute | solution.py:23
  26.5 32.3 %collective-permute-start.10 = (bf16[1024,256]{1,0:T(8,128)(2,1)}, bf16[1024,256]{1,0:T(8,128)(2,1)S(1)}, u32[]{:S(2)}, u32[]{:S(2)}) collective-permute-start(bf16[1024,256]{1,0:T(8,128)(2,1)} %add_convert_fusion.3), channel_id=1, source_target_pairs={{0,224},{32,0},{64,32},{96,64},{128,96},{160,128},{192,160},{224,1... | collective-permute-start | bytes 1572872 | tf_op jit(solution)/shard_map/ppermute | solution.py:23
  30.7 23.9 %copy-start.5 = (pred[1024]{0:T(1024)(128)(4,1)S(1)}, pred[1024]{0:T(1024)(128)(4,1)}, u32[]{:S(2)}) copy-start(pred[1024]{0:T(1024)(128)(4,1)} %constant.75.clone.1) | copy-start | bytes 3076
  31.5 17.3 %all-to-all-start.2 = ((bf16[8,2,32,128]{3,1,2,0:T(2,128)(2,1)}), bf16[8,2,32,128]{3,1,2,0:T(2,128)(2,1)S(1)}, u32[]{:S(2)}, u32[]{:S(2)}) async-start(bf16[8,2,32,128]{3,1,2,0:T(2,128)(2,1)} %copy.19), calls=%async_computation.2 | async-start | bytes 262144 | tf_op jit(solution)/shard_map/all_to_all | solution.py:233
  37.5 11.3 %collective-permute-start = (bf16[128,256]{1,0:T(8,128)(2,1)}, bf16[128,256]{1,0:T(8,128)(2,1)}, u32[]{:S(2)}, u32[]{:S(2)}) collective-permute-start(bf16[128,256]{1,0:T(8,128)(2,1)} %param.13), channel_id=1, source_target_pairs={{0,0},{1,64},{2,128},{3,192},{32,32},{33,96},{34,160},{35,224},{64... | collective-permute-start | bytes 196616 | tf_op jit(solution)/shard_map/ppermute | solution.py:31
  50.5 32.5 %all-to-all-start = ((bf16[8,128,256]{2,1,0:T(8,128)(2,1)}), bf16[8,128,256]{2,1,0:T(8,128)(2,1)}, u32[]{:S(2)}, u32[]{:S(2)}) async-start(bf16[8,128,256]{2,1,0:T(8,128)(2,1)} %broadcast_in_dim.6), calls=%async_computation | async-start | bytes 1048576 | tf_op jit(solution)/shard_map/all_to_all | solution.py:241
  57.0 20.9 %collective-permute-start.7 = (bf16[1024,256]{1,0:T(8,128)(2,1)}, bf16[1024,256]{1,0:T(8,128)(2,1)}, u32[]{:S(2)}, u32[]{:S(2)}) collective-permute-start(bf16[1024,256]{1,0:T(8,128)(2,1)} %add_convert_fusion.5), channel_id=1, source_target_pairs={{0,32},{32,64},{64,96},{96,128},{128,160},{160,192},{192,224},{224... | collective-permute-start | bytes 1572872 | tf_op jit(solution)/shard_map/ppermute | solution.py:23
  60.2 21.0 %collective-permute-start.11 = (bf16[1024,256]{1,0:T(8,128)(2,1)}, bf16[1024,256]{1,0:T(8,128)(2,1)}, u32[]{:S(2)}, u32[]{:S(2)}) collective-permute-start(bf16[1024,256]{1,0:T(8,128)(2,1)} %add_convert_fusion.2), channel_id=1, source_target_pairs={{0,224},{32,0},{64,32},{96,64},{128,96},{160,128},{192,160},{224,1... | collective-permute-start | bytes 1572872 | tf_op jit(solution)/shard_map/ppermute | solution.py:23
  81.2 19.0 %collective-permute-start.8 = (bf16[1024,256]{1,0:T(8,128)(2,1)}, bf16[1024,256]{1,0:T(8,128)(2,1)S(1)}, u32[]{:S(2)}, u32[]{:S(2)}) collective-permute-start(bf16[1024,256]{1,0:T(8,128)(2,1)} %add_convert_fusion.4), channel_id=1, source_target_pairs={{0,32},{32,64},{64,96},{96,128},{128,160},{160,192},{192,224},{224... | collective-permute-start | bytes 1572872 | tf_op jit(solution)/shard_map/ppermute | solution.py:23
  83.9 30.8 %all-to-all-start.3 = ((bf16[8,256,128]{2,1,0:T(8,128)(2,1)}), bf16[8,256,128]{2,1,0:T(8,128)(2,1)S(1)}, u32[]{:S(2)}, u32[]{:S(2)}) async-start(bf16[8,256,128]{2,1,0:T(8,128)(2,1)} %bitcast.13), calls=%async_computation.3 | async-start | bytes 1048576 | tf_op jit(solution)/shard_map/all_to_all | solution.py:236
  92.3 20.3 %collective-permute-start.12 = (bf16[1024,256]{1,0:T(8,128)(2,1)}, bf16[1024,256]{1,0:T(8,128)(2,1)}, u32[]{:S(2)}, u32[]{:S(2)}) collective-permute-start(bf16[1024,256]{1,0:T(8,128)(2,1)} %add_convert_fusion.1), channel_id=1, source_target_pairs={{0,224},{32,0},{64,32},{96,64},{128,96},{160,128},{192,160},{224,1... | collective-permute-start | bytes 1572872 | tf_op jit(solution)/shard_map/ppermute | solution.py:23
  96.0 24.9 %collective-permute-start.1 = (bf16[4,2,128,256]{3,2,1,0:T(8,128)(2,1)}, bf16[4,2,128,256]{3,2,1,0:T(8,128)(2,1)}, u32[]{:S(2)}, u32[]{:S(2)}) collective-permute-start(bf16[4,2,128,256]{3,2,1,0:T(8,128)(2,1)} %bitcast.6), channel_id=1, source_target_pairs={{0,16},{16,0},{1,17},{17,1},{2,18},{18,2},{3,19},{19,3},{4,20},{20... | collective-permute-start | bytes 1572872 | tf_op jit(solution)/shard_map/ppermute | solution.py:23
  114.6 16.2 %all-to-all-start.1 = ((bf16[8,128,256]{2,1,0:T(8,128)(2,1)}), bf16[8,128,256]{2,1,0:T(8,128)(2,1)S(1)}, u32[]{:S(2)}, u32[]{:S(2)}) async-start(bf16[8,128,256]{2,1,0:T(8,128)(2,1)} %bitcast.8), calls=%async_computation.1 | async-start | bytes 1048576 | tf_op jit(solution)/shard_map/all_to_all | solution.py:256
  123.3 37.8 %collective-permute-start.2 = (bf16[2,4,2,128,256]{4,3,2,1,0:T(8,128)(2,1)}, bf16[2,4,2,128,256]{4,3,2,1,0:T(8,128)(2,1)}, u32[]{:S(2)}, u32[]{:S(2)}) collective-permute-start(bf16[2,4,2,128,256]{4,3,2,1,0:T(8,128)(2,1)} %pad_maximum_fusion.w_ref), channel_id=1, source_target_pairs={{0,4},{4,8},{8,12},{12,0},{1,5},{5,9},{9,13},{13,1},{2,6},{6,10},{... | collective-permute-start | bytes 3145736 | tf_op jit(solution)/shard_map/ppermute | solution.py:23
  131.7 5.2 %copy-start.4 = (s32[4]{0:T(128)S(1)}, s32[4]{0:T(128)}, u32[]{:S(2)}) copy-start(s32[4]{0:T(128)} %refs_0_.1) | copy-start | bytes 52
  133.1 31.3 %all-to-all-start.4 = ((bf16[8,256,256]{2,1,0:T(8,128)(2,1)}), bf16[8,256,256]{2,1,0:T(8,128)(2,1)S(1)}, u32[]{:S(2)}, u32[]{:S(2)}) async-start(bf16[8,256,256]{2,1,0:T(8,128)(2,1)} %bitcast.40), calls=%async_computation.4 | async-start | bytes 2097152 | tf_op jit(solution)/shard_map/all_to_all | solution.py:264
  137.3 62.8 %collective-permute-start.4 = (bf16[2,4,2,128,256]{4,3,2,1,0:T(8,128)(2,1)}, bf16[2,4,2,128,256]{4,3,2,1,0:T(8,128)(2,1)}, u32[]{:S(2)}, u32[]{:S(2)}) collective-permute-start(bf16[2,4,2,128,256]{4,3,2,1,0:T(8,128)(2,1)} %pad_maximum_fusion.w_ref), channel_id=1, source_target_pairs={{0,12},{4,0},{8,4},{12,8},{1,13},{5,1},{9,5},{13,9},{2,14},{6,2},{... | collective-permute-start | bytes 3145736 | tf_op jit(solution)/shard_map/ppermute | solution.py:23
  161.1 48.3 %collective-permute-start.3 = (bf16[2,4,2,128,256]{4,3,2,1,0:T(8,128)(2,1)}, bf16[2,4,2,128,256]{4,3,2,1,0:T(8,128)(2,1)}, u32[]{:S(2)}, u32[]{:S(2)}) collective-permute-start(bf16[2,4,2,128,256]{4,3,2,1,0:T(8,128)(2,1)} %collective-permute-done.2.w_ref), channel_id=1, source_target_pairs={{0,4},{4,8},{8,12},{12,0},{1,5},{5,9},{9,13},{13,1},{2,6},{6,10},{... | collective-permute-start | bytes 3145736 | tf_op jit(solution)/shard_map/ppermute | solution.py:23
  164.6 17.6 %collective-permute-start.14 = (f32[2,2,32,256]{3,2,1,0:T(8,128)S(1)}, f32[2,2,32,256]{3,2,1,0:T(8,128)S(1)}, u32[]{:S(2)}, u32[]{:S(2)}) collective-permute-start(f32[2,2,32,256]{3,2,1,0:T(8,128)S(1)} %dynamic-slice_bitcast_fusion), channel_id=1, source_target_pairs={{0,1},{1,0},{2,3},{3,2},{4,5},{5,4},{6,7},{7,6},{8,9},{9,8},{10,11... | collective-permute-start | bytes 393224 | tf_op jit(solution)/shard_map/ppermute | solution.py:23
  173.9 13.4 %collective-permute-start.13 = (bf16[128,256]{1,0:T(8,128)(2,1)S(1)}, bf16[128,256]{1,0:T(8,128)(2,1)S(1)}, u32[]{:S(2)}, u32[]{:S(2)}) collective-permute-start(bf16[128,256]{1,0:T(8,128)(2,1)S(1)} %subtract_convert_fusion), channel_id=1, source_target_pairs={{0,0},{1,64},{2,128},{3,192},{32,32},{33,96},{34,160},{35,224},{64... | collective-permute-start | bytes 196616 | tf_op jit(solution)/shard_map/ppermute | solution.py:31
  182.3 9.9 %collective-permute-start.15 = (f32[2,32,256]{2,1,0:T(8,128)S(1)}, f32[2,32,256]{2,1,0:T(8,128)S(1)}, u32[]{:S(2)}, u32[]{:S(2)}) collective-permute-start(f32[2,32,256]{2,1,0:T(8,128)S(1)} %dynamic-slice_bitcast_fusion.2), channel_id=1, source_target_pairs={{0,2},{2,0},{1,3},{3,1},{4,6},{6,4},{5,7},{7,5},{8,10},{10,8},{9,1... | collective-permute-start | bytes 196616 | tf_op jit(solution)/shard_map/ppermute | solution.py:23
  192.2 12.8 %collective-permute-start.16 = (f32[32,256]{1,0:T(8,128)S(1)}, f32[32,256]{1,0:T(8,128)S(1)}, u32[]{:S(2)}, u32[]{:S(2)}) collective-permute-start(f32[32,256]{1,0:T(8,128)S(1)} %get-tuple-element.17), channel_id=1, source_target_pairs={{0,0},{1,64},{2,128},{3,192},{32,32},{33,96},{34,160},{35,224},{64... | collective-permute-start | bytes 98312 | tf_op jit(solution)/shard_map/ppermute | solution.py:31
  198.1 7.9 %collective-permute-start.17 = (f32[32,256]{1,0:T(8,128)S(1)}, f32[32,256]{1,0:T(8,128)S(1)}, u32[]{:S(2)}, u32[]{:S(2)}) collective-permute-start(f32[32,256]{1,0:T(8,128)S(1)} %get-tuple-element.16), channel_id=1, source_target_pairs={{0,32},{1,96},{2,160},{3,224},{32,0},{33,64},{34,128},{35,192},{64... | collective-permute-start | bytes 98312 | tf_op jit(solution)/shard_map/ppermute | solution.py:31
  205.0 1.0 copy-start.2
  206.0 0.6 copy-start.3

commit v4 on v3

--- a/solution.py
+++ b/solution.py
@@ -11,7 +11,8 @@
 D = 8192
 HD = 128
 NZ, NX, NY, NL, NC = 8, 2, 4, 2, 2
-FSDP = ("z", "xh", "y")
+FSDP = ("zh", "zl", "xh", "y")
+Z = ("zh", "zl")
 TP = ("xl", "c")
 F32 = jnp.float32
 BF16 = jnp.bfloat16
@@ -23,16 +24,12 @@
     return lax.ppermute(x, axis, [(i, (i + step) % size) for i in range(size)])
 
 
-def swap_owner(x, flip=0):
+def swap_owner(x):
     pairs = []
     for z in range(NZ):
         for t in range(NL * NC):
-            pairs.append((z * 4 + t, (2 * t + (z % 2 ^ flip)) * 4 + z // 2))
-    return lax.ppermute(x, ("z", "xl", "c"), pairs)
-
-
-def pick(x, index, axis):
-    return lax.dynamic_index_in_dim(x, index, axis, keepdims=False)
+            pairs.append((z * 4 + t, (2 * t + z % 2) * 4 + z // 2))
+    return lax.ppermute(x, Z + TP, pairs)
 
 
 def ring_sum(term, axis, size, me):
@@ -53,8 +50,6 @@
             up, down = up.astype(F32), down.astype(F32)
             if hop == last - 1:
                 up, down = low(up), high(down)
-            else:
-                up, down = low(up[:half]) + high(up[half:]), low(down[:half]) + high(down[half:])
             up, down = (plus + up).astype(BF16), (minus + down).astype(BF16)
         up = shift(up, axis, size, 1)
         down = shift(down, axis, size, -1)
@@ -115,7 +110,7 @@
 
 
 def fresh_kernel(
-    same_ref, other_ref, cos_ref, sin_ref, q_ref, v_ref, mixed_ref, top_ref, total_ref, keys_ref, out_ref
+    raw_ref, cos_ref, sin_ref, q_ref, v_ref, mixed_ref, top_ref, total_ref, keys_ref, out_ref
 ):
     count, steps, width = q_ref.shape
     groups = v_ref.shape[2] // HD
@@ -125,7 +120,7 @@
         for j in range(groups):
             lanes = slice(j * HD, (j + 1) * HD)
             heads = slice(j * share * HD, (j + 1) * share * HD)
-            raw = same_ref[lines, lanes] + other_ref[lines, lanes]
+            raw = raw_ref[lines, lanes]
             keys = raw * cos_ref[lines, :] + pltpu.roll(raw, HD // 2, 1) * sin_ref[lines, :]
             keys = keys.astype(BF16)
             keys_ref[r, :, lanes] = keys
@@ -147,7 +142,7 @@
             out_ref[r, :, heads] = jnp.concatenate(flat, axis=1).astype(BF16)
 
 
-def attend_fresh(same, other, cosine, sine, queries, new_values, mixed, top, total):
+def attend_fresh(raw, cosine, sine, queries, new_values, mixed, top, total):
     return pl.pallas_call(
         fresh_kernel,
         out_shape=(
@@ -155,36 +150,51 @@
             jax.ShapeDtypeStruct(queries.shape, BF16),
         ),
         name="fresh_attention",
-    )(same, other, cosine, sine, queries, new_values, mixed, top, total)
-
-
-def input_kernel(place, m_ref, w_ref, *refs):
-    weight = jnp.concatenate([w_ref[0, b, 0] for b in range(w_ref.shape[1])], axis=1)
-    refs[-1][...] = lax.dot_general(
-        m_ref[...], weight, (((1,), (1,)), ((), ())), preferred_element_type=F32
-    ).astype(BF16)
+    )(raw, cosine, sine, queries, new_values, mixed, top, total)
+
+
+def input_kernel(place, m_ref, w_ref, *refs, number):
+    out_ref, stage, sems = refs[-3:]
+    pieces, blocks, two, rows, cols = w_ref.shape
+    copies = []
+    for q in range(pieces):
+        weight = jnp.concatenate(
+            [w_ref[q, b].reshape(two * rows, cols) for b in range(blocks)], axis=1
+        )
+        product = lax.dot_general(
+            m_ref[...], weight, (((1,), (1,)), ((), ())), preferred_element_type=F32
+        ).astype(BF16)
+        for j in range(two):
+            slot = q * two + j
+            stage[slot] = product[:, j * rows : (j + 1) * rows]
+            column = (j * NX * NY + (q ^ place[0]) * NY + place[number]) * rows
+            copy = pltpu.make_async_copy(
+                stage.at[slot], out_ref.at[:, pl.ds(pl.multiple_of(column, rows), rows)], sems.at[slot]
+            )
+            copy.start()
+            copies.append(copy)
+    for copy in copies:
+        copy.wait()
 
 
 def input_grad(masked, weight, place, number, out, wide):
-    pieces, blocks, two, rows, cols = weight.shape
+    pieces, _, two, rows, _ = weight.shape
     count = masked.shape[0]
     more = [] if out is None else [out]
     return pl.pallas_call(
-        input_kernel,
+        lambda *refs: input_kernel(*refs, number=number),
         out_shape=jax.ShapeDtypeStruct((count, wide), BF16),
-        grid_spec=pltpu.PrefetchScalarGridSpec(
-            num_scalar_prefetch=1,
-            grid=(pieces, two),
-            in_specs=[
-                pl.BlockSpec((count, blocks * cols), lambda q, j, n: (0, 0)),
-                pl.BlockSpec((1, blocks, 1, rows, cols), lambda q, j, n: (q, 0, j, 0, 0)),
-            ]
-            + [pl.BlockSpec(memory_space=pl.ANY) for _ in more],
-            out_specs=pl.BlockSpec(
-                (count, rows),
-                lambda q, j, n: (0, j * NX * NY + (q ^ n[0]) * NY + n[number]),
-            ),
-        ),
+        in_specs=[
+            pl.BlockSpec(memory_space=pltpu.SMEM),
+            pl.BlockSpec(memory_space=pltpu.VMEM),
+            pl.BlockSpec(memory_space=pltpu.VMEM),
+        ]
+        + [pl.BlockSpec(memory_space=pl.ANY) for _ in more],
+        out_specs=pl.BlockSpec(memory_space=pl.ANY),
+        scratch_shapes=[
+            pltpu.VMEM((pieces * two, count, rows), BF16),
+            pltpu.SemaphoreType.DMA((pieces * two,)),
+        ],
         input_output_aliases={3: 0} if more else {},
         cost_estimate=pl.CostEstimate(
             flops=2 * count * weight.size, bytes_accessed=2 * weight.size, transcendentals=0
@@ -214,10 +224,8 @@
     cache_values,
     cache_lengths,
 ):
-    z, xh, y = lax.axis_index("z"), lax.axis_index("xh"), lax.axis_index("y")
-    xl, c = lax.axis_index("xl"), lax.axis_index("c")
-    tp = xl * NC + c
-    odd = z & 1
+    z, xh, y = lax.axis_index(Z), lax.axis_index("xh"), lax.axis_index("y")
+    tp = lax.axis_index(TP)
     wide = tokens.shape[1]
     cols = cotangent.shape[1]
     rows = key_weight.shape[0]
@@ -233,12 +241,12 @@
     hidden = lax.all_to_all(hidden, ("xh", "y"), 0, 0, tiled=True)
     hidden = hidden.transpose(1, 0, 2, 3).reshape(1, 2, NX * NY * lines, rows)
     hidden = jnp.broadcast_to(hidden, (NZ // 2,) + hidden.shape[1:]).reshape(NZ, NX * NY * lines, rows)
-    hidden = lax.all_to_all(hidden, "z", 0, 0, tiled=True)
+    hidden = lax.all_to_all(hidden, Z, 0, 0, tiled=True)
     hidden = hidden.reshape(NZ, NX * NY, lines, rows).transpose(1, 0, 2, 3).reshape(-1, rows)
 
     own_weight = swap_owner(key_weight)
     old = jnp.broadcast_to(own_weight, (NZ, rows, cols))
-    old = lax.all_to_all(old, "z", 0, 0, tiled=True)
+    old = lax.all_to_all(old, Z, 0, 0, tiled=True)
     old = old.reshape(NL * NC, 2, rows, cols)
     other = shift(old, "xh", NX, 1)
     old = jnp.stack([old, other])
@@ -251,7 +259,7 @@
         right = lax.dynamic_slice_in_dim(masked_all, (k >> 1) * cols, cols, 1)
         return lax.dot_general(left, right, (((0,), (0,)), ((), ())), preferred_element_type=F32)
 
-    part = ring_sum(term, "z", NZ, z).reshape(NX, NY, rows, cols)
+    part = ring_sum(term, Z, NZ, z).reshape(NX, NY, rows, cols)
     part = part.astype(BF16).reshape(NX * NY, rows, cols)
     part = lax.all_to_all(part, ("xh", "y"), 0, 0, tiled=True)
     grad = jnp.sum(part.astype(F32), axis=0)
@@ -262,19 +270,16 @@
     raw = jnp.dot(hidden, own_weight, preferred_element_type=F32).astype(BF16)
     raw = raw.reshape(NX * NY, NZ * lines, cols)
     raw = lax.all_to_all(raw, ("xh", "y"), 0, 0, tiled=True)
-    raw = jnp.sum(raw.astype(F32), axis=0).reshape(NL, NC, 2, lines, cols)
-    other = shift(pick(raw, 1 - c, 1), "c", NC, 1)
-    raw = pick(raw, c, 1) + other
-    other = shift(pick(raw, 1 - xl, 0), "xl", NL, 1)
-    raw = pick(raw, xl, 0) + other
-    same = swap_owner(pick(raw, odd, 0))
-    other = swap_owner(pick(raw, 1 - odd, 0), 1)
+    raw = jnp.sum(raw.astype(F32), axis=0).reshape(NL * NC, 2, lines, cols)
+    raw = raw.transpose(1, 0, 2, 3).reshape(2 * NL * NC, lines, cols).astype(BF16)
+    raw = lax.all_to_all(raw, ("zl",) + TP, 0, 0, tiled=True)
+    raw = swap_owner(jnp.sum(raw.astype(F32), axis=0))
 
     learner_weight = swap_owner(own_weight)
 
     state = attend_cache(queries, cache_keys, cache_values, cache_lengths)
     cosine, sine = angles(cache_lengths, steps)
-    new_keys, context = attend_fresh(same, other, cosine, sine, queries, new_values, *state)
+    new_keys, context = attend_fresh(raw, cosine, sine, queries, new_values, *state)
 
     place = jnp.stack([xh, y, (y - 1) & (NY - 1), (y + 1) & (NY - 1), y ^ 2]).astype(jnp.int32)
     grad_inputs = None
@@ -284,7 +289,7 @@
 
 
 def solution(mesh):
-    split = Mesh(mesh.devices.reshape(NZ, NX, NY, NL, NC), ("z", "xh", "y", "xl", "c"))
+    split = Mesh(mesh.devices.reshape(NZ // 2, 2, NX, NY, NL, NC), ("zh", "zl", "xh", "y", "xl", "c"))
     placed = (
         P(FSDP, TP),
         P(FSDP, TP),

time: 216 us -> 205 us (0.949)
  the two profiles are of different devices: /device:TPU:2 before, /device:TPU:34 now
where the time goes in v4:
time: 205 us; the launch traced here: 204 us
  waiting for transfers between devices  74.1 us (36%)
  starting transfers between devices  66.1 us (32%)
  Pallas kernels  22 us (11%)
  other arithmetic  15.7 us (8%)
  local copies, waits for them, and re-layouts  8.9 us (4%)
  blocking collectives  8.19 us (4%)
  matrix products  7.76 us (4%)
    ppermute x12, waiting for transfers between devices, shift(): return lax.ppermute(x, axis, [(i, (i + step) % size) for i in range(size)])  58.6 us
    ppermute x3, starting transfers between devices, swap_owner(): return lax.ppermute(x, Z + TP, pairs)  16.7 us
    ppermute x12, starting transfers between devices, shift(): return lax.ppermute(x, axis, [(i, (i + step) % size) for i in range(size)])  15.2 us
    pallas_call x4, Pallas kernels, input_grad(): pl.pallas_call(lambda *refs: input_kernel(*refs, number=number), out_shap...  11.4 us
    all_to_all x1, starting transfers between devices, update_and_decode(): hidden = lax.all_to_all(hidden, Z, 0, 0, tiled=True)  8.44 us
    all_gather x1, blocking collectives, update_and_decode(): masked_all = lax.all_gather(masked, TP, axis=1, tiled=True)  8.19 us
    pallas_call x1, Pallas kernels, attend_cache(): pl.pallas_call(lambda *refs: cache_kernel(*refs, groups=groups, share=sha...  7.83 us
    dot_general x8, matrix products, term(): lax.dot_general(left, right, (((0,), (0,)), ((), ())), preferred_element_...  6.37 us
  transfers between devices with their start and end apart: 21, of which 10 were waited for; matrix products, arithmetic and copies ran while one was open for 14% of the time, Pallas kernels for 9%

profile of v4, /device:TPU:34, one launch (start us, length us, event | category | flops | bytes accessed | tf_op | source)
XLA Modules:
  0.0 203.7 jit_solution(7849693296286662295)
XLA Ops:
  0.7 0.8 convert_element_type.92
  1.5 1.0 broadcast_multiply_fusion
  2.5 8.2 %all_gather.3.refs_1_ = bf16[384,1024]{1,0:T(8,128)(2,1)S(1)} all-gather(bf16[384,256]{1,0:T(8,128)(2,1)S(1)} %broadcast_multiply_fusion), channel_id=1, replica_groups=mesh['zh'=4,'zl'=2,'xh'=2,'y'=4,'xl'=2,'c'=2] {'xl','c'}, dimensions={1}, use_global_device_ids=true | all-gather | bytes 983040 | tf_op jit(solution)/shard_map/all_gather | solution.py:236
  10.7 0.5 convolution_convert_fusion.1
  11.2 1.3 collective-permute-start.9
  12.6 0.8 collective-permute-start.5
  13.3 6.7 %collective-permute-done.9 = bf16[512,256]{1,0:T(8,128)(2,1)S(1)} collective-permute-done((bf16[512,256]{1,0:T(8,128)(2,1)S(1)}, bf16[512,256]{1,0:T(8,128)(2,1)S(1)}, u32[]{:S(2)}, u32[]{:S(2)}) %collective-permute-start.9) | collective-permute-done | bytes 262176 | tf_op jit(solution)/shard_map/ppermute | solution.py:24
  20.0 1.3 add_convert_fusion.3
  21.3 3.3 %collective-permute-start.10 = (bf16[1024,256]{1,0:T(8,128)(2,1)}, bf16[1024,256]{1,0:T(8,128)(2,1)}, u32[]{:S(2)}, u32[]{:S(2)}) collective-permute-start(bf16[1024,256]{1,0:T(8,128)(2,1)} %add_convert_fusion.3), channel_id=1, source_target_pairs={{0,224},{32,0},{64,32},{96,64},{128,96},{160,128},{192,160},{224,1... | collective-permute-start | bytes 1572872 | tf_op jit(solution)/shard_map/ppermute | solution.py:24
  24.6 6.1 %collective-permute-start = (bf16[128,256]{1,0:T(8,128)(2,1)}, bf16[128,256]{1,0:T(8,128)(2,1)}, u32[]{:S(2)}, u32[]{:S(2)}) collective-permute-start(bf16[128,256]{1,0:T(8,128)(2,1)} %param.13), channel_id=1, source_target_pairs={{0,0},{1,64},{2,128},{3,192},{32,32},{33,96},{34,160},{35,224},{64... | collective-permute-start | bytes 196616 | tf_op jit(solution)/shard_map/ppermute | solution.py:32
  30.7 0.9 dynamic-slice_bitcast_fusion
  31.7 0.8 copy.20
  32.4 6.0 %all-to-all-start.2 = ((bf16[8,2,32,128]{3,1,2,0:T(2,128)(2,1)}), bf16[8,2,32,128]{3,1,2,0:T(2,128)(2,1)S(1)}, u32[]{:S(2)}, u32[]{:S(2)}) async-start(bf16[8,2,32,128]{3,1,2,0:T(2,128)(2,1)} %copy.20), calls=%async_computation.2 | async-start | bytes 262144 | tf_op jit(solution)/shard_map/all_to_all | solution.py:241
  38.5 1.3 add_convert_fusion.6
  39.8 1.4 fusion.2
  41.2 0.5 fusion.9
  41.7 0.8 collective-permute-done
  42.5 4.0 %all-to-all-done.2 = bf16[8,2,32,128]{3,1,2,0:T(2,128)(2,1)S(1)} async-done(((bf16[8,2,32,128]{3,1,2,0:T(2,128)(2,1)}), bf16[8,2,32,128]{3,1,2,0:T(2,128)(2,1)S(1)}, u32[]{:S(2)}, u32[]{:S(2)}) %all-to-all-start.2) | async-done | bytes 131104 | tf_op jit(solution)/shard_map/all_to_all | solution.py:241
  46.6 1.7 broadcast_in_dim.6
  48.3 5.5 %all-to-all-start = ((bf16[8,128,256]{2,1,0:T(8,128)(2,1)}), bf16[8,128,256]{2,1,0:T(8,128)(2,1)}, u32[]{:S(2)}, u32[]{:S(2)}) async-start(bf16[8,128,256]{2,1,0:T(8,128)(2,1)} %broadcast_in_dim.6), calls=%async_computation | async-start | bytes 1048576 | tf_op jit(solution)/shard_map/all_to_all | solution.py:249
  53.8 1.5 add_convert_fusion.2
  55.5 1.9 add_convert_fusion.5
  57.5 1.9 collective-permute-start.7
  59.8 0.5 fusion.11
  60.4 15.7 %collective-permute-done.11 = bf16[1024,256]{1,0:T(8,128)(2,1)S(1)} collective-permute-done((bf16[1024,256]{1,0:T(8,128)(2,1)S(1)}, bf16[1024,256]{1,0:T(8,128)(2,1)S(1)}, u32[]{:S(2)}, u32[]{:S(2)}) %collective-permute-start.11) | collective-permute-done | bytes 524320 | tf_op jit(solution)/shard_map/ppermute | solution.py:24
  76.1 0.9 add_convert_fusion.1
  77.0 0.5 collective-permute-start.12
  77.5 0.9 broadcast_in_dim.8
  78.4 8.4 %all-to-all-start.3 = ((bf16[8,256,128]{2,1,0:T(8,128)(2,1)}), bf16[8,256,128]{2,1,0:T(8,128)(2,1)}, u32[]{:S(2)}, u32[]{:S(2)}) async-start(bf16[8,256,128]{2,1,0:T(8,128)(2,1)} %bitcast.33), calls=%async_computation.3 | async-start | bytes 1048576 | tf_op jit(solution)/shard_map/all_to_all | solution.py:244
  86.8 1.9 add_convert_fusion.4
  88.8 1.5 collective-permute-start.8
  90.2 0.5 collective-permute-start.1
  91.2 1.9 collective-permute-done.12
  93.1 15.1 %collective-permute-done.8 = bf16[1024,256]{1,0:T(8,128)(2,1)S(1)} collective-permute-done((bf16[1024,256]{1,0:T(8,128)(2,1)}, bf16[1024,256]{1,0:T(8,128)(2,1)S(1)}, u32[]{:S(2)}, u32[]{:S(2)}) %collective-permute-start.8) | collective-permute-done | bytes 524320 | tf_op jit(solution)/shard_map/ppermute | solution.py:24
  108.2 2.0 add_convert_fusion
  110.2 4.3 %all-to-all-start.1 = ((bf16[8,128,256]{2,1,0:T(8,128)(2,1)}), bf16[8,128,256]{2,1,0:T(8,128)(2,1)}, u32[]{:S(2)}, u32[]{:S(2)}) async-start(bf16[8,128,256]{2,1,0:T(8,128)(2,1)} %bitcast.8), calls=%async_computation.1 | async-start | bytes 1048576 | tf_op jit(solution)/shard_map/all_to_all | solution.py:264
  114.6 0.8 copy-done.5
  115.3 1.3 pad_maximum_fusion.refs_2_
  116.7 2.1 %collective-permute-start.2 = (bf16[2,4,2,128,256]{4,3,2,1,0:T(8,128)(2,1)S(1)}, bf16[2,4,2,128,256]{4,3,2,1,0:T(8,128)(2,1)}, u32[]{:S(2)}, u32[]{:S(2)}) collective-permute-start(bf16[2,4,2,128,256]{4,3,2,1,0:T(8,128)(2,1)S(1)} %pad_maximum_fusion.refs_2_), channel_id=1, source_target_pairs={{0,4},{4,8},{8,12},{12,0},{1,5},{5,9},{9,13},{13,1},{2,6},{6,10},{... | collective-permute-start | bytes 3145736 | tf_op jit(solution)/shard_map/ppermute | solution.py:24
  118.8 1.1 copy.22
  119.8 4.7 %all-to-all-done.1 = bf16[8,128,256]{2,1,0:T(8,128)(2,1)} async-done(((bf16[8,128,256]{2,1,0:T(8,128)(2,1)}), bf16[8,128,256]{2,1,0:T(8,128)(2,1)}, u32[]{:S(2)}, u32[]{:S(2)}) %all-to-all-start.1) | async-done | bytes 524320 | tf_op jit(solution)/shard_map/all_to_all | solution.py:264
  124.5 1.1 convert_reduce_fusion
  125.7 0.9 subtract_convert_fusion
  126.5 1.4 convolution_convert_fusion
  127.9 4.2 %all-to-all-start.4 = ((bf16[8,256,256]{2,1,0:T(8,128)(2,1)}), bf16[8,256,256]{2,1,0:T(8,128)(2,1)}, u32[]{:S(2)}, u32[]{:S(2)}) async-start(bf16[8,256,256]{2,1,0:T(8,128)(2,1)} %bitcast.31), calls=%async_computation.4 | async-start | bytes 2097152 | tf_op jit(solution)/shard_map/all_to_all | solution.py:272
  132.2 3.1 %collective-permute-start.4 = (bf16[2,4,2,128,256]{4,3,2,1,0:T(8,128)(2,1)S(1)}, bf16[2,4,2,128,256]{4,3,2,1,0:T(8,128)(2,1)}, u32[]{:S(2)}, u32[]{:S(2)}) collective-permute-start(bf16[2,4,2,128,256]{4,3,2,1,0:T(8,128)(2,1)S(1)} %pad_maximum_fusion.refs_2_), channel_id=1, source_target_pairs={{0,12},{4,0},{8,4},{12,8},{1,13},{5,1},{9,5},{13,9},{2,14},{6,2},{... | collective-permute-start | bytes 3145736 | tf_op jit(solution)/shard_map/ppermute | solution.py:24
  135.3 19.1 %collective-permute-done.2.refs_2_ = bf16[2,4,2,128,256]{4,3,2,1,0:T(8,128)(2,1)} collective-permute-done((bf16[2,4,2,128,256]{4,3,2,1,0:T(8,128)(2,1)S(1)}, bf16[2,4,2,128,256]{4,3,2,1,0:T(8,128)(2,1)}, u32[]{:S(2)}, u32[]{:S(2)}) %collective-permute-start.2) | collective-permute-done | bytes 1048608 | tf_op jit(solution)/shard_map/ppermute | solution.py:24
  154.6 0.6 stack.29.refs_0_
  155.4 2.9 %all-to-all-done.4 = bf16[8,256,256]{2,1,0:T(8,128)(2,1)} async-done(((bf16[8,256,256]{2,1,0:T(8,128)(2,1)}), bf16[8,256,256]{2,1,0:T(8,128)(2,1)}, u32[]{:S(2)}, u32[]{:S(2)}) %all-to-all-start.4) | async-done | bytes 1048608 | tf_op jit(solution)/shard_map/all_to_all | solution.py:272
  158.2 1.4 reduce_sum.31
  159.6 0.7 copy.23
  160.3 5.7 %all-to-all-start.5 = ((bf16[8,32,256]{2,1,0:T(8,128)(2,1)}), bf16[8,32,256]{2,1,0:T(8,128)(2,1)S(1)}, u32[]{:S(2)}, u32[]{:S(2)}) async-start(bf16[8,32,256]{2,1,0:T(8,128)(2,1)} %bitcast.20), calls=%async_computation.5 | async-start | bytes 262144 | tf_op jit(solution)/shard_map/all_to_all | solution.py:275
  165.9 0.7 pad_maximum_fusion.1
  166.6 6.1 %collective-permute-start.13 = (bf16[128,256]{1,0:T(8,128)(2,1)S(1)}, bf16[128,256]{1,0:T(8,128)(2,1)S(1)}, u32[]{:S(2)}, u32[]{:S(2)}) collective-permute-start(bf16[128,256]{1,0:T(8,128)(2,1)S(1)} %subtract_convert_fusion), channel_id=1, source_target_pairs={{0,0},{1,64},{2,128},{3,192},{32,32},{33,96},{34,160},{35,224},{64... | collective-permute-start | bytes 196616 | tf_op jit(solution)/shard_map/ppermute | solution.py:32
  172.7 7.8 %cache_attention.1 = (f32[4,2,64,128]{3,2,1,0:T(8,128)}, f32[4,2,64,128]{3,2,1,0:T(8,128)}, f32[4,2,64,128]{3,2,1,0:T(8,128)}) custom-call(s32[4]{0:T(128)} %refs_0_.1, bf16[4,8,2048]{2,1,0:T(8,128)(2,1)} %q_ref.1, bf16[4,2048,256]{2,1,0:T(8,128)(2,1)} %refs_2_.1, bf16[4,2048,256]{2,1,0:T(8,128)(2,1)} %refs_3_.1), custom_call_target="tpu_custom_call" | custom-call | flops 536870912 | bytes 8388608 | tf_op jit(solution)/shard_map/cache_attention/pallas_call | solution.py:90
  180.5 2.8 %input_grad.4.refs_3_ = bf16[384,2048]{1,0:T(8,128)(2,1)} custom-call(s32[5]{0:T(128)} %stack.29.refs_0_, bf16[384,1024]{1,0:T(8,128)(2,1)} %copy-done.1, bf16[2,4,2,128,256]{4,3,2,1,0:T(8,128)(2,1)} %copy-done.2), custom_call_target="tpu_custom_call" | custom-call | flops 402653184 | bytes 1048576 | tf_op jit(solution)/shard_map/input_grad/pallas_call | solution.py:184
  183.4 2.9 %input_grad.5.refs_3_ = bf16[384,2048]{1,0:T(8,128)(2,1)} custom-call(s32[5]{0:T(128)} %stack.29.refs_0_, bf16[384,1024]{1,0:T(8,128)(2,1)} %copy-done.1, bf16[2,4,2,128,256]{4,3,2,1,0:T(8,128)(2,1)} %collective-permute-done.2.refs_2_, bf16[384,2048]{1,0:T(8,128)(2,1)} %input_grad.4.refs_3_), custom_call_target="tpu_custom_call", output_to_operand_aliasing={{}: (3, {})} | custom-call | flops 402653184 | bytes 1048576 | tf_op jit(solution)/shard_map/input_grad/pallas_call | solution.py:184
  186.3 4.6 %collective-permute-start.14 = (f32[32,256]{1,0:T(8,128)S(1)}, f32[32,256]{1,0:T(8,128)S(1)}, u32[]{:S(2)}, u32[]{:S(2)}) collective-permute-start(f32[32,256]{1,0:T(8,128)S(1)} %convert_reduce_fusion.1), channel_id=1, source_target_pairs={{0,0},{1,64},{2,128},{3,192},{32,32},{33,96},{34,160},{35,224},{64... | collective-permute-start | bytes 98312 | tf_op jit(solution)/shard_map/ppermute | solution.py:32
  190.9 2.9 %input_grad.6.refs_3_ = bf16[384,2048]{1,0:T(8,128)(2,1)} custom-call(s32[5]{0:T(128)} %stack.29.refs_0_, bf16[384,1024]{1,0:T(8,128)(2,1)} %copy-done.1, bf16[2,4,2,128,256]{4,3,2,1,0:T(8,128)(2,1)} %collective-permute-done.4.refs_2_, bf16[384,2048]{1,0:T(8,128)(2,1)} %input_grad.5.refs_3_), custom_call_target="tpu_custom_call", output_to_operand_aliasing={{}: (3, {})} | custom-call | flops 402653184 | bytes 1048576 | tf_op jit(solution)/shard_map/input_grad/pallas_call | solution.py:184
  193.7 3.1 %collective-permute-done.14.raw_ref = f32[32,256]{1,0:T(8,128)S(1)} collective-permute-done((f32[32,256]{1,0:T(8,128)S(1)}, f32[32,256]{1,0:T(8,128)S(1)}, u32[]{:S(2)}, u32[]{:S(2)}) %collective-permute-start.14) | collective-permute-done | bytes 32800 | tf_op jit(solution)/shard_map/ppermute | solution.py:32
  196.9 0.6 copy-done.6
  197.5 2.7 %fresh_attention.1 = (bf16[4,8,256]{2,1,0:T(8,128)(2,1)}, bf16[4,8,2048]{2,1,0:T(8,128)(2,1)}) custom-call(f32[32,256]{1,0:T(8,128)} %copy-done.6, f32[32,128]{1,0:T(8,128)} %get-tuple-element.19.cos_ref, f32[32,128]{1,0:T(8,128)} %get-tuple-element.20.sin_ref, bf16[4,8,2048]{2,1,0:T(8,128)(2,1)} %q_ref.1, bf16[4,8,256]{2,1,0:T(8,128)(2,1)} %v_ref.1, ...), custom_call_target="tpu_custom_call" | custom-call | tf_op jit(solution)/shard_map/fresh_attention/pallas_call | solution.py:146
  200.3 2.8 %input_grad.7 = bf16[384,2048]{1,0:T(8,128)(2,1)} custom-call(s32[5]{0:T(128)} %stack.29.refs_0_, bf16[384,1024]{1,0:T(8,128)(2,1)} %copy-done.1, bf16[2,4,2,128,256]{4,3,2,1,0:T(8,128)(2,1)} %collective-permute-done.3.refs_2_, bf16[384,2048]{1,0:T(8,128)(2,1)} %input_grad.6.refs_3_), custom_call_target="tpu_custom_call", output_to_operand_aliasing={{}: (3, {})} | custom-call | flops 402653184 | bytes 1048576 | tf_op jit(solution)/shard_map/input_grad/pallas_call | solution.py:184
  203.1 0.6 copy.29
  (38 shorter events, 1.6 us)
Async XLA Ops:
  0.6 10.1 %copy-start = (bf16[384,2048]{1,0:T(8,128)(2,1)S(1)}, bf16[384,2048]{1,0:T(8,128)(2,1)}, u32[]{:S(2)}) copy-start(bf16[384,2048]{1,0:T(8,128)(2,1)} %param.10) | copy-start | bytes 4718596
  10.7 80.0 %copy-start.1 = (bf16[384,1024]{1,0:T(8,128)(2,1)}, bf16[384,1024]{1,0:T(8,128)(2,1)S(1)}, u32[]{:S(2)}) copy-start(bf16[384,1024]{1,0:T(8,128)(2,1)S(1)} %all_gather.3.refs_1_) | copy-start | bytes 2359300
  11.2 8.8 %collective-permute-start.9 = (bf16[512,256]{1,0:T(8,128)(2,1)S(1)}, bf16[512,256]{1,0:T(8,128)(2,1)S(1)}, u32[]{:S(2)}, u32[]{:S(2)}) collective-permute-start(bf16[512,256]{1,0:T(8,128)(2,1)S(1)} %get-tuple-element.15), channel_id=1, source_target_pairs={{0,224},{32,0},{64,32},{96,64},{128,96},{160,128},{192,160},{224,1... | collective-permute-start | bytes 786440 | tf_op jit(solution)/shard_map/ppermute | solution.py:24
  12.6 25.9 %collective-permute-start.5 = (bf16[512,256]{1,0:T(8,128)(2,1)S(1)}, bf16[512,256]{1,0:T(8,128)(2,1)S(1)}, u32[]{:S(2)}, u32[]{:S(2)}) collective-permute-start(bf16[512,256]{1,0:T(8,128)(2,1)S(1)} %get-tuple-element.14), channel_id=1, source_target_pairs={{0,32},{32,64},{64,96},{96,128},{128,160},{160,192},{192,224},{224... | collective-permute-start | bytes 786440 | tf_op jit(solution)/shard_map/ppermute | solution.py:24
  21.3 32.5 %collective-permute-start.10 = (bf16[1024,256]{1,0:T(8,128)(2,1)}, bf16[1024,256]{1,0:T(8,128)(2,1)}, u32[]{:S(2)}, u32[]{:S(2)}) collective-permute-start(bf16[1024,256]{1,0:T(8,128)(2,1)} %add_convert_fusion.3), channel_id=1, source_target_pairs={{0,224},{32,0},{64,32},{96,64},{128,96},{160,128},{192,160},{224,1... | collective-permute-start | bytes 1572872 | tf_op jit(solution)/shard_map/ppermute | solution.py:24
  24.6 17.9 %collective-permute-start = (bf16[128,256]{1,0:T(8,128)(2,1)}, bf16[128,256]{1,0:T(8,128)(2,1)}, u32[]{:S(2)}, u32[]{:S(2)}) collective-permute-start(bf16[128,256]{1,0:T(8,128)(2,1)} %param.13), channel_id=1, source_target_pairs={{0,0},{1,64},{2,128},{3,192},{32,32},{33,96},{34,160},{35,224},{64... | collective-permute-start | bytes 196616 | tf_op jit(solution)/shard_map/ppermute | solution.py:32
  32.4 14.1 %all-to-all-start.2 = ((bf16[8,2,32,128]{3,1,2,0:T(2,128)(2,1)}), bf16[8,2,32,128]{3,1,2,0:T(2,128)(2,1)S(1)}, u32[]{:S(2)}, u32[]{:S(2)}) async-start(bf16[8,2,32,128]{3,1,2,0:T(2,128)(2,1)} %copy.20), calls=%async_computation.2 | async-start | bytes 262144 | tf_op jit(solution)/shard_map/all_to_all | solution.py:241
  39.8 15.8 %collective-permute-start.6 = (bf16[1024,256]{1,0:T(8,128)(2,1)}, bf16[1024,256]{1,0:T(8,128)(2,1)}, u32[]{:S(2)}, u32[]{:S(2)}) collective-permute-start(bf16[1024,256]{1,0:T(8,128)(2,1)} %add_convert_fusion.6), channel_id=1, source_target_pairs={{0,32},{32,64},{64,96},{96,128},{128,160},{160,192},{192,224},{224... | collective-permute-start | bytes 1572872 | tf_op jit(solution)/shard_map/ppermute | solution.py:24
  46.6 8.7 %copy-start.3 = (bf16[8,2,32,128]{3,1,2,0:T(2,128)(2,1)}, bf16[8,2,32,128]{3,1,2,0:T(2,128)(2,1)S(1)}, u32[]{:S(2)}) copy-start(bf16[8,2,32,128]{3,1,2,0:T(2,128)(2,1)S(1)} %all-to-all-done.2) | copy-start | bytes 393220
  48.3 29.2 %all-to-all-start = ((bf16[8,128,256]{2,1,0:T(8,128)(2,1)}), bf16[8,128,256]{2,1,0:T(8,128)(2,1)}, u32[]{:S(2)}, u32[]{:S(2)}) async-start(bf16[8,128,256]{2,1,0:T(8,128)(2,1)} %broadcast_in_dim.6), calls=%async_computation | async-start | bytes 1048576 | tf_op jit(solution)/shard_map/all_to_all | solution.py:249
  55.3 20.8 %collective-permute-start.11 = (bf16[1024,256]{1,0:T(8,128)(2,1)S(1)}, bf16[1024,256]{1,0:T(8,128)(2,1)S(1)}, u32[]{:S(2)}, u32[]{:S(2)}) collective-permute-start(bf16[1024,256]{1,0:T(8,128)(2,1)S(1)} %add_convert_fusion.2), channel_id=1, source_target_pairs={{0,224},{32,0},{64,32},{96,64},{128,96},{160,128},{192,160},{224,1... | collective-permute-start | bytes 1572872 | tf_op jit(solution)/shard_map/ppermute | solution.py:24
  57.5 2.9 %copy-start.4 = (bf16[8,2,32,128]{3,1,2,0:T(2,128)(2,1)S(1)}, bf16[8,2,32,128]{3,1,2,0:T(2,128)(2,1)}, u32[]{:S(2)}) copy-start(bf16[8,2,32,128]{3,1,2,0:T(2,128)(2,1)} %copy-done.3) | copy-start | bytes 393220
  57.5 29.3 %collective-permute-start.7 = (bf16[1024,256]{1,0:T(8,128)(2,1)}, bf16[1024,256]{1,0:T(8,128)(2,1)}, u32[]{:S(2)}, u32[]{:S(2)}) collective-permute-start(bf16[1024,256]{1,0:T(8,128)(2,1)} %add_convert_fusion.5), channel_id=1, source_target_pairs={{0,32},{32,64},{64,96},{96,128},{128,160},{160,192},{192,224},{224... | collective-permute-start | bytes 1572872 | tf_op jit(solution)/shard_map/ppermute | solution.py:24
  77.0 16.1 %collective-permute-start.12 = (bf16[1024,256]{1,0:T(8,128)(2,1)}, bf16[1024,256]{1,0:T(8,128)(2,1)}, u32[]{:S(2)}, u32[]{:S(2)}) collective-permute-start(bf16[1024,256]{1,0:T(8,128)(2,1)} %add_convert_fusion.1), channel_id=1, source_target_pairs={{0,224},{32,0},{64,32},{96,64},{128,96},{160,128},{192,160},{224,1... | collective-permute-start | bytes 1572872 | tf_op jit(solution)/shard_map/ppermute | solution.py:24
  78.4 31.8 %all-to-all-start.3 = ((bf16[8,256,128]{2,1,0:T(8,128)(2,1)}), bf16[8,256,128]{2,1,0:T(8,128)(2,1)}, u32[]{:S(2)}, u32[]{:S(2)}) async-start(bf16[8,256,128]{2,1,0:T(8,128)(2,1)} %bitcast.33), calls=%async_computation.3 | async-start | bytes 1048576 | tf_op jit(solution)/shard_map/all_to_all | solution.py:244
  88.8 19.4 %collective-permute-start.8 = (bf16[1024,256]{1,0:T(8,128)(2,1)}, bf16[1024,256]{1,0:T(8,128)(2,1)S(1)}, u32[]{:S(2)}, u32[]{:S(2)}) collective-permute-start(bf16[1024,256]{1,0:T(8,128)(2,1)} %add_convert_fusion.4), channel_id=1, source_target_pairs={{0,32},{32,64},{64,96},{96,128},{128,160},{160,192},{192,224},{224... | collective-permute-start | bytes 1572872 | tf_op jit(solution)/shard_map/ppermute | solution.py:24
  90.2 24.3 %collective-permute-start.1 = (bf16[4,2,128,256]{3,2,1,0:T(8,128)(2,1)}, bf16[4,2,128,256]{3,2,1,0:T(8,128)(2,1)S(1)}, u32[]{:S(2)}, u32[]{:S(2)}) collective-permute-start(bf16[4,2,128,256]{3,2,1,0:T(8,128)(2,1)} %bitcast.6), channel_id=1, source_target_pairs={{0,16},{16,0},{1,17},{17,1},{2,18},{18,2},{3,19},{19,3},{4,20},{20... | collective-permute-start | bytes 1572872 | tf_op jit(solution)/shard_map/ppermute | solution.py:24
  110.2 14.3 %all-to-all-start.1 = ((bf16[8,128,256]{2,1,0:T(8,128)(2,1)}), bf16[8,128,256]{2,1,0:T(8,128)(2,1)}, u32[]{:S(2)}, u32[]{:S(2)}) async-start(bf16[8,128,256]{2,1,0:T(8,128)(2,1)} %bitcast.8), calls=%async_computation.1 | async-start | bytes 1048576 | tf_op jit(solution)/shard_map/all_to_all | solution.py:264
  114.6 0.8 copy-start.5
  116.6 15.5 %copy-start.2 = (bf16[2,4,2,128,256]{4,3,2,1,0:T(8,128)(2,1)}, bf16[2,4,2,128,256]{4,3,2,1,0:T(8,128)(2,1)S(1)}, u32[]{:S(2)}) copy-start(bf16[2,4,2,128,256]{4,3,2,1,0:T(8,128)(2,1)S(1)} %pad_maximum_fusion.refs_2_) | copy-start | bytes 3145732
  116.7 37.8 %collective-permute-start.2 = (bf16[2,4,2,128,256]{4,3,2,1,0:T(8,128)(2,1)S(1)}, bf16[2,4,2,128,256]{4,3,2,1,0:T(8,128)(2,1)}, u32[]{:S(2)}, u32[]{:S(2)}) collective-permute-start(bf16[2,4,2,128,256]{4,3,2,1,0:T(8,128)(2,1)S(1)} %pad_maximum_fusion.refs_2_), channel_id=1, source_target_pairs={{0,4},{4,8},{8,12},{12,0},{1,5},{5,9},{9,13},{13,1},{2,6},{6,10},{... | collective-permute-start | bytes 3145736 | tf_op jit(solution)/shard_map/ppermute | solution.py:24
  126.5 27.9 %copy-start.7 = (s32[4]{0:T(128)S(1)}, s32[4]{0:T(128)}, u32[]{:S(2)}) copy-start(s32[4]{0:T(128)} %refs_0_.1) | copy-start | bytes 52
  127.9 30.3 %all-to-all-start.4 = ((bf16[8,256,256]{2,1,0:T(8,128)(2,1)}), bf16[8,256,256]{2,1,0:T(8,128)(2,1)}, u32[]{:S(2)}, u32[]{:S(2)}) async-start(bf16[8,256,256]{2,1,0:T(8,128)(2,1)} %bitcast.31), calls=%async_computation.4 | async-start | bytes 2097152 | tf_op jit(solution)/shard_map/all_to_all | solution.py:272
  132.2 58.7 %collective-permute-start.4 = (bf16[2,4,2,128,256]{4,3,2,1,0:T(8,128)(2,1)S(1)}, bf16[2,4,2,128,256]{4,3,2,1,0:T(8,128)(2,1)}, u32[]{:S(2)}, u32[]{:S(2)}) collective-permute-start(bf16[2,4,2,128,256]{4,3,2,1,0:T(8,128)(2,1)S(1)} %pad_maximum_fusion.refs_2_), channel_id=1, source_target_pairs={{0,12},{4,0},{8,4},{12,8},{1,13},{5,1},{9,5},{13,9},{2,14},{6,2},{... | collective-permute-start | bytes 3145736 | tf_op jit(solution)/shard_map/ppermute | solution.py:24
  154.4 45.8 %collective-permute-start.3 = (bf16[2,4,2,128,256]{4,3,2,1,0:T(8,128)(2,1)}, bf16[2,4,2,128,256]{4,3,2,1,0:T(8,128)(2,1)}, u32[]{:S(2)}, u32[]{:S(2)}) collective-permute-start(bf16[2,4,2,128,256]{4,3,2,1,0:T(8,128)(2,1)} %collective-permute-done.2.refs_2_), channel_id=1, source_target_pairs={{0,4},{4,8},{8,12},{12,0},{1,5},{5,9},{9,13},{13,1},{2,6},{6,10},{... | collective-permute-start | bytes 3145736 | tf_op jit(solution)/shard_map/ppermute | solution.py:24
  160.3 26.0 %all-to-all-start.5 = ((bf16[8,32,256]{2,1,0:T(8,128)(2,1)}), bf16[8,32,256]{2,1,0:T(8,128)(2,1)S(1)}, u32[]{:S(2)}, u32[]{:S(2)}) async-start(bf16[8,32,256]{2,1,0:T(8,128)(2,1)} %bitcast.20), calls=%async_computation.5 | async-start | bytes 262144 | tf_op jit(solution)/shard_map/all_to_all | solution.py:275
  166.6 16.7 %collective-permute-start.13 = (bf16[128,256]{1,0:T(8,128)(2,1)S(1)}, bf16[128,256]{1,0:T(8,128)(2,1)S(1)}, u32[]{:S(2)}, u32[]{:S(2)}) collective-permute-start(bf16[128,256]{1,0:T(8,128)(2,1)S(1)} %subtract_convert_fusion), channel_id=1, source_target_pairs={{0,0},{1,64},{2,128},{3,192},{32,32},{33,96},{34,160},{35,224},{64... | collective-permute-start | bytes 196616 | tf_op jit(solution)/shard_map/ppermute | solution.py:32
  186.3 10.6 %collective-permute-start.14 = (f32[32,256]{1,0:T(8,128)S(1)}, f32[32,256]{1,0:T(8,128)S(1)}, u32[]{:S(2)}, u32[]{:S(2)}) collective-permute-start(f32[32,256]{1,0:T(8,128)S(1)} %convert_reduce_fusion.1), channel_id=1, source_target_pairs={{0,0},{1,64},{2,128},{3,192},{32,32},{33,96},{34,160},{35,224},{64... | collective-permute-start | bytes 98312 | tf_op jit(solution)/shard_map/ppermute | solution.py:32
  196.9 0.6 copy-start.6

commit v5 on v4

--- a/solution.py
+++ b/solution.py
@@ -11,8 +11,7 @@
 D = 8192
 HD = 128
 NZ, NX, NY, NL, NC = 8, 2, 4, 2, 2
-FSDP = ("zh", "zl", "xh", "y")
-Z = ("zh", "zl")
+FSDP = ("z", "xh", "y")
 TP = ("xl", "c")
 F32 = jnp.float32
 BF16 = jnp.bfloat16
@@ -24,12 +23,16 @@
     return lax.ppermute(x, axis, [(i, (i + step) % size) for i in range(size)])
 
 
-def swap_owner(x):
+def swap_owner(x, flip=0):
     pairs = []
     for z in range(NZ):
         for t in range(NL * NC):
-            pairs.append((z * 4 + t, (2 * t + z % 2) * 4 + z // 2))
-    return lax.ppermute(x, Z + TP, pairs)
+            pairs.append((z * 4 + t, (2 * t + (z % 2 ^ flip)) * 4 + z // 2))
+    return lax.ppermute(x, ("z", "xl", "c"), pairs)
+
+
+def pick(x, index, axis):
+    return lax.dynamic_index_in_dim(x, index, axis, keepdims=False)
 
 
 def ring_sum(term, axis, size, me):
@@ -110,7 +113,7 @@
 
 
 def fresh_kernel(
-    raw_ref, cos_ref, sin_ref, q_ref, v_ref, mixed_ref, top_ref, total_ref, keys_ref, out_ref
+    same_ref, other_ref, cos_ref, sin_ref, q_ref, v_ref, mixed_ref, top_ref, total_ref, keys_ref, out_ref
 ):
     count, steps, width = q_ref.shape
     groups = v_ref.shape[2] // HD
@@ -120,7 +123,7 @@
         for j in range(groups):
             lanes = slice(j * HD, (j + 1) * HD)
             heads = slice(j * share * HD, (j + 1) * share * HD)
-            raw = raw_ref[lines, lanes]
+            raw = same_ref[lines, lanes] + other_ref[lines, lanes]
             keys = raw * cos_ref[lines, :] + pltpu.roll(raw, HD // 2, 1) * sin_ref[lines, :]
             keys = keys.astype(BF16)
             keys_ref[r, :, lanes] = keys
@@ -142,7 +145,7 @@
             out_ref[r, :, heads] = jnp.concatenate(flat, axis=1).astype(BF16)
 
 
-def attend_fresh(raw, cosine, sine, queries, new_values, mixed, top, total):
+def attend_fresh(same, other, cosine, sine, queries, new_values, mixed, top, total):
     return pl.pallas_call(
         fresh_kernel,
         out_shape=(
@@ -150,7 +153,7 @@
             jax.ShapeDtypeStruct(queries.shape, BF16),
         ),
         name="fresh_attention",
-    )(raw, cosine, sine, queries, new_values, mixed, top, total)
+    )(same, other, cosine, sine, queries, new_values, mixed, top, total)
 
 
 def input_kernel(place, m_ref, w_ref, *refs, number):
@@ -224,8 +227,10 @@
     cache_values,
     cache_lengths,
 ):
-    z, xh, y = lax.axis_index(Z), lax.axis_index("xh"), lax.axis_index("y")
-    tp = lax.axis_index(TP)
+    z, xh, y = lax.axis_index("z"), lax.axis_index("xh"), lax.axis_index("y")
+    xl, c = lax.axis_index("xl"), lax.axis_index("c")
+    tp = xl * NC + c
+    odd = z & 1
     wide = tokens.shape[1]
     cols = cotangent.shape[1]
     rows = key_weight.shape[0]
@@ -241,12 +246,12 @@
     hidden = lax.all_to_all(hidden, ("xh", "y"), 0, 0, tiled=True)
     hidden = hidden.transpose(1, 0, 2, 3).reshape(1, 2, NX * NY * lines, rows)
     hidden = jnp.broadcast_to(hidden, (NZ // 2,) + hidden.shape[1:]).reshape(NZ, NX * NY * lines, rows)
-    hidden = lax.all_to_all(hidden, Z, 0, 0, tiled=True)
+    hidden = lax.all_to_all(hidden, "z", 0, 0, tiled=True)
     hidden = hidden.reshape(NZ, NX * NY, lines, rows).transpose(1, 0, 2, 3).reshape(-1, rows)
 
     own_weight = swap_owner(key_weight)
     old = jnp.broadcast_to(own_weight, (NZ, rows, cols))
-    old = lax.all_to_all(old, Z, 0, 0, tiled=True)
+    old = lax.all_to_all(old, "z", 0, 0, tiled=True)
     old = old.reshape(NL * NC, 2, rows, cols)
     other = shift(old, "xh", NX, 1)
     old = jnp.stack([old, other])
@@ -259,7 +264,7 @@
         right = lax.dynamic_slice_in_dim(masked_all, (k >> 1) * cols, cols, 1)
         return lax.dot_general(left, right, (((0,), (0,)), ((), ())), preferred_element_type=F32)
 
-    part = ring_sum(term, Z, NZ, z).reshape(NX, NY, rows, cols)
+    part = ring_sum(term, "z", NZ, z).reshape(NX, NY, rows, cols)
     part = part.astype(BF16).reshape(NX * NY, rows, cols)
     part = lax.all_to_all(part, ("xh", "y"), 0, 0, tiled=True)
     grad = jnp.sum(part.astype(F32), axis=0)
@@ -270,16 +275,19 @@
     raw = jnp.dot(hidden, own_weight, preferred_element_type=F32).astype(BF16)
     raw = raw.reshape(NX * NY, NZ * lines, cols)
     raw = lax.all_to_all(raw, ("xh", "y"), 0, 0, tiled=True)
-    raw = jnp.sum(raw.astype(F32), axis=0).reshape(NL * NC, 2, lines, cols)
-    raw = raw.transpose(1, 0, 2, 3).reshape(2 * NL * NC, lines, cols).astype(BF16)
-    raw = lax.all_to_all(raw, ("zl",) + TP, 0, 0, tiled=True)
-    raw = swap_owner(jnp.sum(raw.astype(F32), axis=0))
+    raw = jnp.sum(raw.astype(F32), axis=0).reshape(NL, NC, 2, lines, cols)
+    other = shift(pick(raw, 1 - c, 1), "c", NC, 1)
+    raw = pick(raw, c, 1) + other
+    other = shift(pick(raw, 1 - xl, 0), "xl", NL, 1)
+    raw = pick(raw, xl, 0) + other
+    same = swap_owner(pick(raw, odd, 0))
+    other = swap_owner(pick(raw, 1 - odd, 0), 1)
 
     learner_weight = swap_owner(own_weight)
 
     state = attend_cache(queries, cache_keys, cache_values, cache_lengths)
     cosine, sine = angles(cache_lengths, steps)
-    new_keys, context = attend_fresh(raw, cosine, sine, queries, new_values, *state)
+    new_keys, context = attend_fresh(same, other, cosine, sine, queries, new_values, *state)
 
     place = jnp.stack([xh, y, (y - 1) & (NY - 1), (y + 1) & (NY - 1), y ^ 2]).astype(jnp.int32)
     grad_inputs = None
@@ -289,7 +297,7 @@
 
 
 def solution(mesh):
-    split = Mesh(mesh.devices.reshape(NZ // 2, 2, NX, NY, NL, NC), ("zh", "zl", "xh", "y", "xl", "c"))
+    split = Mesh(mesh.devices.reshape(NZ, NX, NY, NL, NC), ("z", "xh", "y", "xl", "c"))
     placed = (
         P(FSDP, TP),
         P(FSDP, TP),

time: 205 us -> 204 us (level)
  the two profiles are of different devices: /device:TPU:34 before, /device:TPU:2 now
where the time goes in v5:
time: 204 us; the launch traced here: 203 us
  waiting for transfers between devices  79.5 us (39%)
  starting transfers between devices  61.7 us (30%)
  Pallas kernels  22 us (11%)
  other arithmetic  14.3 us (7%)
  blocking collectives  9.35 us (5%)
  matrix products  7.74 us (4%)
  local copies, waits for them, and re-layouts  7.48 us (4%)
    ppermute x14, waiting for transfers between devices, shift(): return lax.ppermute(x, axis, [(i, (i + step) % size) for i in range(size)])  59.9 us
    ppermute x14, starting transfers between devices, shift(): return lax.ppermute(x, axis, [(i, (i + step) % size) for i in range(size)])  22.1 us
    ppermute x4, starting transfers between devices, swap_owner(): return lax.ppermute(x, ('z', 'xl', 'c'), pairs)  14.7 us
    pallas_call x4, Pallas kernels, input_grad(): pl.pallas_call(lambda *refs: input_kernel(*refs, number=number), out_shap...  11.4 us
    all_gather x1, blocking collectives, update_and_decode(): masked_all = lax.all_gather(masked, TP, axis=1, tiled=True)  9.35 us
    pallas_call x1, Pallas kernels, attend_cache(): pl.pallas_call(lambda *refs: cache_kernel(*refs, groups=groups, share=sha...  7.82 us
    all_to_all x1, starting transfers between devices, update_and_decode(): hidden = lax.all_to_all(hidden, 'z', 0, 0, tiled=True)  6.81 us
    ppermute x4, waiting for transfers between devices, swap_owner(): return lax.ppermute(x, ('z', 'xl', 'c'), pairs)  6.42 us
  transfers between devices with their start and end apart: 23, of which 11 were waited for; matrix products, arithmetic and copies ran while one was open for 13% of the time, Pallas kernels for 9%

profile of v5, /device:TPU:2, one launch (start us, length us, event | category | flops | bytes accessed | tf_op | source)
XLA Modules:
  0.0 202.9 jit_solution(8256763015727341443)
XLA Ops:
  0.7 0.8 convert_element_type.81
  1.5 1.0 broadcast_multiply_fusion
  2.5 9.3 %all_gather.3.refs_1_ = bf16[384,1024]{1,0:T(8,128)(2,1)S(1)} all-gather(bf16[384,256]{1,0:T(8,128)(2,1)S(1)} %broadcast_multiply_fusion), channel_id=1, replica_groups=mesh['z'=8,'xh'=2,'y'=4,'xl'=2,'c'=2] {'xl','c'}, dimensions={1}, use_global_device_ids=true | all-gather | bytes 983040 | tf_op jit(solution)/shard_map/all_gather | solution.py:241
  11.9 0.5 convolution_convert_fusion.1
  12.4 4.8 %collective-permute-start.9 = (bf16[512,256]{1,0:T(8,128)(2,1)S(1)}, bf16[512,256]{1,0:T(8,128)(2,1)S(1)}, u32[]{:S(2)}, u32[]{:S(2)}) collective-permute-start(bf16[512,256]{1,0:T(8,128)(2,1)S(1)} %get-tuple-element.15), channel_id=1, source_target_pairs={{0,224},{32,0},{64,32},{96,64},{128,96},{160,128},{192,160},{224,1... | collective-permute-start | bytes 786440 | tf_op jit(solution)/shard_map/ppermute | solution.py:23
  17.2 6.1 %collective-permute-done.9 = bf16[512,256]{1,0:T(8,128)(2,1)S(1)} collective-permute-done((bf16[512,256]{1,0:T(8,128)(2,1)S(1)}, bf16[512,256]{1,0:T(8,128)(2,1)S(1)}, u32[]{:S(2)}, u32[]{:S(2)}) %collective-permute-start.9) | collective-permute-done | bytes 262176 | tf_op jit(solution)/shard_map/ppermute | solution.py:23
  23.2 1.3 add_convert_fusion.3
  24.5 3.7 %collective-permute-start.10 = (bf16[1024,256]{1,0:T(8,128)(2,1)}, bf16[1024,256]{1,0:T(8,128)(2,1)}, u32[]{:S(2)}, u32[]{:S(2)}) collective-permute-start(bf16[1024,256]{1,0:T(8,128)(2,1)} %add_convert_fusion.3), channel_id=1, source_target_pairs={{0,224},{32,0},{64,32},{96,64},{128,96},{160,128},{192,160},{224,1... | collective-permute-start | bytes 1572872 | tf_op jit(solution)/shard_map/ppermute | solution.py:23
  28.2 3.9 %collective-permute-start = (bf16[128,256]{1,0:T(8,128)(2,1)}, bf16[128,256]{1,0:T(8,128)(2,1)}, u32[]{:S(2)}, u32[]{:S(2)}) collective-permute-start(bf16[128,256]{1,0:T(8,128)(2,1)} %param.13), channel_id=1, source_target_pairs={{0,0},{1,64},{2,128},{3,192},{32,32},{33,96},{34,160},{35,224},{64... | collective-permute-start | bytes 196616 | tf_op jit(solution)/shard_map/ppermute | solution.py:31
  32.1 0.9 dynamic-slice_bitcast_fusion.1
  33.0 0.8 copy.19
  33.8 6.0 %all-to-all-start.2 = ((bf16[8,2,32,128]{3,1,2,0:T(2,128)(2,1)}), bf16[8,2,32,128]{3,1,2,0:T(2,128)(2,1)S(1)}, u32[]{:S(2)}, u32[]{:S(2)}) async-start(bf16[8,2,32,128]{3,1,2,0:T(2,128)(2,1)} %copy.19), calls=%async_computation.2 | async-start | bytes 262144 | tf_op jit(solution)/shard_map/all_to_all | solution.py:246
  39.8 1.3 add_convert_fusion.6
  41.1 0.5 collective-permute-start.6
  41.7 1.4 fusion.2
  43.1 0.5 fusion.9
  43.6 4.3 %all-to-all-done.2 = bf16[8,2,32,128]{3,1,2,0:T(2,128)(2,1)S(1)} async-done(((bf16[8,2,32,128]{3,1,2,0:T(2,128)(2,1)}), bf16[8,2,32,128]{3,1,2,0:T(2,128)(2,1)S(1)}, u32[]{:S(2)}, u32[]{:S(2)}) %all-to-all-start.2) | async-done | bytes 131104 | tf_op jit(solution)/shard_map/all_to_all | solution.py:246
  47.9 1.7 broadcast_in_dim.6
  49.7 4.1 %all-to-all-start = ((bf16[8,128,256]{2,1,0:T(8,128)(2,1)}), bf16[8,128,256]{2,1,0:T(8,128)(2,1)}, u32[]{:S(2)}, u32[]{:S(2)}) async-start(bf16[8,128,256]{2,1,0:T(8,128)(2,1)} %broadcast_in_dim.6), calls=%async_computation | async-start | bytes 1048576 | tf_op jit(solution)/shard_map/all_to_all | solution.py:254
  53.8 1.5 add_convert_fusion.2
  55.3 3.2 %collective-permute-start.11 = (bf16[1024,256]{1,0:T(8,128)(2,1)S(1)}, bf16[1024,256]{1,0:T(8,128)(2,1)S(1)}, u32[]{:S(2)}, u32[]{:S(2)}) collective-permute-start(bf16[1024,256]{1,0:T(8,128)(2,1)S(1)} %add_convert_fusion.2), channel_id=1, source_target_pairs={{0,224},{32,0},{64,32},{96,64},{128,96},{160,128},{192,160},{224,1... | collective-permute-start | bytes 1572872 | tf_op jit(solution)/shard_map/ppermute | solution.py:23
  58.5 2.0 add_convert_fusion.5
  60.5 0.5 fusion.4
  60.9 0.5 fusion.11
  61.5 15.0 %collective-permute-done.11 = bf16[1024,256]{1,0:T(8,128)(2,1)S(1)} collective-permute-done((bf16[1024,256]{1,0:T(8,128)(2,1)S(1)}, bf16[1024,256]{1,0:T(8,128)(2,1)S(1)}, u32[]{:S(2)}, u32[]{:S(2)}) %collective-permute-start.11) | collective-permute-done | bytes 524320 | tf_op jit(solution)/shard_map/ppermute | solution.py:23
  76.4 0.9 add_convert_fusion.1
  77.3 1.6 collective-permute-start.12
  79.0 0.9 broadcast_in_dim.8
  79.8 6.8 %all-to-all-start.3 = ((bf16[8,256,128]{2,1,0:T(8,128)(2,1)}), bf16[8,256,128]{2,1,0:T(8,128)(2,1)}, u32[]{:S(2)}, u32[]{:S(2)}) async-start(bf16[8,256,128]{2,1,0:T(8,128)(2,1)} %bitcast.42), calls=%async_computation.3 | async-start | bytes 1048576 | tf_op jit(solution)/shard_map/all_to_all | solution.py:249
  86.6 2.0 add_convert_fusion.4
  88.6 2.0 collective-permute-start.8
  90.6 0.5 fusion.13
  91.1 0.8 collective-permute-start.1
  91.9 2.2 %collective-permute-done.12 = bf16[1024,256]{1,0:T(8,128)(2,1)} collective-permute-done((bf16[1024,256]{1,0:T(8,128)(2,1)}, bf16[1024,256]{1,0:T(8,128)(2,1)}, u32[]{:S(2)}, u32[]{:S(2)}) %collective-permute-start.12) | collective-permute-done | bytes 524320 | tf_op jit(solution)/shard_map/ppermute | solution.py:23
  94.0 16.9 %collective-permute-done.8 = bf16[1024,256]{1,0:T(8,128)(2,1)S(1)} collective-permute-done((bf16[1024,256]{1,0:T(8,128)(2,1)}, bf16[1024,256]{1,0:T(8,128)(2,1)S(1)}, u32[]{:S(2)}, u32[]{:S(2)}) %collective-permute-start.8) | collective-permute-done | bytes 524320 | tf_op jit(solution)/shard_map/ppermute | solution.py:23
  110.9 2.0 add_convert_fusion
  112.9 4.3 %all-to-all-start.1 = ((bf16[8,128,256]{2,1,0:T(8,128)(2,1)}), bf16[8,128,256]{2,1,0:T(8,128)(2,1)S(1)}, u32[]{:S(2)}, u32[]{:S(2)}) async-start(bf16[8,128,256]{2,1,0:T(8,128)(2,1)} %bitcast.8), calls=%async_computation.1 | async-start | bytes 1048576 | tf_op jit(solution)/shard_map/all_to_all | solution.py:269
  117.3 1.1 copy.21
  118.4 2.1 %pad_maximum_fusion.refs_2_ = bf16[2,4,2,128,256]{4,3,2,1,0:T(8,128)(2,1)} fusion(bf16[1,4,2,128,256]{4,3,2,1,0:T(8,128)(2,1)S(1)} %bitcast.47, bf16[1,4,2,128,256]{4,3,2,1,0:T(8,128)(2,1)} %bitcast.5), kind=kLoop, calls=%fused_computation.3 | loop fusion | flops 524288 | bytes 2097152 | tf_op jit(solution)/shard_map/stack | solution.py:257
  120.5 2.0 collective-permute-start.2
  122.5 5.2 %all-to-all-done.1 = bf16[8,128,256]{2,1,0:T(8,128)(2,1)S(1)} async-done(((bf16[8,128,256]{2,1,0:T(8,128)(2,1)}), bf16[8,128,256]{2,1,0:T(8,128)(2,1)S(1)}, u32[]{:S(2)}, u32[]{:S(2)}) %all-to-all-start.1) | async-done | bytes 524320 | tf_op jit(solution)/shard_map/all_to_all | solution.py:269
  127.8 0.9 subtract_convert_fusion
  128.7 1.4 convolution_convert_fusion
  130.1 3.6 %all-to-all-start.4 = ((bf16[8,256,256]{2,1,0:T(8,128)(2,1)}), bf16[8,256,256]{2,1,0:T(8,128)(2,1)S(1)}, u32[]{:S(2)}, u32[]{:S(2)}) async-start(bf16[8,256,256]{2,1,0:T(8,128)(2,1)} %bitcast.40), calls=%async_computation.4 | async-start | bytes 2097152 | tf_op jit(solution)/shard_map/all_to_all | solution.py:277
  133.8 0.1 fusion.39
  134.0 3.2 %collective-permute-start.4 = (bf16[2,4,2,128,256]{4,3,2,1,0:T(8,128)(2,1)}, bf16[2,4,2,128,256]{4,3,2,1,0:T(8,128)(2,1)}, u32[]{:S(2)}, u32[]{:S(2)}) collective-permute-start(bf16[2,4,2,128,256]{4,3,2,1,0:T(8,128)(2,1)} %pad_maximum_fusion.refs_2_), channel_id=1, source_target_pairs={{0,12},{4,0},{8,4},{12,8},{1,13},{5,1},{9,5},{13,9},{2,14},{6,2},{... | collective-permute-start | bytes 3145736 | tf_op jit(solution)/shard_map/ppermute | solution.py:23
  137.2 19.8 %collective-permute-done.2.refs_2_ = bf16[2,4,2,128,256]{4,3,2,1,0:T(8,128)(2,1)} collective-permute-done((bf16[2,4,2,128,256]{4,3,2,1,0:T(8,128)(2,1)}, bf16[2,4,2,128,256]{4,3,2,1,0:T(8,128)(2,1)}, u32[]{:S(2)}, u32[]{:S(2)}) %collective-permute-start.2) | collective-permute-done | bytes 1048608 | tf_op jit(solution)/shard_map/ppermute | solution.py:23
  157.0 3.6 %all-to-all-done.4 = bf16[8,256,256]{2,1,0:T(8,128)(2,1)S(1)} async-done(((bf16[8,256,256]{2,1,0:T(8,128)(2,1)}), bf16[8,256,256]{2,1,0:T(8,128)(2,1)S(1)}, u32[]{:S(2)}, u32[]{:S(2)}) %all-to-all-start.4) | async-done | bytes 1048608 | tf_op jit(solution)/shard_map/all_to_all | solution.py:277
  160.9 7.8 %cache_attention.1 = (f32[4,2,64,128]{3,2,1,0:T(8,128)}, f32[4,2,64,128]{3,2,1,0:T(8,128)}, f32[4,2,64,128]{3,2,1,0:T(8,128)}) custom-call(s32[4]{0:T(128)} %refs_0_.1, bf16[4,8,2048]{2,1,0:T(8,128)(2,1)} %q_ref.1, bf16[4,2048,256]{2,1,0:T(8,128)(2,1)} %refs_2_.1, bf16[4,2048,256]{2,1,0:T(8,128)(2,1)} %refs_3_.1), custom_call_target="tpu_custom_call" | custom-call | flops 536870912 | bytes 8388608 | tf_op jit(solution)/shard_map/cache_attention/pallas_call | solution.py:93
  168.7 0.7 stack.29.refs_0_
  169.3 0.7 pad_maximum_fusion.1
  170.0 4.2 %collective-permute-start.13 = (bf16[128,256]{1,0:T(8,128)(2,1)S(1)}, bf16[128,256]{1,0:T(8,128)(2,1)S(1)}, u32[]{:S(2)}, u32[]{:S(2)}) collective-permute-start(bf16[128,256]{1,0:T(8,128)(2,1)S(1)} %subtract_convert_fusion), channel_id=1, source_target_pairs={{0,0},{1,64},{2,128},{3,192},{32,32},{33,96},{34,160},{35,224},{64... | collective-permute-start | bytes 196616 | tf_op jit(solution)/shard_map/ppermute | solution.py:31
  174.4 2.8 %input_grad.4.refs_3_ = bf16[384,2048]{1,0:T(8,128)(2,1)} custom-call(s32[5]{0:T(128)} %stack.29.refs_0_, bf16[384,1024]{1,0:T(8,128)(2,1)} %copy-done.1, bf16[2,4,2,128,256]{4,3,2,1,0:T(8,128)(2,1)} %pad_maximum_fusion.refs_2_), custom_call_target="tpu_custom_call" | custom-call | flops 402653184 | bytes 1048576 | tf_op jit(solution)/shard_map/input_grad/pallas_call | solution.py:187
  177.2 3.8 %collective-permute-done.13 = bf16[128,256]{1,0:T(8,128)(2,1)S(1)} collective-permute-done((bf16[128,256]{1,0:T(8,128)(2,1)S(1)}, bf16[128,256]{1,0:T(8,128)(2,1)S(1)}, u32[]{:S(2)}, u32[]{:S(2)}) %collective-permute-start.13) | collective-permute-done | bytes 65568 | tf_op jit(solution)/shard_map/ppermute | solution.py:31
  181.0 2.8 %input_grad.5.refs_3_ = bf16[384,2048]{1,0:T(8,128)(2,1)} custom-call(s32[5]{0:T(128)} %stack.29.refs_0_, bf16[384,1024]{1,0:T(8,128)(2,1)} %copy-done.1, bf16[2,4,2,128,256]{4,3,2,1,0:T(8,128)(2,1)} %collective-permute-done.2.refs_2_, bf16[384,2048]{1,0:T(8,128)(2,1)} %input_grad.4.refs_3_), custom_call_target="tpu_custom_call", output_to_operand_aliasing={{}: (3, {})} | custom-call | flops 402653184 | bytes 1048576 | tf_op jit(solution)/shard_map/input_grad/pallas_call | solution.py:187
  183.9 4.3 %collective-permute-start.16 = (f32[32,256]{1,0:T(8,128)S(1)}, f32[32,256]{1,0:T(8,128)S(1)}, u32[]{:S(2)}, u32[]{:S(2)}) collective-permute-start(f32[32,256]{1,0:T(8,128)S(1)} %get-tuple-element.17), channel_id=1, source_target_pairs={{0,0},{1,64},{2,128},{3,192},{32,32},{33,96},{34,160},{35,224},{64... | collective-permute-start | bytes 98312 | tf_op jit(solution)/shard_map/ppermute | solution.py:31
  188.2 2.4 %collective-permute-start.17 = (f32[32,256]{1,0:T(8,128)S(1)}, f32[32,256]{1,0:T(8,128)S(1)}, u32[]{:S(2)}, u32[]{:S(2)}) collective-permute-start(f32[32,256]{1,0:T(8,128)S(1)} %get-tuple-element.16), channel_id=1, source_target_pairs={{0,32},{1,96},{2,160},{3,224},{32,0},{33,64},{34,128},{35,192},{64... | collective-permute-start | bytes 98312 | tf_op jit(solution)/shard_map/ppermute | solution.py:31
  190.6 2.8 %input_grad.6.refs_3_ = bf16[384,2048]{1,0:T(8,128)(2,1)} custom-call(s32[5]{0:T(128)} %stack.29.refs_0_, bf16[384,1024]{1,0:T(8,128)(2,1)} %copy-done.1, bf16[2,4,2,128,256]{4,3,2,1,0:T(8,128)(2,1)} %collective-permute-done.4.refs_2_, bf16[384,2048]{1,0:T(8,128)(2,1)} %input_grad.5.refs_3_), custom_call_target="tpu_custom_call", output_to_operand_aliasing={{}: (3, {})} | custom-call | flops 402653184 | bytes 1048576 | tf_op jit(solution)/shard_map/input_grad/pallas_call | solution.py:187
  193.4 1.1 collective-permute-done.16.same_ref
  194.5 1.6 collective-permute-done.17.other_ref
  196.1 0.6 copy-done.5
  196.7 2.8 %fresh_attention.1 = (bf16[4,8,256]{2,1,0:T(8,128)(2,1)}, bf16[4,8,2048]{2,1,0:T(8,128)(2,1)}) custom-call(f32[32,256]{1,0:T(8,128)} %copy-done.4, f32[32,256]{1,0:T(8,128)} %copy-done.5, f32[32,128]{1,0:T(8,128)} %get-tuple-element.21.cos_ref, f32[32,128]{1,0:T(8,128)} %get-tuple-element.22.sin_ref, bf16[4,8,2048]{2,1,0:T(8,128)(2,1)} %q_ref.1, ...), custom_call_target="tpu_custom_call" | custom-call | tf_op jit(solution)/shard_map/fresh_attention/pallas_call | solution.py:149
  199.5 2.8 %input_grad.7 = bf16[384,2048]{1,0:T(8,128)(2,1)} custom-call(s32[5]{0:T(128)} %stack.29.refs_0_, bf16[384,1024]{1,0:T(8,128)(2,1)} %copy-done.1, bf16[2,4,2,128,256]{4,3,2,1,0:T(8,128)(2,1)} %collective-permute-done.3.refs_2_, bf16[384,2048]{1,0:T(8,128)(2,1)} %input_grad.6.refs_3_), custom_call_target="tpu_custom_call", output_to_operand_aliasing={{}: (3, {})} | custom-call | flops 402653184 | bytes 1048576 | tf_op jit(solution)/shard_map/input_grad/pallas_call | solution.py:187
  202.3 0.6 copy.27
  (43 shorter events, 0.8 us)
Async XLA Ops:
  0.6 11.2 %copy-start = (bf16[384,2048]{1,0:T(8,128)(2,1)S(1)}, bf16[384,2048]{1,0:T(8,128)(2,1)}, u32[]{:S(2)}) copy-start(bf16[384,2048]{1,0:T(8,128)(2,1)} %param.10) | copy-start | bytes 4718596
  11.9 78.8 %copy-start.1 = (bf16[384,1024]{1,0:T(8,128)(2,1)}, bf16[384,1024]{1,0:T(8,128)(2,1)S(1)}, u32[]{:S(2)}) copy-start(bf16[384,1024]{1,0:T(8,128)(2,1)S(1)} %all_gather.3.refs_1_) | copy-start | bytes 2359300
  12.4 10.9 %collective-permute-start.9 = (bf16[512,256]{1,0:T(8,128)(2,1)S(1)}, bf16[512,256]{1,0:T(8,128)(2,1)S(1)}, u32[]{:S(2)}, u32[]{:S(2)}) collective-permute-start(bf16[512,256]{1,0:T(8,128)(2,1)S(1)} %get-tuple-element.15), channel_id=1, source_target_pairs={{0,224},{32,0},{64,32},{96,64},{128,96},{160,128},{192,160},{224,1... | collective-permute-start | bytes 786440 | tf_op jit(solution)/shard_map/ppermute | solution.py:23
  17.2 22.7 %collective-permute-start.5 = (bf16[512,256]{1,0:T(8,128)(2,1)S(1)}, bf16[512,256]{1,0:T(8,128)(2,1)S(1)}, u32[]{:S(2)}, u32[]{:S(2)}) collective-permute-start(bf16[512,256]{1,0:T(8,128)(2,1)S(1)} %get-tuple-element.14), channel_id=1, source_target_pairs={{0,32},{32,64},{64,96},{96,128},{128,160},{160,192},{192,224},{224... | collective-permute-start | bytes 786440 | tf_op jit(solution)/shard_map/ppermute | solution.py:23
  24.5 29.3 %collective-permute-start.10 = (bf16[1024,256]{1,0:T(8,128)(2,1)}, bf16[1024,256]{1,0:T(8,128)(2,1)}, u32[]{:S(2)}, u32[]{:S(2)}) collective-permute-start(bf16[1024,256]{1,0:T(8,128)(2,1)} %add_convert_fusion.3), channel_id=1, source_target_pairs={{0,224},{32,0},{64,32},{96,64},{128,96},{160,128},{192,160},{224,1... | collective-permute-start | bytes 1572872 | tf_op jit(solution)/shard_map/ppermute | solution.py:23
  28.2 15.4 %collective-permute-start = (bf16[128,256]{1,0:T(8,128)(2,1)}, bf16[128,256]{1,0:T(8,128)(2,1)}, u32[]{:S(2)}, u32[]{:S(2)}) collective-permute-start(bf16[128,256]{1,0:T(8,128)(2,1)} %param.13), channel_id=1, source_target_pairs={{0,0},{1,64},{2,128},{3,192},{32,32},{33,96},{34,160},{35,224},{64... | collective-permute-start | bytes 196616 | tf_op jit(solution)/shard_map/ppermute | solution.py:31
  33.8 14.1 %all-to-all-start.2 = ((bf16[8,2,32,128]{3,1,2,0:T(2,128)(2,1)}), bf16[8,2,32,128]{3,1,2,0:T(2,128)(2,1)S(1)}, u32[]{:S(2)}, u32[]{:S(2)}) async-start(bf16[8,2,32,128]{3,1,2,0:T(2,128)(2,1)} %copy.19), calls=%async_computation.2 | async-start | bytes 262144 | tf_op jit(solution)/shard_map/all_to_all | solution.py:246
  41.1 17.4 %collective-permute-start.6 = (bf16[1024,256]{1,0:T(8,128)(2,1)}, bf16[1024,256]{1,0:T(8,128)(2,1)}, u32[]{:S(2)}, u32[]{:S(2)}) collective-permute-start(bf16[1024,256]{1,0:T(8,128)(2,1)} %add_convert_fusion.6), channel_id=1, source_target_pairs={{0,32},{32,64},{64,96},{96,128},{128,160},{160,192},{192,224},{224... | collective-permute-start | bytes 1572872 | tf_op jit(solution)/shard_map/ppermute | solution.py:23
  47.9 7.4 %copy-start.2 = (bf16[8,2,32,128]{3,1,2,0:T(2,128)(2,1)}, bf16[8,2,32,128]{3,1,2,0:T(2,128)(2,1)S(1)}, u32[]{:S(2)}) copy-start(bf16[8,2,32,128]{3,1,2,0:T(2,128)(2,1)S(1)} %all-to-all-done.2) | copy-start | bytes 393220
  49.7 29.3 %all-to-all-start = ((bf16[8,128,256]{2,1,0:T(8,128)(2,1)}), bf16[8,128,256]{2,1,0:T(8,128)(2,1)}, u32[]{:S(2)}, u32[]{:S(2)}) async-start(bf16[8,128,256]{2,1,0:T(8,128)(2,1)} %broadcast_in_dim.6), calls=%async_computation | async-start | bytes 1048576 | tf_op jit(solution)/shard_map/all_to_all | solution.py:254
  55.3 21.1 %collective-permute-start.11 = (bf16[1024,256]{1,0:T(8,128)(2,1)S(1)}, bf16[1024,256]{1,0:T(8,128)(2,1)S(1)}, u32[]{:S(2)}, u32[]{:S(2)}) collective-permute-start(bf16[1024,256]{1,0:T(8,128)(2,1)S(1)} %add_convert_fusion.2), channel_id=1, source_target_pairs={{0,224},{32,0},{64,32},{96,64},{128,96},{160,128},{192,160},{224,1... | collective-permute-start | bytes 1572872 | tf_op jit(solution)/shard_map/ppermute | solution.py:23
  60.5 1.0 copy-start.3
  60.5 26.2 %collective-permute-start.7 = (bf16[1024,256]{1,0:T(8,128)(2,1)}, bf16[1024,256]{1,0:T(8,128)(2,1)}, u32[]{:S(2)}, u32[]{:S(2)}) collective-permute-start(bf16[1024,256]{1,0:T(8,128)(2,1)} %add_convert_fusion.5), channel_id=1, source_target_pairs={{0,32},{32,64},{64,96},{96,128},{128,160},{160,192},{192,224},{224... | collective-permute-start | bytes 1572872 | tf_op jit(solution)/shard_map/ppermute | solution.py:23
  77.3 16.7 %collective-permute-start.12 = (bf16[1024,256]{1,0:T(8,128)(2,1)}, bf16[1024,256]{1,0:T(8,128)(2,1)}, u32[]{:S(2)}, u32[]{:S(2)}) collective-permute-start(bf16[1024,256]{1,0:T(8,128)(2,1)} %add_convert_fusion.1), channel_id=1, source_target_pairs={{0,224},{32,0},{64,32},{96,64},{128,96},{160,128},{192,160},{224,1... | collective-permute-start | bytes 1572872 | tf_op jit(solution)/shard_map/ppermute | solution.py:23
  79.8 33.1 %all-to-all-start.3 = ((bf16[8,256,128]{2,1,0:T(8,128)(2,1)}), bf16[8,256,128]{2,1,0:T(8,128)(2,1)}, u32[]{:S(2)}, u32[]{:S(2)}) async-start(bf16[8,256,128]{2,1,0:T(8,128)(2,1)} %bitcast.42), calls=%async_computation.3 | async-start | bytes 1048576 | tf_op jit(solution)/shard_map/all_to_all | solution.py:249
  88.6 22.3 %collective-permute-start.8 = (bf16[1024,256]{1,0:T(8,128)(2,1)}, bf16[1024,256]{1,0:T(8,128)(2,1)S(1)}, u32[]{:S(2)}, u32[]{:S(2)}) collective-permute-start(bf16[1024,256]{1,0:T(8,128)(2,1)} %add_convert_fusion.4), channel_id=1, source_target_pairs={{0,32},{32,64},{64,96},{96,128},{128,160},{160,192},{192,224},{224... | collective-permute-start | bytes 1572872 | tf_op jit(solution)/shard_map/ppermute | solution.py:23
  91.1 27.2 %collective-permute-start.1 = (bf16[4,2,128,256]{3,2,1,0:T(8,128)(2,1)}, bf16[4,2,128,256]{3,2,1,0:T(8,128)(2,1)S(1)}, u32[]{:S(2)}, u32[]{:S(2)}) collective-permute-start(bf16[4,2,128,256]{3,2,1,0:T(8,128)(2,1)} %bitcast.6), channel_id=1, source_target_pairs={{0,16},{16,0},{1,17},{17,1},{2,18},{18,2},{3,19},{19,3},{4,20},{20... | collective-permute-start | bytes 1572872 | tf_op jit(solution)/shard_map/ppermute | solution.py:23
  112.9 14.8 %all-to-all-start.1 = ((bf16[8,128,256]{2,1,0:T(8,128)(2,1)}), bf16[8,128,256]{2,1,0:T(8,128)(2,1)S(1)}, u32[]{:S(2)}, u32[]{:S(2)}) async-start(bf16[8,128,256]{2,1,0:T(8,128)(2,1)} %bitcast.8), calls=%async_computation.1 | async-start | bytes 1048576 | tf_op jit(solution)/shard_map/all_to_all | solution.py:269
  120.5 36.5 %collective-permute-start.2 = (bf16[2,4,2,128,256]{4,3,2,1,0:T(8,128)(2,1)}, bf16[2,4,2,128,256]{4,3,2,1,0:T(8,128)(2,1)}, u32[]{:S(2)}, u32[]{:S(2)}) collective-permute-start(bf16[2,4,2,128,256]{4,3,2,1,0:T(8,128)(2,1)} %pad_maximum_fusion.refs_2_), channel_id=1, source_target_pairs={{0,4},{4,8},{8,12},{12,0},{1,5},{5,9},{9,13},{13,1},{2,6},{6,10},{... | collective-permute-start | bytes 3145736 | tf_op jit(solution)/shard_map/ppermute | solution.py:23
  128.7 5.0 %copy-start.6 = (s32[4]{0:T(128)S(1)}, s32[4]{0:T(128)}, u32[]{:S(2)}) copy-start(s32[4]{0:T(128)} %refs_0_.1) | copy-start | bytes 52
  130.1 30.5 %all-to-all-start.4 = ((bf16[8,256,256]{2,1,0:T(8,128)(2,1)}), bf16[8,256,256]{2,1,0:T(8,128)(2,1)S(1)}, u32[]{:S(2)}, u32[]{:S(2)}) async-start(bf16[8,256,256]{2,1,0:T(8,128)(2,1)} %bitcast.40), calls=%async_computation.4 | async-start | bytes 2097152 | tf_op jit(solution)/shard_map/all_to_all | solution.py:277
  134.0 56.6 %collective-permute-start.4 = (bf16[2,4,2,128,256]{4,3,2,1,0:T(8,128)(2,1)}, bf16[2,4,2,128,256]{4,3,2,1,0:T(8,128)(2,1)}, u32[]{:S(2)}, u32[]{:S(2)}) collective-permute-start(bf16[2,4,2,128,256]{4,3,2,1,0:T(8,128)(2,1)} %pad_maximum_fusion.refs_2_), channel_id=1, source_target_pairs={{0,12},{4,0},{8,4},{12,8},{1,13},{5,1},{9,5},{13,9},{2,14},{6,2},{... | collective-permute-start | bytes 3145736 | tf_op jit(solution)/shard_map/ppermute | solution.py:23
  157.0 42.4 %collective-permute-start.3 = (bf16[2,4,2,128,256]{4,3,2,1,0:T(8,128)(2,1)}, bf16[2,4,2,128,256]{4,3,2,1,0:T(8,128)(2,1)}, u32[]{:S(2)}, u32[]{:S(2)}) collective-permute-start(bf16[2,4,2,128,256]{4,3,2,1,0:T(8,128)(2,1)} %collective-permute-done.2.refs_2_), channel_id=1, source_target_pairs={{0,4},{4,8},{8,12},{12,0},{1,5},{5,9},{9,13},{13,1},{2,6},{6,10},{... | collective-permute-start | bytes 3145736 | tf_op jit(solution)/shard_map/ppermute | solution.py:23
  160.8 13.4 %collective-permute-start.14 = (f32[2,2,32,256]{3,2,1,0:T(8,128)S(1)}, f32[2,2,32,256]{3,2,1,0:T(8,128)S(1)}, u32[]{:S(2)}, u32[]{:S(2)}) collective-permute-start(f32[2,2,32,256]{3,2,1,0:T(8,128)S(1)} %dynamic-slice_bitcast_fusion), channel_id=1, source_target_pairs={{0,1},{1,0},{2,3},{3,2},{4,5},{5,4},{6,7},{7,6},{8,9},{9,8},{10,11... | collective-permute-start | bytes 393224 | tf_op jit(solution)/shard_map/ppermute | solution.py:23
  170.0 11.0 %collective-permute-start.13 = (bf16[128,256]{1,0:T(8,128)(2,1)S(1)}, bf16[128,256]{1,0:T(8,128)(2,1)S(1)}, u32[]{:S(2)}, u32[]{:S(2)}) collective-permute-start(bf16[128,256]{1,0:T(8,128)(2,1)S(1)} %subtract_convert_fusion), channel_id=1, source_target_pairs={{0,0},{1,64},{2,128},{3,192},{32,32},{33,96},{34,160},{35,224},{64... | collective-permute-start | bytes 196616 | tf_op jit(solution)/shard_map/ppermute | solution.py:31
  174.3 9.6 %collective-permute-start.15 = (f32[2,32,256]{2,1,0:T(8,128)S(1)}, f32[2,32,256]{2,1,0:T(8,128)S(1)}, u32[]{:S(2)}, u32[]{:S(2)}) collective-permute-start(f32[2,32,256]{2,1,0:T(8,128)S(1)} %dynamic-slice_bitcast_fusion.2), channel_id=1, source_target_pairs={{0,2},{2,0},{1,3},{3,1},{4,6},{6,4},{5,7},{7,5},{8,10},{10,8},{9,1... | collective-permute-start | bytes 196616 | tf_op jit(solution)/shard_map/ppermute | solution.py:23
  183.9 10.6 %collective-permute-start.16 = (f32[32,256]{1,0:T(8,128)S(1)}, f32[32,256]{1,0:T(8,128)S(1)}, u32[]{:S(2)}, u32[]{:S(2)}) collective-permute-start(f32[32,256]{1,0:T(8,128)S(1)} %get-tuple-element.17), channel_id=1, source_target_pairs={{0,0},{1,64},{2,128},{3,192},{32,32},{33,96},{34,160},{35,224},{64... | collective-permute-start | bytes 98312 | tf_op jit(solution)/shard_map/ppermute | solution.py:31
  188.2 7.9 %collective-permute-start.17 = (f32[32,256]{1,0:T(8,128)S(1)}, f32[32,256]{1,0:T(8,128)S(1)}, u32[]{:S(2)}, u32[]{:S(2)}) collective-permute-start(f32[32,256]{1,0:T(8,128)S(1)} %get-tuple-element.16), channel_id=1, source_target_pairs={{0,32},{1,96},{2,160},{3,224},{32,0},{33,64},{34,128},{35,192},{64... | collective-permute-start | bytes 98312 | tf_op jit(solution)/shard_map/ppermute | solution.py:31
  194.5 1.6 copy-start.4
  196.1 0.6 copy-start.5
